TPU v7x, 32 devices: a whole 2x2x4 slice. The times are simulated.
32 devices in a mesh: gx: 4 (over y, core), gy: 8 (over z, x).
Axes of the slice: x: 2, y: 2, z: 4, core: 2. Of those that a mesh axis runs over, the one named last changes fastest.
Arguments:
- permeability: float32 [3, 8, 32, 1024], P(None, None, 'gx', 'gy'), may hold values from 0.01 to 10
- layer_map: int32 [8], replicated, may hold values from 0 to 3, never falling along the last dimension, each value on 1 to 3 neighbouring positions
Outputs:
- coarse_perm: float32 [3, 4, 4, 128], P(None, None, 'gx', 'gy')
- coarse_trans: float32 [3, 4, 4, 128], P(None, None, 'gx', 'gy')
Inputs may be any that keep to these rules, and one draw needn't show every extreme that they name: layer_map never falls along the fine layers and every one of the 4 coarse layers holds one or more fine layers.
All inputs are finite; a program needn't handle non-finite values.
Results may differ from a plain program's by a relative error of at most 0.0003.
Values sent between devices are 32-bit elements; how exact they have to be, the bound alone decides.
No kernel may reach another device: no remote copies, remote signals or barrier semaphores. Data moves between devices by JAX's collectives and lax.ppermute only.
A program may use at most 64 MiB of HBM per device.

v0:
```python
import math

import jax
import jax.numpy as jnp
from jax import lax
from jax.sharding import PartitionSpec as P

NCL = 4
BXY = 8
SWEEPS = 4


KMIN = 0.01
EPS = 1e-06


def with_halo(block, sides, width):
    for axis, dim in sides:
        count = lax.axis_size(axis)
        forward = [(i, i + 1) for i in range(count - 1)]
        backward = [(target, source) for source, target in forward]
        low = lax.ppermute(
            lax.slice_in_dim(block, block.shape[dim] - width, None, axis=dim), axis, forward
        )
        high = lax.ppermute(lax.slice_in_dim(block, 0, width, axis=dim), axis, backward)
        block = jnp.concatenate([low, block, high], axis=dim)
    return block


def shifted(value, axis, steps):
    count = lax.axis_size(axis)
    initial, last = (max(0, -steps), min(count, count - steps))
    return lax.ppermute(value, axis, [(source, source + steps) for source in range(initial, last)])


def sweep_weights(count):
    return [
        1.0 / (1.05 + 0.95 * math.cos(math.pi * (2 * s + 1) / (2 * count))) for s in range(count)
    ]


def harmonic(left, right):
    return 2.0 * left * right / (left + right)


def linear_field(depth, width, height):
    zc = (jnp.arange(depth + 2, dtype=jnp.float32) - 0.5 - depth / 2.0) / depth
    xc = (jnp.arange(width + 2, dtype=jnp.float32) - 0.5 - width / 2.0) / width
    yc = (jnp.arange(height + 2, dtype=jnp.float32) - 0.5 - height / 2.0) / height
    shape = (depth + 2, width + 2, height + 2)
    return jnp.stack(
        [
            jnp.broadcast_to(xc[None, :, None], shape),
            jnp.broadcast_to(yc[None, None, :], shape),
            jnp.broadcast_to(zc[:, None, None], shape),
        ]
    )


def patch_partials(kext, layer_map):
    depth, width, height = (kext.shape[1], kext.shape[2], kext.shape[3])
    perm = kext + KMIN
    tx = jnp.concatenate(
        [perm[0][:, :1], harmonic(perm[0][:, :-1], perm[0][:, 1:]), perm[0][:, -1:]], axis=1
    )
    ty = jnp.concatenate(
        [perm[1][:, :, :1], harmonic(perm[1][:, :, :-1], perm[1][:, :, 1:]), perm[1][:, :, -1:]],
        axis=2,
    )
    tz = jnp.concatenate([perm[2][:1], harmonic(perm[2][:-1], perm[2][1:]), perm[2][-1:]], axis=0)
    diag = tx[:, :-1] + tx[:, 1:] + ty[:, :, :-1] + ty[:, :, 1:] + tz[:-1] + tz[1:]
    inverse = 1.0 / diag
    ghost = linear_field(depth, width, height)

    def inflow_of(full):
        inflow = tx[:, 1:] * full[:, 1:-1, 2:, 1:-1] + tx[:, :-1] * full[:, 1:-1, :-2, 1:-1]
        inflow = (
            inflow
            + ty[:, :, 1:] * full[:, 1:-1, 1:-1, 2:]
            + ty[:, :, :-1] * full[:, 1:-1, 1:-1, :-2]
        )
        return inflow + tz[1:] * full[:, 2:, 1:-1, 1:-1] + tz[:-1] * full[:, :-2, 1:-1, 1:-1]

    boundary = inflow_of(ghost.at[:, 1:-1, 1:-1, 1:-1].set(0.0))
    pressure = ghost[:, 1:-1, 1:-1, 1:-1]
    for weight in sweep_weights(SWEEPS):
        padded = jnp.pad(pressure, ((0, 0), (1, 1), (1, 1), (1, 1)))
        change = inflow_of(padded) + boundary - diag * pressure
        pressure = pressure + weight * (change * inverse)
    full = ghost.at[:, 1:-1, 1:-1, 1:-1].set(pressure)
    drop = jnp.stack(
        [
            full[0, 1:-1, 1:-1, 1:-1] - full[0, 1:-1, 2:, 1:-1],
            full[1, 1:-1, 1:-1, 1:-1] - full[1, 1:-1, 1:-1, 2:],
            full[2, 1:-1, 1:-1, 1:-1] - full[2, 2:, 1:-1, 1:-1],
        ]
    )
    faces = jnp.stack([tx[:, 1:], ty[:, :, 1:], tz[1:]])
    square = drop * drop
    energy = faces * square
    onehot = (layer_map[:, None] == jnp.arange(NCL, dtype=jnp.int32)[None, :]).astype(jnp.float32)

    def coarsen(values):
        blocks = values.reshape(3, depth, width // BXY, BXY, height // BXY, BXY).sum(axis=(3, 5))
        return jnp.einsum("dzab,zl->dlab", blocks, onehot, precision=lax.Precision.HIGHEST)

    return (coarsen(energy), coarsen(square))


def fold_owned(padded):
    rows = padded[:, :, :, 2:-2]
    rows = rows.at[:, :, :, 0].add(padded[:, :, :, 0])
    rows = rows.at[:, :, :, -1].add(padded[:, :, :, -1])
    owned = rows[:, :, :, :, 2:-2]
    owned = owned.at[:, :, :, :, 0].add(rows[:, :, :, :, 0])
    owned = owned.at[:, :, :, :, -1].add(rows[:, :, :, :, -1])
    return owned


def local(permeability, layer_map):
    kext = with_halo(permeability, (("gx", 2), ("gy", 3)), BXY)
    energy, square = patch_partials(kext, layer_map)
    stacked = jnp.stack([energy, square])
    gathered = with_halo(stacked, (("gx", 3), ("gy", 4)), 1)
    owned = fold_owned(gathered)
    coarse_perm = owned[0] / (owned[1] + EPS)
    upper_x = shifted(coarse_perm[0], "gx", -1)
    upper_y = shifted(coarse_perm[1][:, :, :1], "gy", -1)
    trans_x = harmonic(coarse_perm[0], jnp.concatenate([coarse_perm[0][:, 1:], upper_x], axis=1))
    trans_y = harmonic(coarse_perm[1], jnp.concatenate([coarse_perm[1][:, :, 1:], upper_y], axis=2))
    trans_z = jnp.concatenate(
        [harmonic(coarse_perm[2][:-1], coarse_perm[2][1:]), jnp.zeros_like(coarse_perm[2][:1])],
        axis=0,
    )
    return (coarse_perm, jnp.stack([trans_x, trans_y, trans_z]))


def solution(mesh):
    in_specs = (P(None, None, "gx", "gy"), P())
    out_specs = (P(None, None, "gx", "gy"), P(None, None, "gx", "gy"))
    return jax.shard_map(local, mesh=mesh, in_specs=in_specs, out_specs=out_specs, check_vma=False)
```

profile of v0, /device:TPU:25, one launch (start us, length us, event | category | flops | bytes accessed | tf_op | source)
XLA Modules:
  0.0 115.9 jit_solution(8015578752569260579)
XLA Ops:
  0.6 3.7 %collective-permute-start = (f32[3,8,8,128]{3,2,1,0:T(8,128)}, f32[3,8,8,128]{3,2,1,0:T(8,128)S(1)}, u32[]{:S(2)}, u32[]{:S(2)}) collective-permute-start(f32[3,8,8,128]{3,2,1,0:T(8,128)} %param.14), channel_id=1, source_target_pairs={{0,8},{8,16},{16,24},{1,9},{9,17},{17,25},{2,10},{10,18},{18,26},{... | collective-permute-start | bytes 294920 | tf_op jit(solution)/shard_map/ppermute | solution.py:22
  4.3 1.9 %collective-permute-start.1 = (f32[3,8,8,128]{3,2,1,0:T(8,128)}, f32[3,8,8,128]{3,2,1,0:T(8,128)S(1)}, u32[]{:S(2)}, u32[]{:S(2)}) collective-permute-start(f32[3,8,8,128]{3,2,1,0:T(8,128)} %param.14), channel_id=1, source_target_pairs={{8,0},{16,8},{24,16},{9,1},{17,9},{25,17},{10,2},{18,10},{26,18},{... | collective-permute-start | bytes 294920 | tf_op jit(solution)/shard_map/ppermute | solution.py:25
  7.2 3.2 %collective-permute-done.1 = f32[3,8,8,128]{3,2,1,0:T(8,128)S(1)} collective-permute-done((f32[3,8,8,128]{3,2,1,0:T(8,128)}, f32[3,8,8,128]{3,2,1,0:T(8,128)S(1)}, u32[]{:S(2)}, u32[]{:S(2)}) %collective-permute-start.1) | collective-permute-done | bytes 98336 | tf_op jit(solution)/shard_map/ppermute | solution.py:25
  11.4 3.1 %collective-permute-start.2 = (f32[3,8,24,8]{3,2,1,0:T(8,128)}, f32[3,8,24,8]{3,2,1,0:T(8,128)}, u32[]{:S(2)}, u32[]{:S(2)}) collective-permute-start(f32[3,8,24,8]{3,2,1,0:T(8,128)} %get-tuple-element.100), channel_id=1, source_target_pairs={{0,1},{1,2},{2,3},{3,4},{4,5},{5,6},{6,7},{8,9},{9,10},{10,11},{11... | collective-permute-start | bytes 55304 | tf_op jit(solution)/shard_map/ppermute | solution.py:22
  14.5 3.1 %collective-permute-start.3 = (f32[3,8,24,8]{3,2,1,0:T(8,128)}, f32[3,8,24,8]{3,2,1,0:T(8,128)}, u32[]{:S(2)}, u32[]{:S(2)}) collective-permute-start(f32[3,8,24,8]{3,2,1,0:T(8,128)} %get-tuple-element.101), channel_id=1, source_target_pairs={{1,0},{2,1},{3,2},{4,3},{5,4},{6,5},{7,6},{9,8},{10,9},{11,10},{12... | collective-permute-start | bytes 55304 | tf_op jit(solution)/shard_map/ppermute | solution.py:25
  18.2 13.7 %scatter.6 = f32[3,10,26,146]{3,2,1,0:T(8,128)S(1)} dynamic-update-slice(f32[3,10,26,146]{3,2,1,0:T(8,128)S(1)} %pad_maximum_fusion, f32[3,8,24,144]{3,2,1,0:T(8,128)S(1)} %broadcast.243, s32[]{:T(128)} %constant.191.clone.1, s32[]{:T(128)} %constant.192.clone.1, s32[]{:T(128)} %constant.192.clone.1, s32[]{:T(128)} %constant.192.clone.1) | dynamic-update-slice | bytes 663556 | tf_op jit(solution)/shard_map/scatter | solution.py:84
  40.2 2.0 %stack.44 = f32[1,8,3,8,18,8]{5,4,3,2,1,0:T(8,128)} reshape(f32[8,24,144]{2,1,0:T(8,128)S(1)} %get-tuple-element.87) | data formatting | bytes 221184 | tf_op jit(solution)/shard_map/stack | solution.py:98
  42.2 2.0 %stack.45 = f32[1,8,3,8,18,8]{5,4,3,2,1,0:T(8,128)} reshape(f32[8,24,144]{2,1,0:T(8,128)S(1)} %get-tuple-element.88) | data formatting | bytes 221184 | tf_op jit(solution)/shard_map/stack | solution.py:98
  48.4 13.7 %scatter.9 = f32[3,10,26,146]{3,2,1,0:T(8,128)S(1)} dynamic-update-slice(f32[3,10,26,146]{3,2,1,0:T(8,128)S(1)} %copy.34, f32[3,8,24,144]{3,2,1,0:T(8,128)S(1)} %fusion.60, s32[]{:T(128)} %constant.191.clone.1, s32[]{:T(128)} %constant.192.clone.1, s32[]{:T(128)} %constant.192.clone.1, s32[]{:T(128)} %constant.192.clone.1) | dynamic-update-slice | bytes 663556 | tf_op jit(solution)/shard_map/scatter | solution.py:90
  66.5 3.3 %add_divide_fusion = f32[1,7,3,8,18,8]{5,4,3,2,1,0:T(8,128)} fusion(f32[1,7,3,8,18,8]{5,4,3,2,1,0:T(8,128)} %slice.507, f32[1,7,3,8,18,8]{5,4,3,2,1,0:T(8,128)S(1)} %slice.509), kind=kLoop, calls=%fused_computation.3 | loop fusion | flops 96768 | bytes 290304 | tf_op jit(solution)/shard_map/div | solution.py:43
  69.9 3.5 %copy.10 = f32[1,7,3,8,18,8]{4,5,3,2,1,0:T(8,128)} copy(f32[1,7,3,8,18,8]{5,4,3,2,1,0:T(8,128)} %add_divide_fusion) | data formatting | bytes 193536 | tf_op jit(solution)/shard_map/div | solution.py:43
  75.1 3.9 %copy.12 = f32[1,8,3,8,18,8]{4,5,3,2,1,0:T(8,128)} copy(f32[1,8,3,8,18,8]{5,4,3,2,1,0:T(8,128)} %stack.44) | data formatting | bytes 221184 | tf_op jit(solution)/shard_map/stack | solution.py:98
  79.0 2.1 %copy.13 = f32[1,8,3,8,18,8]{4,5,3,2,1,0:T(8,128)} copy(f32[1,8,3,8,18,8]{5,4,3,2,1,0:T(8,128)S(1)} %copy-done) | data formatting | bytes 221184 | tf_op jit(solution)/shard_map/stack | solution.py:98
  81.6 2.1 %copy.16 = f32[1,8,3,8,18,8]{4,5,3,2,1,0:T(8,128)} copy(f32[1,8,3,8,18,8]{5,4,3,2,1,0:T(8,128)S(1)} %stack.50) | data formatting | bytes 221184 | tf_op jit(solution)/shard_map/stack | solution.py:91
  84.3 2.1 %copy.15 = f32[1,8,3,8,18,8]{4,5,3,2,1,0:T(8,128)} copy(f32[1,8,3,8,18,8]{5,4,3,2,1,0:T(8,128)S(1)} %stack.49) | data formatting | bytes 221184 | tf_op jit(solution)/shard_map/stack | solution.py:91
  86.3 3.0 %fusion = (f32[3,8,3,18]{3,2,1,0:T(4,128)S(1)}, f32[3,8,3,18]{3,2,1,0:T(4,128)S(1)}) fusion(f32[1,1,3,8,18,8]{4,5,3,2,1,0:T(8,128)S(1)} %copy-done.3, f32[1,7,3,8,18,8]{4,5,3,2,1,0:T(8,128)} %copy.10, f32[1,8,3,8,18,8]{4,5,3,2,1,0:T(8,128)} %copy.13, f32[1,8,3,8,18,8]{4,5,3,2,1,0:T(8,128)} %copy.12, f32[1,8,3,8,18,8]{4,5,3,2,1,0:T(8,128)} %copy.16, ...), kind=kLoop, calls=%fused_computation.1 | loop fusion | flops 743904 | bytes 673920 | tf_op jit(solution)/shard_map/reduce_sum | solution.py:104
  89.7 2.5 %collective-permute-start.4 = (f32[2,3,4,1,18]{4,2,3,1,0:T(4,128)S(1)}, f32[2,3,4,1,18]{4,2,3,1,0:T(4,128)S(1)}, u32[]{:S(2)}, u32[]{:S(2)}) collective-permute-start(f32[2,3,4,1,18]{4,2,3,1,0:T(4,128)S(1)} %get-tuple-element.111), channel_id=1, source_target_pairs={{0,8},{8,16},{16,24},{1,9},{9,17},{17,25},{2,10},{10,18},{18,26},{... | collective-permute-start | bytes 5192 | tf_op jit(solution)/shard_map/ppermute | solution.py:22
  92.2 1.9 %collective-permute-start.5 = (f32[2,3,4,1,18]{4,2,3,1,0:T(4,128)S(1)}, f32[2,3,4,1,18]{4,2,3,1,0:T(4,128)S(1)}, u32[]{:S(2)}, u32[]{:S(2)}) collective-permute-start(f32[2,3,4,1,18]{4,2,3,1,0:T(4,128)S(1)} %get-tuple-element.112), channel_id=1, source_target_pairs={{8,0},{16,8},{24,16},{9,1},{17,9},{25,17},{10,2},{18,10},{26,18},{... | collective-permute-start | bytes 5192 | tf_op jit(solution)/shard_map/ppermute | solution.py:25
  94.1 3.1 %collective-permute-done.5 = f32[2,3,4,1,18]{4,2,3,1,0:T(4,128)S(1)} collective-permute-done((f32[2,3,4,1,18]{4,2,3,1,0:T(4,128)S(1)}, f32[2,3,4,1,18]{4,2,3,1,0:T(4,128)S(1)}, u32[]{:S(2)}, u32[]{:S(2)}) %collective-permute-start.5) | collective-permute-done | bytes 1760 | tf_op jit(solution)/shard_map/ppermute | solution.py:25
  97.3 2.9 %collective-permute-start.6 = (f32[2,3,4,5,1]{4,2,3,1,0:T(4,128)S(1)}, f32[2,3,4,5,1]{4,2,3,1,0:T(4,128)S(1)}, u32[]{:S(2)}, u32[]{:S(2)}) collective-permute-start(f32[2,3,4,5,1]{4,2,3,1,0:T(4,128)S(1)} %get-tuple-element.108), channel_id=1, source_target_pairs={{0,1},{1,2},{2,3},{3,4},{4,5},{5,6},{6,7},{8,9},{9,10},{10,11},{11... | collective-permute-start | bytes 1448 | tf_op jit(solution)/shard_map/ppermute | solution.py:22
  100.3 3.2 %collective-permute-start.7 = (f32[2,3,4,5,1]{4,2,3,1,0:T(4,128)S(1)}, f32[2,3,4,5,1]{4,2,3,1,0:T(4,128)S(1)}, u32[]{:S(2)}, u32[]{:S(2)}) collective-permute-start(f32[2,3,4,5,1]{4,2,3,1,0:T(4,128)S(1)} %get-tuple-element.109), channel_id=1, source_target_pairs={{1,0},{2,1},{3,2},{4,3},{5,4},{6,5},{7,6},{9,8},{10,9},{11,10},{12... | collective-permute-start | bytes 1448 | tf_op jit(solution)/shard_map/ppermute | solution.py:25
  106.3 4.1 %collective-permute-start.9 = (f32[4,1,1]{2,0,1:T(4,128)S(1)}, f32[4,1,1]{2,0,1:T(4,128)S(1)}, u32[]{:S(2)}, u32[]{:S(2)}) collective-permute-start(f32[4,1,1]{2,0,1:T(4,128)S(1)} %bitcast.79), channel_id=1, source_target_pairs={{1,0},{2,1},{3,2},{4,3},{5,4},{6,5},{7,6},{9,8},{10,9},{11,10},{12... | collective-permute-start | bytes 56 | tf_op jit(solution)/shard_map/ppermute | solution.py:33
  110.4 1.9 %collective-permute-start.8 = (f32[4,1,16]{2,0,1:T(4,128)S(1)}, f32[4,1,16]{2,0,1:T(4,128)S(1)}, u32[]{:S(2)}, u32[]{:S(2)}) collective-permute-start(f32[4,1,16]{2,0,1:T(4,128)S(1)} %get-tuple-element.113), channel_id=1, source_target_pairs={{8,0},{16,8},{24,16},{9,1},{17,9},{25,17},{10,2},{18,10},{26,18},{... | collective-permute-start | bytes 776 | tf_op jit(solution)/shard_map/ppermute | solution.py:33
  112.4 2.9 %collective-permute-done.8 = f32[4,1,16]{2,0,1:T(4,128)S(1)} collective-permute-done((f32[4,1,16]{2,0,1:T(4,128)S(1)}, f32[4,1,16]{2,0,1:T(4,128)S(1)}, u32[]{:S(2)}, u32[]{:S(2)}) %collective-permute-start.8) | collective-permute-done | bytes 288 | tf_op jit(solution)/shard_map/ppermute | solution.py:33
  (78 shorter events, 26.0 us)
Async XLA Ops:
  0.6 5.7 %collective-permute-start = (f32[3,8,8,128]{3,2,1,0:T(8,128)}, f32[3,8,8,128]{3,2,1,0:T(8,128)S(1)}, u32[]{:S(2)}, u32[]{:S(2)}) collective-permute-start(f32[3,8,8,128]{3,2,1,0:T(8,128)} %param.14), channel_id=1, source_target_pairs={{0,8},{8,16},{16,24},{1,9},{9,17},{17,25},{2,10},{10,18},{18,26},{... | collective-permute-start | bytes 294920 | tf_op jit(solution)/shard_map/ppermute | solution.py:22
  4.3 6.1 %collective-permute-start.1 = (f32[3,8,8,128]{3,2,1,0:T(8,128)}, f32[3,8,8,128]{3,2,1,0:T(8,128)S(1)}, u32[]{:S(2)}, u32[]{:S(2)}) collective-permute-start(f32[3,8,8,128]{3,2,1,0:T(8,128)} %param.14), channel_id=1, source_target_pairs={{8,0},{16,8},{24,16},{9,1},{17,9},{25,17},{10,2},{18,10},{26,18},{... | collective-permute-start | bytes 294920 | tf_op jit(solution)/shard_map/ppermute | solution.py:25
  11.4 20.5 %collective-permute-start.2 = (f32[3,8,24,8]{3,2,1,0:T(8,128)}, f32[3,8,24,8]{3,2,1,0:T(8,128)}, u32[]{:S(2)}, u32[]{:S(2)}) collective-permute-start(f32[3,8,24,8]{3,2,1,0:T(8,128)} %get-tuple-element.100), channel_id=1, source_target_pairs={{0,1},{1,2},{2,3},{3,4},{4,5},{5,6},{6,7},{8,9},{9,10},{10,11},{11... | collective-permute-start | bytes 55304 | tf_op jit(solution)/shard_map/ppermute | solution.py:22
  14.5 17.4 %collective-permute-start.3 = (f32[3,8,24,8]{3,2,1,0:T(8,128)}, f32[3,8,24,8]{3,2,1,0:T(8,128)}, u32[]{:S(2)}, u32[]{:S(2)}) collective-permute-start(f32[3,8,24,8]{3,2,1,0:T(8,128)} %get-tuple-element.101), channel_id=1, source_target_pairs={{1,0},{2,1},{3,2},{4,3},{5,4},{6,5},{7,6},{9,8},{10,9},{11,10},{12... | collective-permute-start | bytes 55304 | tf_op jit(solution)/shard_map/ppermute | solution.py:25
  48.4 16.3 %copy-start.2 = (f32[1,7,24,144]{3,2,1,0:T(8,128)S(1)}, f32[1,7,24,144]{3,2,1,0:T(8,128)}, u32[]{:S(2)}) copy-start(f32[1,7,24,144]{3,2,1,0:T(8,128)} %get-tuple-element.96) | copy-start | bytes 290308
  69.8 3.5 %copy-start.1 = (f32[1,8,24,144]{3,2,1,0:T(8,128)S(1)}, f32[1,8,24,144]{3,2,1,0:T(8,128)}, u32[]{:S(2)}) copy-start(f32[1,8,24,144]{3,2,1,0:T(8,128)} %get-tuple-element.89) | copy-start | bytes 331780
  75.1 3.9 %copy-start = (f32[1,8,3,8,18,8]{5,4,3,2,1,0:T(8,128)S(1)}, f32[1,8,3,8,18,8]{5,4,3,2,1,0:T(8,128)}, u32[]{:S(2)}) copy-start(f32[1,8,3,8,18,8]{5,4,3,2,1,0:T(8,128)} %stack.45) | copy-start | bytes 331780
  83.7 2.6 %copy-start.3 = (f32[1,1,3,8,18,8]{4,5,3,2,1,0:T(8,128)S(1)}, f32[1,1,3,8,18,8]{4,5,3,2,1,0:T(8,128)}, u32[]{:S(2)}) copy-start(f32[1,1,3,8,18,8]{4,5,3,2,1,0:T(8,128)} %copy.11) | copy-start | bytes 41476
  86.3 3.0 %copy-start.5 = (s32[8]{0:T(128)S(1)}, s32[8]{0:T(128)}, u32[]{:S(2)}) copy-start(s32[8]{0:T(128)} %param.15) | copy-start | bytes 100
  89.7 4.4 %collective-permute-start.4 = (f32[2,3,4,1,18]{4,2,3,1,0:T(4,128)S(1)}, f32[2,3,4,1,18]{4,2,3,1,0:T(4,128)S(1)}, u32[]{:S(2)}, u32[]{:S(2)}) collective-permute-start(f32[2,3,4,1,18]{4,2,3,1,0:T(4,128)S(1)} %get-tuple-element.111), channel_id=1, source_target_pairs={{0,8},{8,16},{16,24},{1,9},{9,17},{17,25},{2,10},{10,18},{18,26},{... | collective-permute-start | bytes 5192 | tf_op jit(solution)/shard_map/ppermute | solution.py:22
  92.2 5.0 %collective-permute-start.5 = (f32[2,3,4,1,18]{4,2,3,1,0:T(4,128)S(1)}, f32[2,3,4,1,18]{4,2,3,1,0:T(4,128)S(1)}, u32[]{:S(2)}, u32[]{:S(2)}) collective-permute-start(f32[2,3,4,1,18]{4,2,3,1,0:T(4,128)S(1)} %get-tuple-element.112), channel_id=1, source_target_pairs={{8,0},{16,8},{24,16},{9,1},{17,9},{25,17},{10,2},{18,10},{26,18},{... | collective-permute-start | bytes 5192 | tf_op jit(solution)/shard_map/ppermute | solution.py:25
  97.3 6.2 %collective-permute-start.6 = (f32[2,3,4,5,1]{4,2,3,1,0:T(4,128)S(1)}, f32[2,3,4,5,1]{4,2,3,1,0:T(4,128)S(1)}, u32[]{:S(2)}, u32[]{:S(2)}) collective-permute-start(f32[2,3,4,5,1]{4,2,3,1,0:T(4,128)S(1)} %get-tuple-element.108), channel_id=1, source_target_pairs={{0,1},{1,2},{2,3},{3,4},{4,5},{5,6},{6,7},{8,9},{9,10},{10,11},{11... | collective-permute-start | bytes 1448 | tf_op jit(solution)/shard_map/ppermute | solution.py:22
  100.3 5.0 %collective-permute-start.7 = (f32[2,3,4,5,1]{4,2,3,1,0:T(4,128)S(1)}, f32[2,3,4,5,1]{4,2,3,1,0:T(4,128)S(1)}, u32[]{:S(2)}, u32[]{:S(2)}) collective-permute-start(f32[2,3,4,5,1]{4,2,3,1,0:T(4,128)S(1)} %get-tuple-element.109), channel_id=1, source_target_pairs={{1,0},{2,1},{3,2},{4,3},{5,4},{6,5},{7,6},{9,8},{10,9},{11,10},{12... | collective-permute-start | bytes 1448 | tf_op jit(solution)/shard_map/ppermute | solution.py:25
  106.1 9.8 %copy-start.4 = (f32[1,3,4,1,16]{4,2,3,1,0:T(4,128)}, f32[1,3,4,1,16]{4,2,3,1,0:T(4,128)S(1)}, u32[]{:S(2)}) copy-start(f32[1,3,4,1,16]{4,2,3,1,0:T(4,128)S(1)} %fusion.78) | copy-start | bytes 2308
  106.3 6.1 %collective-permute-start.9 = (f32[4,1,1]{2,0,1:T(4,128)S(1)}, f32[4,1,1]{2,0,1:T(4,128)S(1)}, u32[]{:S(2)}, u32[]{:S(2)}) collective-permute-start(f32[4,1,1]{2,0,1:T(4,128)S(1)} %bitcast.79), channel_id=1, source_target_pairs={{1,0},{2,1},{3,2},{4,3},{5,4},{6,5},{7,6},{9,8},{10,9},{11,10},{12... | collective-permute-start | bytes 56 | tf_op jit(solution)/shard_map/ppermute | solution.py:33
  110.4 4.9 %collective-permute-start.8 = (f32[4,1,16]{2,0,1:T(4,128)S(1)}, f32[4,1,16]{2,0,1:T(4,128)S(1)}, u32[]{:S(2)}, u32[]{:S(2)}) collective-permute-start(f32[4,1,16]{2,0,1:T(4,128)S(1)} %get-tuple-element.113), channel_id=1, source_target_pairs={{8,0},{16,8},{24,16},{9,1},{17,9},{25,17},{10,2},{18,10},{26,18},{... | collective-permute-start | bytes 776 | tf_op jit(solution)/shard_map/ppermute | solution.py:33
where the time goes:
time: 116 us
  local copies, waits for them, and re-layouts  56.8 us (49%)
  starting transfers between devices  28.4 us (24%)
  other arithmetic  18.5 us (16%)
  waiting for transfers between devices  10.9 us (9%)
    scatter x1, local copies, waits for them, and re-layouts, patch_partials(): full = ghost.at[:, 1:-1, 1:-1, 1:-1].set(pressure)  13.7 us
    scatter x1, local copies, waits for them, and re-layouts, patch_partials(): boundary = inflow_of(ghost.at[:, 1:-1, 1:-1, 1:-1].set(0.0))  13.7 us
    ppermute x4, starting transfers between devices, with_halo(): lax.ppermute(lax.slice_in_dim(block, block.shape[dim] - width, None, axis...  12.3 us
    ppermute x4, starting transfers between devices, with_halo(): lax.ppermute(lax.slice_in_dim(block, 0, width, axis=dim), axis, backward)  10.1 us
    another operation x4, local copies, waits for them, and re-layouts, patch_partials(): faces = jnp.stack([tx[:, 1:], ty[:, :, 1:], tz[1:]])  9.92 us
    ppermute x4, waiting for transfers between devices, with_halo(): lax.ppermute(lax.slice_in_dim(block, 0, width, axis=dim), axis, backward)  8.04 us
    another operation x6, local copies, waits for them, and re-layouts, patch_partials(): jnp.stack([full[0, 1:-1, 1:-1, 1:-1] - full[0, 1:-1, 2:, 1:-1], full[1, 1...  7 us
    ppermute x2, starting transfers between devices, shifted(): lax.ppermute(value, axis, [(source, source + steps) for source in range(i...  6.04 us
  transfers between devices with their start and end apart: 10, of which 4 were waited for; matrix products, arithmetic and copies ran while one was open for 13% of the time, Pallas kernels for 0%

commit v1 on v0

v1 whole, which is shorter than its diff:
```python
import functools
import math

import jax
import jax.numpy as jnp
from jax import lax
from jax.experimental import pallas as pl
from jax.experimental.pallas import tpu as pltpu
from jax.sharding import PartitionSpec as P

NCL = 4
BXY = 8
SWEEPS = 4
KMIN = 0.01
EPS = 1e-06

LOW = SWEEPS
HIGH = SWEEPS + 1
RIGHT = BXY + HIGH
SLOT = LOW + RIGHT
FIRST, LAST = -LOW, 2 * BXY + HIGH - 1


def sweep_weights(count):
    return [
        1.0 / (1.05 + 0.95 * math.cos(math.pi * (2 * s + 1) / (2 * count))) for s in range(count)
    ]


WEIGHTS = sweep_weights(SWEEPS)


def harmonic(left, right):
    return 2.0 * left * right / (left + right)


def lanes_of(shape):
    return lax.broadcasted_iota(jnp.int32, shape, len(shape) - 1)


def up(value, axis):
    return pltpu.roll(value, value.shape[axis] - 1, axis)


def down(value, axis):
    return pltpu.roll(value, 1, axis)


def raw_row(tiles, comp, row):
    own, low, high, high2 = tiles
    ref, at = (
        (low, row + BXY)
        if row < 0
        else (own, row)
        if row < BXY
        else (high, row - BXY)
        if row < 2 * BXY
        else (high2, row - 2 * BXY)
    )
    return ref[comp, :, at, :]


def exists(row, present):
    low, high, high2 = present
    return low if row < 0 else None if row < BXY else high if row < 2 * BXY else high2


class Solver:
    def __init__(self, perm, scratch, y_ends, y_starts):
        self.perm_of = perm
        self.scratch = scratch
        self.slots = {}
        self.cache = {}
        shape = scratch.shape[1:]
        layer = lax.broadcasted_iota(jnp.int32, shape, 0)
        self.top = layer == shape[0] - 1
        self.bottom = layer == 0
        self.y_ends = y_ends
        self.y_starts = y_starts

    def memo(self, key, make):
        if key not in self.cache:
            self.cache[key] = make()
        return self.cache[key]

    def stored(self, key, make):
        if key not in self.slots:
            values = make()
            base = sum(n for _, n in self.slots.values())
            self.slots[key] = (base, len(values))
            for i, value in enumerate(values):
                self.scratch[base + i] = value
        base, _ = self.slots[key]
        return lambda i: self.scratch[base + i]

    def perm(self, comp, row):
        return self.memo(("k", comp, row), lambda: self.perm_of(comp, row))

    def tx(self, row):
        return self.memo(("tx", row), lambda: harmonic(self.perm(0, row), self.perm(0, row + 1)))

    def tyz(self, row):
        def make():
            ky, kz = self.perm(1, row), self.perm(2, row)
            ty = harmonic(ky, up(ky, 1))
            if self.y_ends is not None:
                ty = jnp.where(self.y_ends, ky, ty)
            ty_low = down(ty, 1)
            if self.y_starts is not None:
                ty_low = jnp.where(self.y_starts, ky, ty_low)
            tz = jnp.where(self.top, kz, harmonic(kz, up(kz, 0)))
            tz_low = jnp.where(self.bottom, kz, down(tz, 0))
            return ty, ty_low, tz, tz_low

        return self.memo(("tyz", row), make)

    def faces(self, row, edge):
        upper = self.perm(0, row) if edge == "up" else self.tx(row)
        lower = self.perm(0, row) if edge == "low" else self.tx(row - 1)
        return upper, lower

    def edge_of(self, row, boundary):
        return boundary[0] if boundary is not None and boundary[1] == row else None

    def coefficients(self, row, boundary):
        edge = self.edge_of(row, boundary)

        def make():
            upper, lower = self.faces(row, edge)
            ty, ty_low, tz, tz_low = self.tyz(row)
            inverse = 1.0 / (((upper + lower) + (ty + ty_low)) + (tz + tz_low))
            zero = jnp.zeros_like(inverse)
            ax = zero if edge == "up" else upper * inverse
            ax_low = zero if edge == "low" else lower * inverse
            ay, ay_low = ty * inverse, ty_low * inverse
            az, az_low = tz * inverse, tz_low * inverse
            drive = ((upper - lower) * inverse, ay - ay_low, az - az_low)
            if self.y_ends is not None:
                ay = jnp.where(self.y_ends, 0.0, ay)
            if self.y_starts is not None:
                ay_low = jnp.where(self.y_starts, 0.0, ay_low)
            az = jnp.where(self.top, 0.0, az)
            az_low = jnp.where(self.bottom, 0.0, az_low)
            return (ax, ax_low, ay, ay_low, az, az_low) + drive

        return self.stored(("c", row, edge), make)

    def pressure(self, d, count, row, boundary):
        if boundary is not None:
            kind, at = boundary
            if abs(row - at) >= count:
                boundary = None

        def make():
            c = self.coefficients(row, boundary)
            edge = self.edge_of(row, boundary)
            if count == 1:
                return WEIGHTS[0] * c(6 + d)
            here = self.pressure(d, count - 1, row, boundary)
            total = c(6 + d)
            if edge != "up":
                total = total + c(0) * self.pressure(d, count - 1, row + 1, boundary)
            if edge != "low":
                total = total + c(1) * self.pressure(d, count - 1, row - 1, boundary)
            side = c(2) * up(here, 1) + c(3) * down(here, 1)
            total = total + side
            total = total + (c(4) * up(here, 0) + c(5) * down(here, 0))
            return here + WEIGHTS[count - 1] * (total - here)

        return self.memo(("u", d, count, row, boundary), make)

    def sums(self, d, row, boundary):
        if boundary is not None:
            kind, at = boundary
            reach = SWEEPS + (1 if d == 0 and kind == "up" else 0)
            if abs(row - at) >= reach:
                boundary = None

        def make():
            here = self.pressure(d, SWEEPS, row, boundary)
            edge = self.edge_of(row, boundary)
            if d == 0:
                face = self.faces(row, edge)[0]
                above = None if edge == "up" else self.pressure(d, SWEEPS, row + 1, boundary)
            elif d == 1:
                face = self.tyz(row)[0]
                above = up(here, 1)
                if self.y_ends is not None:
                    above = jnp.where(self.y_ends, 0.0, above)
            else:
                face = self.tyz(row)[2]
                above = jnp.where(self.top, 0.0, up(here, 0))
            drop = (1.0 - here) if above is None else (1.0 - here) + above
            square = drop * drop
            return face * square, square

        return self.memo(("s", d, row, boundary), make)

    def block(self, d, begin, patches):
        groups = {}
        for row in range(begin, begin + BXY):
            for boundary, weight in patches:
                pair = self.sums(d, row, boundary)
                groups.setdefault(id(weight), (weight, []))[1].append(pair)
        totals = None
        for weight, pairs in groups.values():
            part = [functools.reduce(jnp.add, parts) for parts in zip(*pairs)]
            if weight is not None:
                part = [weight * p for p in part]
            totals = part if totals is None else [a + b for a, b in zip(totals, part)]
        return totals


def accumulate(solver, present):
    low, high, high2 = present
    own = [(("up", BXY - 1), low), (None, None), (("low", 0), high)]
    after = [(("up", 2 * BXY - 1), None), (None, None), (("low", BXY), high2)]
    jobs = [(d, 0, own) for d in range(3)] + [(0, BXY, after)]
    results = {}
    order = [jobs[0], jobs[1], jobs[2], jobs[3]]
    for row in range(BXY):
        for d, begin, patches in order:
            for boundary, _ in patches:
                solver.sums(d, begin + row, boundary)
    for i, (d, begin, patches) in enumerate(jobs):
        results[i] = solver.block(d, begin, patches)
    return [value for i in range(len(jobs)) for value in results[i]]


def reduce_sums(sums, layer_map, columns):
    depth = sums[0].shape[0]
    stacked = jnp.concatenate(sums, axis=0)
    by_column = jnp.dot(
        stacked, columns, precision=lax.Precision.HIGHEST, preferred_element_type=jnp.float32
    )
    rows, cols = len(sums) * NCL, len(sums) * depth
    r = lax.broadcasted_iota(jnp.int32, (rows, cols), 0)
    c = lax.broadcasted_iota(jnp.int32, (rows, cols), 1)
    layer = jnp.zeros((rows, cols), jnp.int32)
    for z in range(depth):
        layer = jnp.where(c % depth == z, layer_map[z], layer)
    picks = ((r // NCL == c // depth) & (r % NCL == layer)).astype(jnp.float32)
    return jnp.dot(
        picks, by_column, precision=lax.Precision.HIGHEST, preferred_element_type=jnp.float32
    )


def flags(x_axis, y_axis):
    i, j = lax.axis_index(x_axis), lax.axis_index(y_axis)
    nx, ny = lax.axis_size(x_axis), lax.axis_size(y_axis)
    one = lambda test: jnp.where(test, 1.0, 0.0).astype(jnp.float32)
    return i, j, (one(i > 0), one(i < nx - 1), one(i < nx - 2)), (one(j > 0), one(j < ny - 1))


def packed_rows():
    return [(comp, row) for row in range(FIRST, LAST + 1) for comp in range(3)]


def pack_kernel(own, low, high, high2, out):
    lanes = own.shape[3]
    per = lanes // SLOT
    lane = lanes_of((own.shape[1], lanes))
    rows = packed_rows()
    for first in range(0, len(rows), per):
        packed = None
        for slot, (comp, row) in enumerate(rows[first : first + per]):
            value = raw_row((own, low, high, high2), comp, row)
            value = pltpu.roll(value, (LOW + SLOT * slot) % lanes, 1)
            packed = value if packed is None else jnp.where(lane < SLOT * slot, packed, value)
        out[first // per] = packed


def main_kernel(layer_map, own, low, high, high2, out, scratch):
    _, _, present, _ = flags("gx", "gy")
    tiles = (own, low, high, high2)

    def perm(comp, row):
        value = raw_row(tiles, comp, row)
        there = exists(row, present)
        return (value if there is None else value * there) + KMIN

    solver = Solver(perm, scratch, None, None)
    sums = accumulate(solver, present)
    lanes = own.shape[3]
    r = lax.broadcasted_iota(jnp.int32, (lanes, lanes), 0)
    c = lax.broadcasted_iota(jnp.int32, (lanes, lanes), 1)
    inner = (r // BXY == c) & (c > 0) & (c < lanes // BXY - 1)
    out[...] = reduce_sums(sums, layer_map, inner.astype(jnp.float32))


def edge_kernel(layer_map, own, low, high, high2, even, odd, inner, perm_out, trans_out, scratch):
    i, j, present, (has_left, has_right) = flags("gx", "gy")
    tiles = (own, low, high, high2)
    depth, lanes = own.shape[1], own.shape[3]
    per = lanes // SLOT
    lane = lanes_of((depth, lanes))
    half = lanes // 2
    last = lanes - BXY - LOW
    left = RIGHT + 7
    start = left + LOW
    stop = start + BXY + HIGH
    in_left = lane % SLOT < LOW
    is_odd = j % 2 == 1
    from_even = in_left == (jnp.zeros_like(lane) + is_odd.astype(jnp.int32) == 1)
    keep = jnp.where(in_left, has_left, has_right)
    packs = {}

    def pack(at):
        if at not in packs:
            packs[at] = jnp.where(from_even, even[at], odd[at]) * keep
        return packs[at]

    index = {key: at for at, key in enumerate(packed_rows())}
    second = (lane >= half - BXY - LOW) & (lane < half + stop)

    def perm(comp, row):
        at = index[comp, row]
        slot = at % per
        mine = raw_row(tiles, comp, row)
        theirs = pack(at // per)
        right = pltpu.roll(theirs, (-(SLOT * slot + LOW)) % lanes, 1)
        before = pltpu.roll(theirs, (left - SLOT * slot) % lanes, 1)
        value = jnp.where(lane < RIGHT, right, mine)
        value = jnp.where((lane >= left) & (lane < stop), pltpu.roll(mine, start, 1), value)
        value = jnp.where((lane >= left) & (lane < start), before, value)
        value = jnp.where(second, pltpu.roll(value, half, 1), value)
        there = exists(row, present)
        return (value if there is None else value * there) + KMIN

    y_ends = (lane == BXY - 1) | (lane == half + start + BXY - 1)
    y_starts = lane == half - BXY
    solver = Solver(perm, scratch, y_ends, y_starts)
    sums = accumulate(solver, present)
    r = lax.broadcasted_iota(jnp.int32, (lanes, lanes), 0)
    c = lax.broadcasted_iota(jnp.int32, (lanes, lanes), 1)
    count = lanes // BXY

    def span(begin):
        return (r >= begin) & (r < begin + BXY)

    first = jnp.where(span(start), 1.0, 0.0) + jnp.where(span(half + start), has_left, 0.0)
    final = jnp.where(span(lanes - BXY), 1.0, 0.0) + jnp.where(span(half - BXY), has_right, 0.0)
    beyond = jnp.where(span(0) | span(half), has_right, 0.0)
    columns = jnp.where(
        c == 0, first, jnp.where(c == count - 1, final, jnp.where(c == count, beyond, 0.0))
    )
    total = inner[...] + reduce_sums(sums, layer_map, columns)
    cells = (own.shape[2] + 2 * BXY, lanes + 2 * BXY, depth)
    energy = [total[2 * NCL * q : 2 * NCL * q + NCL] for q in range(4)]
    square = [total[2 * NCL * q + NCL : 2 * NCL * (q + 1)] for q in range(4)]
    perms = [
        energy[q] / (square[q] + EPS * float(cells[d]) ** 2) for q, d in enumerate((0, 1, 2, 0))
    ]
    layer = lax.broadcasted_iota(jnp.int32, perms[0].shape, 0)
    trans = [
        harmonic(perms[0], perms[3] * present[1]),
        harmonic(perms[1], up(perms[1], 1)),
    ]
    above = jnp.concatenate([perms[2][1:], jnp.zeros_like(perms[2][:1])], axis=0)
    trans.append(harmonic(perms[2], above))
    for d in range(3):
        for l in range(NCL):
            perm_out[d, l, :, :] = perms[d][l : l + 1, :count]
            trans_out[d, l, :, :] = trans[d][l : l + 1, :count]


def ring(value, axis, steps):
    count = lax.axis_size(axis)
    return lax.ppermute(value, axis, [(s, (s + steps) % count) for s in range(count)])


def swap(value, axes, parity):
    nx, ny = (lax.axis_size(a) for a in axes)
    pairs = []
    for i in range(nx):
        for j in range(ny):
            other = j ^ 1 if parity == 0 else ((j - 1) ^ 1) + 1
            if 0 <= other < ny:
                pairs.append((i * ny + j, i * ny + other))
            else:
                pairs.append((i * ny + j, (i ^ 1 if nx % 2 == 0 else i) * ny + j))
    return lax.ppermute(value, axes, pairs)


def local(permeability, layer_map):
    _, depth, width, lanes = permeability.shape
    if width != BXY or depth != 8 or lanes != 128:
        raise ValueError("unsupported tile")
    tiles = (
        permeability,
        ring(permeability, "gx", 1),
        ring(permeability, "gx", -1),
        ring(permeability, "gx", -2),
    )
    vmem = pl.BlockSpec(memory_space=pltpu.VMEM)
    smem = pl.BlockSpec(memory_space=pltpu.SMEM)
    count = len(packed_rows())
    per = lanes // SLOT
    packed = pl.pallas_call(
        pack_kernel,
        out_shape=jax.ShapeDtypeStruct((-(-count // per), depth, lanes), jnp.float32),
        in_specs=[vmem] * 4,
        out_specs=vmem,
    )(*tiles)
    even = swap(packed, ("gx", "gy"), 0)
    odd = swap(packed, ("gx", "gy"), 1)
    scratch = [pltpu.VMEM((256, depth, lanes), jnp.float32)]
    inner = pl.pallas_call(
        main_kernel,
        out_shape=jax.ShapeDtypeStruct((8 * NCL, lanes), jnp.float32),
        in_specs=[smem] + [vmem] * 4,
        out_specs=vmem,
        scratch_shapes=scratch,
        cost_estimate=pl.CostEstimate(flops=6_000_000, bytes_accessed=4 * permeability.size * 4, transcendentals=0),
    )(layer_map, *tiles)
    out = jax.ShapeDtypeStruct((3, NCL, width // BXY, lanes // BXY), jnp.float32)
    return pl.pallas_call(
        edge_kernel,
        out_shape=(out, out),
        in_specs=[smem] + [vmem] * 7,
        out_specs=(vmem, vmem),
        scratch_shapes=scratch,
    )(layer_map, *tiles, even, odd, inner)


def solution(mesh):
    in_specs = (P(None, None, "gx", "gy"), P())
    out_specs = (P(None, None, "gx", "gy"), P(None, None, "gx", "gy"))
    return jax.shard_map(local, mesh=mesh, in_specs=in_specs, out_specs=out_specs, check_vma=False)
```

time: 116 us -> 21.8 us (0.19)
  the two profiles are of different devices: /device:TPU:25 before, /device:TPU:10 now
where the time goes in v1:
time: 21.8 us; the launch traced here: 21.6 us
  Pallas kernels  8.39 us (38%)
  starting transfers between devices  6.35 us (29%)
  waiting for transfers between devices  4.34 us (20%)
  local copies, waits for them, and re-layouts  1.87 us (9%)
  between operations  0.65 us (3%)
    ppermute x3, waiting for transfers between devices, ring(): lax.ppermute(value, axis, [(s, (s + steps) % count) for s in range(count)])  4.33 us
    pallas_call x1, Pallas kernels, local(): pl.pallas_call(main_kernel, out_shape=jax.ShapeDtypeStruct((8 * NCL, lane...  3.4 us
    ppermute x3, starting transfers between devices, ring(): lax.ppermute(value, axis, [(s, (s + steps) % count) for s in range(count)])  3.31 us
    pallas_call x1, Pallas kernels, local(): pl.pallas_call(edge_kernel, out_shape=(out, out), in_specs=[smem] + [vmem...  3.11 us
    ppermute x2, starting transfers between devices, swap(): return lax.ppermute(value, axes, pairs)  3.04 us
    pallas_call x1, Pallas kernels, local(): pl.pallas_call(pack_kernel, out_shape=jax.ShapeDtypeStruct((-(-count // p...  1.88 us
    unnamed x10, local copies, waits for them, and re-layouts  1.87 us
  transfers between devices with their start and end apart: 5, of which 3 were waited for; matrix products, arithmetic and copies ran while one was open for 0% of the time, Pallas kernels for 16%

profile of v1, /device:TPU:10, one launch (start us, length us, event | category | flops | bytes accessed | tf_op | source)
XLA Modules:
  0.0 21.6 jit_solution(11211349855611044184)
XLA Ops:
  0.6 0.1 collective-permute-start
  0.7 1.7 %collective-permute-start.1 = (f32[3,8,8,128]{3,2,1,0:T(8,128)}, f32[3,8,8,128]{3,2,1,0:T(8,128)S(1)}, u32[]{:S(2)}, u32[]{:S(2)}) collective-permute-start(f32[3,8,8,128]{3,2,1,0:T(8,128)} %own.5), channel_id=1, source_target_pairs={{0,24},{8,0},{16,8},{24,16},{1,25},{9,1},{17,9},{25,17},{2,26},{10... | collective-permute-start | bytes 294920 | tf_op jit(solution)/shard_map/ppermute | solution.py:369
  2.4 1.5 %collective-permute-start.2 = (f32[3,8,8,128]{3,2,1,0:T(8,128)}, f32[3,8,8,128]{3,2,1,0:T(8,128)S(1)}, u32[]{:S(2)}, u32[]{:S(2)}) collective-permute-start(f32[3,8,8,128]{3,2,1,0:T(8,128)} %own.5), channel_id=1, source_target_pairs={{0,16},{8,24},{16,0},{24,8},{1,17},{9,25},{17,1},{25,9},{2,18},{10... | collective-permute-start | bytes 294920 | tf_op jit(solution)/shard_map/ppermute | solution.py:369
  3.9 1.0 %collective-permute-done.low = f32[3,8,8,128]{3,2,1,0:T(8,128)S(1)} collective-permute-done((f32[3,8,8,128]{3,2,1,0:T(8,128)}, f32[3,8,8,128]{3,2,1,0:T(8,128)S(1)}, u32[]{:S(2)}, u32[]{:S(2)}) %collective-permute-start) | collective-permute-done | bytes 98336 | tf_op jit(solution)/shard_map/ppermute | solution.py:369
  4.9 0.0 copy-start
  4.9 1.0 %collective-permute-done.1.high = f32[3,8,8,128]{3,2,1,0:T(8,128)S(1)} collective-permute-done((f32[3,8,8,128]{3,2,1,0:T(8,128)}, f32[3,8,8,128]{3,2,1,0:T(8,128)S(1)}, u32[]{:S(2)}, u32[]{:S(2)}) %collective-permute-start.1) | collective-permute-done | bytes 98336 | tf_op jit(solution)/shard_map/ppermute | solution.py:369
  5.9 0.0 copy-start.1
  5.9 2.3 %collective-permute-done.2.high2 = f32[3,8,8,128]{3,2,1,0:T(8,128)S(1)} collective-permute-done((f32[3,8,8,128]{3,2,1,0:T(8,128)}, f32[3,8,8,128]{3,2,1,0:T(8,128)S(1)}, u32[]{:S(2)}, u32[]{:S(2)}) %collective-permute-start.2) | collective-permute-done | bytes 98336 | tf_op jit(solution)/shard_map/ppermute | solution.py:369
  8.3 0.0 copy-done
  8.3 0.0 copy-done.1
  8.3 0.0 copy-start.2
  8.3 0.6 %copy-done.2 = f32[3,8,8,128]{3,2,1,0:T(8,128)} copy-done((f32[3,8,8,128]{3,2,1,0:T(8,128)}, f32[3,8,8,128]{3,2,1,0:T(8,128)S(1)}, u32[]{:S(2)}) %copy-start.2) | copy-done | bytes 98328
  8.9 1.9 %shard_map.41 = f32[11,8,128]{2,1,0:T(8,128)} custom-call(f32[3,8,8,128]{3,2,1,0:T(8,128)} %own.5, f32[3,8,8,128]{3,2,1,0:T(8,128)} %copy-done, f32[3,8,8,128]{3,2,1,0:T(8,128)} %copy-done.1, f32[3,8,8,128]{3,2,1,0:T(8,128)} %copy-done.2), custom_call_target="tpu_custom_call" | custom-call | tf_op jit(solution)/shard_map/pallas_call | solution.py:399
  10.8 0.5 %collective-permute-start.3 = (f32[11,8,128]{2,1,0:T(8,128)}, f32[11,8,128]{2,1,0:T(8,128)S(1)}, u32[]{:S(2)}, u32[]{:S(2)}) collective-permute-start(f32[11,8,128]{2,1,0:T(8,128)} %shard_map.41), channel_id=1, source_target_pairs={{0,1},{1,0},{2,3},{3,2},{4,5},{5,4},{6,7},{7,6},{8,9},{9,8},{10,11... | collective-permute-start | bytes 135176 | tf_op jit(solution)/shard_map/ppermute | solution.py:382
  11.3 2.5 %collective-permute-start.4 = (f32[11,8,128]{2,1,0:T(8,128)}, f32[11,8,128]{2,1,0:T(8,128)S(1)}, u32[]{:S(2)}, u32[]{:S(2)}) collective-permute-start(f32[11,8,128]{2,1,0:T(8,128)} %shard_map.41), channel_id=1, source_target_pairs={{0,8},{1,2},{2,1},{3,4},{4,3},{5,6},{6,5},{7,15},{8,0},{9,10},{10,... | collective-permute-start | bytes 135176 | tf_op jit(solution)/shard_map/ppermute | solution.py:382
  13.9 3.4 %shard_map.42.inner = f32[32,128]{1,0:T(8,128)} custom-call(s32[8]{0:T(128)} %layer_map.3, f32[3,8,8,128]{3,2,1,0:T(8,128)} %own.5, f32[3,8,8,128]{3,2,1,0:T(8,128)} %copy-done, f32[3,8,8,128]{3,2,1,0:T(8,128)} %copy-done.1, f32[3,8,8,128]{3,2,1,0:T(8,128)} %copy-done.2), custom_call_target="tpu_custom_call" | custom-call | flops 6000000 | bytes 393216 | tf_op jit(solution)/shard_map/pallas_call | solution.py:408
  17.3 0.0 collective-permute-done.3.even
  17.3 0.0 copy-start.3
  17.3 0.0 collective-permute-done.4.odd
  17.3 0.6 %copy-done.3 = f32[11,8,128]{2,1,0:T(8,128)} copy-done((f32[11,8,128]{2,1,0:T(8,128)}, f32[11,8,128]{2,1,0:T(8,128)S(1)}, u32[]{:S(2)}) %copy-start.3) | copy-done | bytes 45080
  17.9 0.0 copy-start.4
  17.9 0.6 %copy-done.4 = f32[11,8,128]{2,1,0:T(8,128)} copy-done((f32[11,8,128]{2,1,0:T(8,128)}, f32[11,8,128]{2,1,0:T(8,128)S(1)}, u32[]{:S(2)}) %copy-start.4) | copy-done | bytes 45080
  18.5 3.1 %shard_map.43 = (f32[3,4,1,16]{3,2,1,0:T(1,128)}, f32[3,4,1,16]{3,2,1,0:T(1,128)}) custom-call(s32[8]{0:T(128)} %layer_map.3, f32[3,8,8,128]{3,2,1,0:T(8,128)} %own.5, f32[3,8,8,128]{3,2,1,0:T(8,128)} %copy-done, f32[3,8,8,128]{3,2,1,0:T(8,128)} %copy-done.1, f32[3,8,8,128]{3,2,1,0:T(8,128)} %copy-done.2, f32[11,8,128]{2,1,0:T(8,128)} %copy-done.3, ...), custom_call_target="tpu_custom_call" | custom-call | tf_op jit(solution)/shard_map/pallas_call | solution.py:417
Async XLA Ops:
  0.6 4.3 %collective-permute-start = (f32[3,8,8,128]{3,2,1,0:T(8,128)}, f32[3,8,8,128]{3,2,1,0:T(8,128)S(1)}, u32[]{:S(2)}, u32[]{:S(2)}) collective-permute-start(f32[3,8,8,128]{3,2,1,0:T(8,128)} %own.5), channel_id=1, source_target_pairs={{0,8},{8,16},{16,24},{24,0},{1,9},{9,17},{17,25},{25,1},{2,10},{10... | collective-permute-start | bytes 294920 | tf_op jit(solution)/shard_map/ppermute | solution.py:369
  0.7 5.2 %collective-permute-start.1 = (f32[3,8,8,128]{3,2,1,0:T(8,128)}, f32[3,8,8,128]{3,2,1,0:T(8,128)S(1)}, u32[]{:S(2)}, u32[]{:S(2)}) collective-permute-start(f32[3,8,8,128]{3,2,1,0:T(8,128)} %own.5), channel_id=1, source_target_pairs={{0,24},{8,0},{16,8},{24,16},{1,25},{9,1},{17,9},{25,17},{2,26},{10... | collective-permute-start | bytes 294920 | tf_op jit(solution)/shard_map/ppermute | solution.py:369
  2.4 5.9 %collective-permute-start.2 = (f32[3,8,8,128]{3,2,1,0:T(8,128)}, f32[3,8,8,128]{3,2,1,0:T(8,128)S(1)}, u32[]{:S(2)}, u32[]{:S(2)}) collective-permute-start(f32[3,8,8,128]{3,2,1,0:T(8,128)} %own.5), channel_id=1, source_target_pairs={{0,16},{8,24},{16,0},{24,8},{1,17},{9,25},{17,1},{25,9},{2,18},{10... | collective-permute-start | bytes 294920 | tf_op jit(solution)/shard_map/ppermute | solution.py:369
  4.9 3.4 %copy-start = (f32[3,8,8,128]{3,2,1,0:T(8,128)}, f32[3,8,8,128]{3,2,1,0:T(8,128)S(1)}, u32[]{:S(2)}) copy-start(f32[3,8,8,128]{3,2,1,0:T(8,128)S(1)} %collective-permute-done.low) | copy-start | bytes 294916
  5.9 2.4 %copy-start.1 = (f32[3,8,8,128]{3,2,1,0:T(8,128)}, f32[3,8,8,128]{3,2,1,0:T(8,128)S(1)}, u32[]{:S(2)}) copy-start(f32[3,8,8,128]{3,2,1,0:T(8,128)S(1)} %collective-permute-done.1.high) | copy-start | bytes 294916
  8.3 0.6 %copy-start.2 = (f32[3,8,8,128]{3,2,1,0:T(8,128)}, f32[3,8,8,128]{3,2,1,0:T(8,128)S(1)}, u32[]{:S(2)}) copy-start(f32[3,8,8,128]{3,2,1,0:T(8,128)S(1)} %collective-permute-done.2.high2) | copy-start | bytes 294916
  10.8 6.4 %collective-permute-start.3 = (f32[11,8,128]{2,1,0:T(8,128)}, f32[11,8,128]{2,1,0:T(8,128)S(1)}, u32[]{:S(2)}, u32[]{:S(2)}) collective-permute-start(f32[11,8,128]{2,1,0:T(8,128)} %shard_map.41), channel_id=1, source_target_pairs={{0,1},{1,0},{2,3},{3,2},{4,5},{5,4},{6,7},{7,6},{8,9},{9,8},{10,11... | collective-permute-start | bytes 135176 | tf_op jit(solution)/shard_map/ppermute | solution.py:382
  11.3 5.9 %collective-permute-start.4 = (f32[11,8,128]{2,1,0:T(8,128)}, f32[11,8,128]{2,1,0:T(8,128)S(1)}, u32[]{:S(2)}, u32[]{:S(2)}) collective-permute-start(f32[11,8,128]{2,1,0:T(8,128)} %shard_map.41), channel_id=1, source_target_pairs={{0,8},{1,2},{2,1},{3,4},{4,3},{5,6},{6,5},{7,15},{8,0},{9,10},{10,... | collective-permute-start | bytes 135176 | tf_op jit(solution)/shard_map/ppermute | solution.py:382
  17.3 0.6 %copy-start.3 = (f32[11,8,128]{2,1,0:T(8,128)}, f32[11,8,128]{2,1,0:T(8,128)S(1)}, u32[]{:S(2)}) copy-start(f32[11,8,128]{2,1,0:T(8,128)S(1)} %collective-permute-done.3.even) | copy-start | bytes 135172
  17.9 0.6 %copy-start.4 = (f32[11,8,128]{2,1,0:T(8,128)}, f32[11,8,128]{2,1,0:T(8,128)S(1)}, u32[]{:S(2)}) copy-start(f32[11,8,128]{2,1,0:T(8,128)S(1)} %collective-permute-done.4.odd) | copy-start | bytes 135172

commit v2 on v1

--- a/solution.py
+++ b/solution.py
@@ -48,16 +48,13 @@
 
 def raw_row(tiles, comp, row):
     own, low, high, high2 = tiles
-    ref, at = (
-        (low, row + BXY)
-        if row < 0
-        else (own, row)
-        if row < BXY
-        else (high, row - BXY)
-        if row < 2 * BXY
-        else (high2, row - 2 * BXY)
-    )
-    return ref[comp, :, at, :]
+    if row < 0:
+        return low[row + low.shape[0], comp]
+    if row < BXY:
+        return own[row, comp]
+    if row < 2 * BXY:
+        return high[comp, :, row - BXY, :]
+    return high2[row - 2 * BXY, comp]
 
 
 def exists(row, present):
@@ -256,10 +253,21 @@
     return [(comp, row) for row in range(FIRST, LAST + 1) for comp in range(3)]
 
 
+def prepare_kernel(tile, own, first, last):
+    for row in range(BXY):
+        for comp in range(3):
+            value = tile[comp, :, row, :]
+            own[row, comp] = value
+            if row < first.shape[0]:
+                first[row, comp] = value
+            if row >= BXY - last.shape[0]:
+                last[row - BXY + last.shape[0], comp] = value
+
+
 def pack_kernel(own, low, high, high2, out):
-    lanes = own.shape[3]
+    depth, lanes = own.shape[2:]
     per = lanes // SLOT
-    lane = lanes_of((own.shape[1], lanes))
+    lane = lanes_of((depth, lanes))
     rows = packed_rows()
     for first in range(0, len(rows), per):
         packed = None
@@ -291,7 +299,7 @@
 def edge_kernel(layer_map, own, low, high, high2, even, odd, inner, perm_out, trans_out, scratch):
     i, j, present, (has_left, has_right) = flags("gx", "gy")
     tiles = (own, low, high, high2)
-    depth, lanes = own.shape[1], own.shape[3]
+    depth, lanes = own.shape[2:]
     per = lanes // SLOT
     lane = lanes_of((depth, lanes))
     half = lanes // 2
@@ -345,7 +353,7 @@
         c == 0, first, jnp.where(c == count - 1, final, jnp.where(c == count, beyond, 0.0))
     )
     total = inner[...] + reduce_sums(sums, layer_map, columns)
-    cells = (own.shape[2] + 2 * BXY, lanes + 2 * BXY, depth)
+    cells = (own.shape[0] + 2 * BXY, lanes + 2 * BXY, depth)
     energy = [total[2 * NCL * q : 2 * NCL * q + NCL] for q in range(4)]
     square = [total[2 * NCL * q + NCL : 2 * NCL * (q + 1)] for q in range(4)]
     perms = [
@@ -386,28 +394,36 @@
     _, depth, width, lanes = permeability.shape
     if width != BXY or depth != 8 or lanes != 128:
         raise ValueError("unsupported tile")
-    tiles = (
-        permeability,
-        ring(permeability, "gx", 1),
-        ring(permeability, "gx", -1),
-        ring(permeability, "gx", -2),
-    )
     vmem = pl.BlockSpec(memory_space=pltpu.VMEM)
     smem = pl.BlockSpec(memory_space=pltpu.SMEM)
     count = len(packed_rows())
     per = lanes // SLOT
+    limit = pltpu.CompilerParams(vmem_limit_bytes=16 << 20)
+    high = ring(permeability, "gx", -1)
+    rows = [pltpu.VMEM((n, 3, depth, lanes), jnp.float32) for n in (width, HIGH, LOW)]
+    own, first, last = pl.pallas_call(
+        prepare_kernel,
+        out_shape=rows,
+        in_specs=[vmem],
+        out_specs=[vmem] * 3,
+        compiler_params=limit,
+    )(permeability)
+    tiles = (own, ring(last, "gx", 1), high, ring(first, "gx", -2))
+    tiles = tuple(pltpu.with_memory_space_constraint(t, pltpu.VMEM) for t in tiles)
     packed = pl.pallas_call(
         pack_kernel,
-        out_shape=jax.ShapeDtypeStruct((-(-count // per), depth, lanes), jnp.float32),
+        out_shape=pltpu.VMEM((-(-count // per), depth, lanes), jnp.float32),
         in_specs=[vmem] * 4,
         out_specs=vmem,
+        compiler_params=limit,
     )(*tiles)
-    even = swap(packed, ("gx", "gy"), 0)
-    odd = swap(packed, ("gx", "gy"), 1)
+    even = pltpu.with_memory_space_constraint(swap(packed, ("gx", "gy"), 0), pltpu.VMEM)
+    odd = pltpu.with_memory_space_constraint(swap(packed, ("gx", "gy"), 1), pltpu.VMEM)
     scratch = [pltpu.VMEM((256, depth, lanes), jnp.float32)]
     inner = pl.pallas_call(
         main_kernel,
-        out_shape=jax.ShapeDtypeStruct((8 * NCL, lanes), jnp.float32),
+        out_shape=pltpu.VMEM((8 * NCL, lanes), jnp.float32),
+        compiler_params=limit,
         in_specs=[smem] + [vmem] * 4,
         out_specs=vmem,
         scratch_shapes=scratch,
@@ -419,8 +435,9 @@
         out_shape=(out, out),
         in_specs=[smem] + [vmem] * 7,
         out_specs=(vmem, vmem),
+        compiler_params=limit,
         scratch_shapes=scratch,
-    )(layer_map, *tiles, even, odd, inner)
+    )(layer_map, *tiles, even, odd, pltpu.with_memory_space_constraint(inner, pltpu.VMEM))
 
 
 def solution(mesh):

time: 21.8 us -> 16.8 us (0.77)
  the two profiles are of different devices: /device:TPU:10 before, /device:TPU:16 now
where the time goes in v2:
time: 16.8 us; the launch traced here: 16.7 us
  waiting for transfers between devices  6.73 us (40%)
  Pallas kernels  4.55 us (27%)
  starting transfers between devices  3.81 us (23%)
  local copies, waits for them, and re-layouts  0.93 us (6%)
  between operations  0.64 us (4%)
    ppermute x3, waiting for transfers between devices, ring(): lax.ppermute(value, axis, [(s, (s + steps) % count) for s in range(count)])  3.98 us
    ppermute x2, waiting for transfers between devices, swap(): return lax.ppermute(value, axes, pairs)  2.74 us
    pallas_call x1, Pallas kernels, local(): pl.pallas_call(edge_kernel, out_shape=(out, out), in_specs=[smem] + [vmem...  2.57 us
    ppermute x2, starting transfers between devices, swap(): return lax.ppermute(value, axes, pairs)  1.98 us
    ppermute x3, starting transfers between devices, ring(): lax.ppermute(value, axis, [(s, (s + steps) % count) for s in range(count)])  1.83 us
    pallas_call x1, Pallas kernels, local(): pl.pallas_call(main_kernel, out_shape=pltpu.VMEM((8 * NCL, lanes), jnp.fl...  1.78 us
    unnamed x4, local copies, waits for them, and re-layouts  0.93 us
  transfers between devices with their start and end apart: 5, of which 4 were waited for; matrix products, arithmetic and copies ran while one was open for 0% of the time, Pallas kernels for 11%

profile of v2, /device:TPU:16, one launch (start us, length us, event | category | flops | bytes accessed | tf_op | source)
XLA Modules:
  0.0 16.7 jit_solution(3574079571704916881)
XLA Ops:
  0.6 1.0 %collective-permute-start.1 = (f32[3,8,8,128]{3,2,1,0:T(8,128)}, f32[3,8,8,128]{3,2,1,0:T(8,128)S(1)}, u32[]{:S(2)}, u32[]{:S(2)}) collective-permute-start(f32[3,8,8,128]{3,2,1,0:T(8,128)} %tile.1), channel_id=1, source_target_pairs={{0,24},{8,0},{16,8},{24,16},{1,25},{9,1},{17,9},{25,17},{2,26},{10... | collective-permute-start | bytes 294920 | tf_op jit(solution)/shard_map/ppermute | solution.py:377
  1.6 0.0 copy-start
  1.6 0.9 %copy-done = f32[3,8,8,128]{3,2,1,0:T(8,128)S(1)} copy-done((f32[3,8,8,128]{3,2,1,0:T(8,128)S(1)}, f32[3,8,8,128]{3,2,1,0:T(8,128)}, u32[]{:S(2)}) %copy-start) | copy-done | bytes 98328
  2.6 0.1 shard_map.41
  2.6 0.6 %collective-permute-start.2 = (f32[5,3,8,128]{3,2,1,0:T(8,128)S(1)}, f32[5,3,8,128]{3,2,1,0:T(8,128)S(1)}, u32[]{:S(2)}, u32[]{:S(2)}) collective-permute-start(f32[5,3,8,128]{3,2,1,0:T(8,128)S(1)} %get-tuple-element.7), channel_id=1, source_target_pairs={{0,16},{8,24},{16,0},{24,8},{1,17},{9,25},{17,1},{25,9},{2,18},{10... | collective-permute-start | bytes 184328 | tf_op jit(solution)/shard_map/ppermute | solution.py:377
  3.3 0.2 %collective-permute-start = (f32[4,3,8,128]{3,2,1,0:T(8,128)S(1)}, f32[4,3,8,128]{3,2,1,0:T(8,128)S(1)}, u32[]{:S(2)}, u32[]{:S(2)}) collective-permute-start(f32[4,3,8,128]{3,2,1,0:T(8,128)S(1)} %get-tuple-element.6), channel_id=1, source_target_pairs={{0,8},{8,16},{16,24},{24,0},{1,9},{9,17},{17,25},{25,1},{2,10},{10... | collective-permute-start | bytes 147464 | tf_op jit(solution)/shard_map/ppermute | solution.py:377
  3.5 3.8 %collective-permute-done.low = f32[4,3,8,128]{3,2,1,0:T(8,128)S(1)} collective-permute-done((f32[4,3,8,128]{3,2,1,0:T(8,128)S(1)}, f32[4,3,8,128]{3,2,1,0:T(8,128)S(1)}, u32[]{:S(2)}, u32[]{:S(2)}) %collective-permute-start) | collective-permute-done | bytes 49184 | tf_op jit(solution)/shard_map/ppermute | solution.py:377
  7.3 0.1 collective-permute-done.2.high2
  7.4 0.0 collective-permute-done.1.high
  7.4 0.0 copy-start.1
  7.4 0.1 shard_map.42
  7.6 1.6 %collective-permute-start.3 = (f32[11,8,128]{2,1,0:T(8,128)S(1)}, f32[11,8,128]{2,1,0:T(8,128)S(1)}, u32[]{:S(2)}, u32[]{:S(2)}) collective-permute-start(f32[11,8,128]{2,1,0:T(8,128)S(1)} %shard_map.42), channel_id=1, source_target_pairs={{0,1},{1,0},{2,3},{3,2},{4,5},{5,4},{6,7},{7,6},{8,9},{9,8},{10,11... | collective-permute-start | bytes 135176 | tf_op jit(solution)/shard_map/ppermute | solution.py:390
  9.1 0.4 %collective-permute-start.4 = (f32[11,8,128]{2,1,0:T(8,128)S(1)}, f32[11,8,128]{2,1,0:T(8,128)S(1)}, u32[]{:S(2)}, u32[]{:S(2)}) collective-permute-start(f32[11,8,128]{2,1,0:T(8,128)S(1)} %shard_map.42), channel_id=1, source_target_pairs={{0,8},{1,2},{2,1},{3,4},{4,3},{5,6},{6,5},{7,15},{8,0},{9,10},{10,... | collective-permute-start | bytes 135176 | tf_op jit(solution)/shard_map/ppermute | solution.py:390
  9.6 0.0 copy-done.1
  9.6 1.8 %shard_map.43.inner = f32[32,128]{1,0:T(8,128)S(1)} custom-call(s32[8]{0:T(128)S(1)} %copy-done.1, f32[8,3,8,128]{3,2,1,0:T(8,128)S(1)} %get-tuple-element.5.own, f32[4,3,8,128]{3,2,1,0:T(8,128)S(1)} %collective-permute-done.low, f32[3,8,8,128]{3,2,1,0:T(8,128)S(1)} %collective-permute-done.1.high, f32[5,3,8,128]{3,2,1,0:T(8,128)S(1)} %collective-permute-done.2.high2), custom_call_target="tpu_custom_call" | custom-call | flops 6000000 | bytes 393216 | tf_op jit(solution)/shard_map/pallas_call | solution.py:423
  11.3 0.6 %collective-permute-done.3.even = f32[11,8,128]{2,1,0:T(8,128)S(1)} collective-permute-done((f32[11,8,128]{2,1,0:T(8,128)S(1)}, f32[11,8,128]{2,1,0:T(8,128)S(1)}, u32[]{:S(2)}, u32[]{:S(2)}) %collective-permute-start.3) | collective-permute-done | bytes 45088 | tf_op jit(solution)/shard_map/ppermute | solution.py:390
  11.9 2.2 %collective-permute-done.4.odd = f32[11,8,128]{2,1,0:T(8,128)S(1)} collective-permute-done((f32[11,8,128]{2,1,0:T(8,128)S(1)}, f32[11,8,128]{2,1,0:T(8,128)S(1)}, u32[]{:S(2)}, u32[]{:S(2)}) %collective-permute-start.4) | collective-permute-done | bytes 45088 | tf_op jit(solution)/shard_map/ppermute | solution.py:390
  14.1 2.6 %shard_map.44 = (f32[3,4,1,16]{3,2,1,0:T(1,128)}, f32[3,4,1,16]{3,2,1,0:T(1,128)}) custom-call(s32[8]{0:T(128)S(1)} %copy-done.1, f32[8,3,8,128]{3,2,1,0:T(8,128)S(1)} %get-tuple-element.5.own, f32[4,3,8,128]{3,2,1,0:T(8,128)S(1)} %collective-permute-done.low, f32[3,8,8,128]{3,2,1,0:T(8,128)S(1)} %collective-permute-done.1.high, ...), custom_call_target="tpu_custom_call" | custom-call | tf_op jit(solution)/shard_map/pallas_call | solution.py:433
Async XLA Ops:
  0.6 6.8 %collective-permute-start.1 = (f32[3,8,8,128]{3,2,1,0:T(8,128)}, f32[3,8,8,128]{3,2,1,0:T(8,128)S(1)}, u32[]{:S(2)}, u32[]{:S(2)}) collective-permute-start(f32[3,8,8,128]{3,2,1,0:T(8,128)} %tile.1), channel_id=1, source_target_pairs={{0,24},{8,0},{16,8},{24,16},{1,25},{9,1},{17,9},{25,17},{2,26},{10... | collective-permute-start | bytes 294920 | tf_op jit(solution)/shard_map/ppermute | solution.py:377
  1.6 0.9 %copy-start = (f32[3,8,8,128]{3,2,1,0:T(8,128)S(1)}, f32[3,8,8,128]{3,2,1,0:T(8,128)}, u32[]{:S(2)}) copy-start(f32[3,8,8,128]{3,2,1,0:T(8,128)} %tile.1) | copy-start | bytes 294916
  2.6 4.8 %collective-permute-start.2 = (f32[5,3,8,128]{3,2,1,0:T(8,128)S(1)}, f32[5,3,8,128]{3,2,1,0:T(8,128)S(1)}, u32[]{:S(2)}, u32[]{:S(2)}) collective-permute-start(f32[5,3,8,128]{3,2,1,0:T(8,128)S(1)} %get-tuple-element.7), channel_id=1, source_target_pairs={{0,16},{8,24},{16,0},{24,8},{1,17},{9,25},{17,1},{25,9},{2,18},{10... | collective-permute-start | bytes 184328 | tf_op jit(solution)/shard_map/ppermute | solution.py:377
  3.3 4.0 %collective-permute-start = (f32[4,3,8,128]{3,2,1,0:T(8,128)S(1)}, f32[4,3,8,128]{3,2,1,0:T(8,128)S(1)}, u32[]{:S(2)}, u32[]{:S(2)}) collective-permute-start(f32[4,3,8,128]{3,2,1,0:T(8,128)S(1)} %get-tuple-element.6), channel_id=1, source_target_pairs={{0,8},{8,16},{16,24},{24,0},{1,9},{9,17},{17,25},{25,1},{2,10},{10... | collective-permute-start | bytes 147464 | tf_op jit(solution)/shard_map/ppermute | solution.py:377
  7.4 2.1 %copy-start.1 = (s32[8]{0:T(128)S(1)}, s32[8]{0:T(128)}, u32[]{:S(2)}) copy-start(s32[8]{0:T(128)} %layer_map.3) | copy-start | bytes 100
  7.6 4.3 %collective-permute-start.3 = (f32[11,8,128]{2,1,0:T(8,128)S(1)}, f32[11,8,128]{2,1,0:T(8,128)S(1)}, u32[]{:S(2)}, u32[]{:S(2)}) collective-permute-start(f32[11,8,128]{2,1,0:T(8,128)S(1)} %shard_map.42), channel_id=1, source_target_pairs={{0,1},{1,0},{2,3},{3,2},{4,5},{5,4},{6,7},{7,6},{8,9},{9,8},{10,11... | collective-permute-start | bytes 135176 | tf_op jit(solution)/shard_map/ppermute | solution.py:390
  9.1 4.9 %collective-permute-start.4 = (f32[11,8,128]{2,1,0:T(8,128)S(1)}, f32[11,8,128]{2,1,0:T(8,128)S(1)}, u32[]{:S(2)}, u32[]{:S(2)}) collective-permute-start(f32[11,8,128]{2,1,0:T(8,128)S(1)} %shard_map.42), channel_id=1, source_target_pairs={{0,8},{1,2},{2,1},{3,4},{4,3},{5,6},{6,5},{7,15},{8,0},{9,10},{10,... | collective-permute-start | bytes 135176 | tf_op jit(solution)/shard_map/ppermute | solution.py:390

commit v3 on v1

--- a/solution.py
+++ b/solution.py
@@ -18,7 +18,6 @@
 HIGH = SWEEPS + 1
 RIGHT = BXY + HIGH
 SLOT = LOW + RIGHT
-FIRST, LAST = -LOW, 2 * BXY + HIGH - 1
 
 
 def sweep_weights(count):
@@ -46,23 +45,13 @@
     return pltpu.roll(value, 1, axis)
 
 
-def raw_row(tiles, comp, row):
-    own, low, high, high2 = tiles
-    ref, at = (
-        (low, row + BXY)
-        if row < 0
-        else (own, row)
-        if row < BXY
-        else (high, row - BXY)
-        if row < 2 * BXY
-        else (high2, row - 2 * BXY)
-    )
-    return ref[comp, :, at, :]
-
-
-def exists(row, present):
-    low, high, high2 = present
-    return low if row < 0 else None if row < BXY else high if row < 2 * BXY else high2
+def layers_of(tile, comp, row):
+    _, depth, width, lanes = tile.shape
+    flat = tile.reshape(3 * depth * width, lanes)
+    return flat[pl.ds(comp * depth * width + row, depth, stride=width), :]
+
+
+LONG = 10**10
 
 
 class Solver:
@@ -147,7 +136,7 @@
 
     def pressure(self, d, count, row, boundary):
         if boundary is not None:
-            kind, at = boundary
+            _, at = boundary
             if abs(row - at) >= count:
                 boundary = None
 
@@ -227,105 +216,131 @@
     return [value for i in range(len(jobs)) for value in results[i]]
 
 
-def reduce_sums(sums, layer_map, columns):
-    depth = sums[0].shape[0]
-    stacked = jnp.concatenate(sums, axis=0)
-    by_column = jnp.dot(
-        stacked, columns, precision=lax.Precision.HIGHEST, preferred_element_type=jnp.float32
+def sum_columns(sums, columns):
+    return jnp.dot(
+        jnp.concatenate(sums, axis=0),
+        columns,
+        precision=lax.Precision.HIGHEST,
+        preferred_element_type=jnp.float32,
     )
-    rows, cols = len(sums) * NCL, len(sums) * depth
-    r = lax.broadcasted_iota(jnp.int32, (rows, cols), 0)
-    c = lax.broadcasted_iota(jnp.int32, (rows, cols), 1)
-    layer = jnp.zeros((rows, cols), jnp.int32)
+
+
+def picks_kernel(layer_map, out):
+    depth = out.shape[1] // (out.shape[0] // NCL)
+    r = lax.broadcasted_iota(jnp.int32, out.shape, 0)
+    c = lax.broadcasted_iota(jnp.int32, out.shape, 1)
+    layer = jnp.zeros(out.shape, jnp.int32)
     for z in range(depth):
         layer = jnp.where(c % depth == z, layer_map[z], layer)
-    picks = ((r // NCL == c // depth) & (r % NCL == layer)).astype(jnp.float32)
-    return jnp.dot(
-        picks, by_column, precision=lax.Precision.HIGHEST, preferred_element_type=jnp.float32
-    )
-
-
-def flags(x_axis, y_axis):
-    i, j = lax.axis_index(x_axis), lax.axis_index(y_axis)
-    nx, ny = lax.axis_size(x_axis), lax.axis_size(y_axis)
+    out[...] = ((r // NCL == c // depth) & (r % NCL == layer)).astype(jnp.float32)
+
+
+def place(axes):
+    i, j = (lax.axis_index(a) for a in axes)
+    nx, ny = (lax.axis_size(a) for a in axes)
+    core, chip = i % 2, i // 2
     one = lambda test: jnp.where(test, 1.0, 0.0).astype(jnp.float32)
-    return i, j, (one(i > 0), one(i < nx - 1), one(i < nx - 2)), (one(j > 0), one(j < ny - 1))
-
-
-def packed_rows():
-    return [(comp, row) for row in range(FIRST, LAST + 1) for comp in range(3)]
-
-
-def pack_kernel(own, low, high, high2, out):
-    lanes = own.shape[3]
+    tiles = one(i > 0), one(i < nx - 1), one(i < nx - 2)
+    chips = one(chip > 0), one(chip < nx // 2 - 1)
+    return core, tiles, chips, (one(j > 0), one(j < ny - 1))
+
+
+def slots(width):
+    return [(comp, row) for row in range(width) for comp in range(3)]
+
+
+def table_kernel(out):
+    lanes = out.shape[0]
+    r = lax.broadcasted_iota(jnp.int32, out.shape, 0)
+    c = lax.broadcasted_iota(jnp.int32, out.shape, 1)
+    inner = (r // BXY == c) & (c > 0) & (c < lanes // BXY - 1)
+    out[...] = inner.astype(jnp.float32)
+
+
+def pack_kernel(mine, other, pair, packed):
+    core, _, _, _ = place(("gx", "gy"))
+    _, depth, width, lanes = mine.shape
     per = lanes // SLOT
-    lane = lanes_of((own.shape[1], lanes))
-    rows = packed_rows()
-    for first in range(0, len(rows), per):
-        packed = None
-        for slot, (comp, row) in enumerate(rows[first : first + per]):
-            value = raw_row((own, low, high, high2), comp, row)
+    lane = lanes_of((depth, lanes))
+    rows = slots(width)
+    count = packed.shape[0] // 2
+    for tile, at in ((mine, core), (other, 1 - core)):
+        strip = None
+        for n, (comp, row) in enumerate(rows):
+            value = layers_of(tile, comp, row)
+            pair[at * width + row, comp] = value
+            slot = n % per
             value = pltpu.roll(value, (LOW + SLOT * slot) % lanes, 1)
-            packed = value if packed is None else jnp.where(lane < SLOT * slot, packed, value)
-        out[first // per] = packed
-
-
-def main_kernel(layer_map, own, low, high, high2, out, scratch):
-    _, _, present, _ = flags("gx", "gy")
-    tiles = (own, low, high, high2)
-
-    def perm(comp, row):
-        value = raw_row(tiles, comp, row)
-        there = exists(row, present)
-        return (value if there is None else value * there) + KMIN
-
-    solver = Solver(perm, scratch, None, None)
-    sums = accumulate(solver, present)
-    lanes = own.shape[3]
-    r = lax.broadcasted_iota(jnp.int32, (lanes, lanes), 0)
-    c = lax.broadcasted_iota(jnp.int32, (lanes, lanes), 1)
-    inner = (r // BXY == c) & (c > 0) & (c < lanes // BXY - 1)
-    out[...] = reduce_sums(sums, layer_map, inner.astype(jnp.float32))
-
-
-def edge_kernel(layer_map, own, low, high, high2, even, odd, inner, perm_out, trans_out, scratch):
-    i, j, present, (has_left, has_right) = flags("gx", "gy")
-    tiles = (own, low, high, high2)
-    depth, lanes = own.shape[1], own.shape[3]
+            strip = value if slot == 0 else jnp.where(lane < SLOT * slot, strip, value)
+            if slot == per - 1 or n == len(rows) - 1:
+                packed[at * count + n // per] = strip
+
+
+def join_kernel(below, beside, above, out):
+    half = beside.shape[0] // 2
+    out[:half] = below[half:]
+    out[half : 3 * half] = beside[...]
+    out[3 * half :] = above[...]
+
+
+def main_kernel(columns, pair, up_mine, up_other, down_mine, down_other, out, stack, scratch):
+    core, present, (has_down, has_up), _ = place(("gx", "gy"))
+    width = up_mine.shape[2]
+    for row in range(2 * width):
+        for comp in range(3):
+            stack[LOW + row, comp] = pair[row, comp] + KMIN
+    first = core == 0
+    for row in range(width):
+        for comp in range(3):
+            mine, other = layers_of(up_mine, comp, row), layers_of(up_other, comp, row)
+            above = LOW + 2 * width + row
+            stack[above, comp] = jnp.where(first, mine, other) * has_up + KMIN
+            if row < HIGH:
+                stack[above + width, comp] = jnp.where(first, other, mine) * has_up + KMIN
+            if row >= width - LOW:
+                if down_mine is not up_mine:
+                    mine, other = layers_of(down_mine, comp, row), layers_of(down_other, comp, row)
+                low = jnp.where(first, other, mine) * has_down + KMIN
+                stack[row - width + LOW, comp] = low
+    base = LOW + core * width
+    solver = Solver(lambda comp, row: stack[base + row, comp], scratch, None, None)
+    out[...] = sum_columns(accumulate(solver, present), columns[...])
+
+
+def edge_kernel(picks, stack, mine, other, inner, perm_out, trans_out, strips, scratch):
+    core, present, (has_down, has_up), (has_left, has_right) = place(("gx", "gy"))
+    depth, lanes = stack.shape[2:]
+    width = BXY
     per = lanes // SLOT
     lane = lanes_of((depth, lanes))
     half = lanes // 2
-    last = lanes - BXY - LOW
     left = RIGHT + 7
     start = left + LOW
     stop = start + BXY + HIGH
     in_left = lane % SLOT < LOW
-    is_odd = j % 2 == 1
-    from_even = in_left == (jnp.zeros_like(lane) + is_odd.astype(jnp.int32) == 1)
+    from_mine = in_left == (jnp.zeros_like(lane) + core == 1)
     keep = jnp.where(in_left, has_left, has_right)
-    packs = {}
-
-    def pack(at):
-        if at not in packs:
-            packs[at] = jnp.where(from_even, even[at], odd[at]) * keep
-        return packs[at]
-
-    index = {key: at for at, key in enumerate(packed_rows())}
+    per_tile = strips.shape[0] // 5
+    for at in range(strips.shape[0]):
+        there = has_down if at < per_tile else None if at < 3 * per_tile else has_up
+        weight = keep if there is None else keep * there
+        strips[at] = jnp.where(from_mine, mine[at], other[at]) * weight + KMIN
+
+    index = {key: at for at, key in enumerate(slots(width))}
     second = (lane >= half - BXY - LOW) & (lane < half + stop)
+    base = LOW + core * width
 
     def perm(comp, row):
-        at = index[comp, row]
+        at = index[comp, row % width]
         slot = at % per
-        mine = raw_row(tiles, comp, row)
-        theirs = pack(at // per)
+        own = stack[base + row, comp]
+        theirs = strips[(core + 1 + row // width) * per_tile + at // per]
         right = pltpu.roll(theirs, (-(SLOT * slot + LOW)) % lanes, 1)
         before = pltpu.roll(theirs, (left - SLOT * slot) % lanes, 1)
-        value = jnp.where(lane < RIGHT, right, mine)
-        value = jnp.where((lane >= left) & (lane < stop), pltpu.roll(mine, start, 1), value)
+        value = jnp.where(lane < RIGHT, right, own)
+        value = jnp.where((lane >= left) & (lane < stop), pltpu.roll(own, start, 1), value)
         value = jnp.where((lane >= left) & (lane < start), before, value)
-        value = jnp.where(second, pltpu.roll(value, half, 1), value)
-        there = exists(row, present)
-        return (value if there is None else value * there) + KMIN
+        return jnp.where(second, pltpu.roll(value, half, 1), value)
 
     y_ends = (lane == BXY - 1) | (lane == half + start + BXY - 1)
     y_starts = lane == half - BXY
@@ -344,8 +359,13 @@
     columns = jnp.where(
         c == 0, first, jnp.where(c == count - 1, final, jnp.where(c == count, beyond, 0.0))
     )
-    total = inner[...] + reduce_sums(sums, layer_map, columns)
-    cells = (own.shape[2] + 2 * BXY, lanes + 2 * BXY, depth)
+    total = jnp.dot(
+        picks[...],
+        inner[...] + sum_columns(sums, columns),
+        precision=lax.Precision.HIGHEST,
+        preferred_element_type=jnp.float32,
+    )
+    cells = (width + 2 * BXY, lanes + 2 * BXY, depth)
     energy = [total[2 * NCL * q : 2 * NCL * q + NCL] for q in range(4)]
     square = [total[2 * NCL * q + NCL : 2 * NCL * (q + 1)] for q in range(4)]
     perms = [
@@ -364,63 +384,109 @@
             trans_out[d, l, :, :] = trans[d][l : l + 1, :count]
 
 
-def ring(value, axis, steps):
-    count = lax.axis_size(axis)
-    return lax.ppermute(value, axis, [(s, (s + steps) % count) for s in range(count)])
-
-
-def swap(value, axes, parity):
-    nx, ny = (lax.axis_size(a) for a in axes)
-    pairs = []
-    for i in range(nx):
-        for j in range(ny):
-            other = j ^ 1 if parity == 0 else ((j - 1) ^ 1) + 1
-            if 0 <= other < ny:
-                pairs.append((i * ny + j, i * ny + other))
-            else:
-                pairs.append((i * ny + j, (i ^ 1 if nx % 2 == 0 else i) * ny + j))
-    return lax.ppermute(value, axes, pairs)
+class Exchange:
+    def __init__(self, axes):
+        self.axes = axes
+        self.nx, self.ny = (lax.axis_size(a) for a in axes)
+        self.sent = {}
+
+    def permute(self, value, target):
+        nx, ny = self.nx, self.ny
+        pairs = []
+        for i in range(nx):
+            for j in range(ny):
+                a, b = target(i, j)
+                pairs.append((i * ny + j, a % nx * ny + b))
+        key = (id(value), tuple(pairs))
+        if key not in self.sent:
+            self.sent[key] = (value, lax.ppermute(value, self.axes, pairs))
+        return self.sent[key][1]
+
+    def swap(self, value):
+        return self.permute(value, lambda i, j: (i ^ 1, j))
+
+    def straight(self, value, pairs):
+        return self.permute(value, lambda i, j: (i - 2 * pairs, j))
+
+    def sideways(self, value, pairs):
+        def target(i, j):
+            to = j - 1 if i % 2 == 0 else j + 1
+            i -= 2 * pairs
+            return (i, to) if 0 <= to < self.ny else (i ^ 1, j)
+
+        return self.permute(value, target)
 
 
 def local(permeability, layer_map):
     _, depth, width, lanes = permeability.shape
-    if width != BXY or depth != 8 or lanes != 128:
+    net = Exchange(("gx", "gy"))
+    if width != BXY or depth != 8 or lanes != 128 or net.nx % 2:
         raise ValueError("unsupported tile")
-    tiles = (
-        permeability,
-        ring(permeability, "gx", 1),
-        ring(permeability, "gx", -1),
-        ring(permeability, "gx", -2),
-    )
     vmem = pl.BlockSpec(memory_space=pltpu.VMEM)
     smem = pl.BlockSpec(memory_space=pltpu.SMEM)
-    count = len(packed_rows())
-    per = lanes // SLOT
-    packed = pl.pallas_call(
+    limit = pltpu.CompilerParams(vmem_limit_bytes=16 << 20)
+    held = lambda value: pltpu.with_memory_space_constraint(value, pltpu.VMEM)
+    strips = -(-len(slots(width)) // (lanes // SLOT))
+
+    columns = pl.pallas_call(
+        table_kernel,
+        out_shape=pltpu.VMEM((lanes, lanes), jnp.float32),
+        out_specs=vmem,
+        compiler_params=limit,
+        cost_estimate=pl.CostEstimate(flops=LONG, bytes_accessed=lanes * lanes * 4, transcendentals=0),
+    )()
+    other = net.swap(permeability)
+    up, down = net.straight(permeability, 1), net.straight(permeability, -1)
+    pair, packed = pl.pallas_call(
         pack_kernel,
-        out_shape=jax.ShapeDtypeStruct((-(-count // per), depth, lanes), jnp.float32),
-        in_specs=[vmem] * 4,
+        out_shape=[
+            pltpu.VMEM((2 * width, 3, depth, lanes), jnp.float32),
+            pltpu.VMEM((2 * strips, depth, lanes), jnp.float32),
+        ],
+        in_specs=[vmem] * 2,
+        out_specs=[vmem] * 2,
+        compiler_params=limit,
+    )(held(permeability), held(other))
+    above, below = net.sideways(packed, 1), net.sideways(packed, -1)
+    beside = net.sideways(packed, 0)
+    up_other, down_other = net.swap(up), net.swap(down)
+    picks = pl.pallas_call(
+        picks_kernel,
+        out_shape=pltpu.VMEM((8 * NCL, 8 * depth), jnp.float32),
+        in_specs=[smem],
         out_specs=vmem,
-    )(*tiles)
-    even = swap(packed, ("gx", "gy"), 0)
-    odd = swap(packed, ("gx", "gy"), 1)
-    scratch = [pltpu.VMEM((256, depth, lanes), jnp.float32)]
-    inner = pl.pallas_call(
+        compiler_params=limit,
+    )(layer_map)
+    scratch = pltpu.VMEM((256, depth, lanes), jnp.float32)
+    inner, stack = pl.pallas_call(
         main_kernel,
-        out_shape=jax.ShapeDtypeStruct((8 * NCL, lanes), jnp.float32),
-        in_specs=[smem] + [vmem] * 4,
+        out_shape=[
+            pltpu.VMEM((8 * depth, lanes), jnp.float32),
+            pltpu.VMEM((LOW + 3 * width + HIGH, 3, depth, lanes), jnp.float32),
+        ],
+        in_specs=[vmem] * 6,
+        out_specs=[vmem] * 2,
+        scratch_shapes=[scratch],
+        compiler_params=limit,
+        cost_estimate=pl.CostEstimate(flops=LONG, bytes_accessed=4 * permeability.size * 4, transcendentals=0),
+    )(held(columns), held(pair), held(up), held(up_other), held(down), held(down_other))
+    joined = pl.pallas_call(
+        join_kernel,
+        out_shape=pltpu.VMEM((5 * strips, depth, lanes), jnp.float32),
+        in_specs=[vmem] * 3,
         out_specs=vmem,
-        scratch_shapes=scratch,
-        cost_estimate=pl.CostEstimate(flops=6_000_000, bytes_accessed=4 * permeability.size * 4, transcendentals=0),
-    )(layer_map, *tiles)
+        compiler_params=limit,
+    )(held(below), held(beside), held(above))
+    theirs = net.swap(joined)
     out = jax.ShapeDtypeStruct((3, NCL, width // BXY, lanes // BXY), jnp.float32)
     return pl.pallas_call(
         edge_kernel,
         out_shape=(out, out),
-        in_specs=[smem] + [vmem] * 7,
+        in_specs=[vmem] * 5,
         out_specs=(vmem, vmem),
-        scratch_shapes=scratch,
-    )(layer_map, *tiles, even, odd, inner)
+        scratch_shapes=[pltpu.VMEM((5 * strips, depth, lanes), jnp.float32), scratch],
+        compiler_params=limit,
+    )(held(picks), held(stack), held(joined), held(theirs), held(inner))
 
 
 def solution(mesh):

time: 21.8 us -> 13.7 us (0.63)
  the two profiles are of different devices: /device:TPU:10 before, /device:TPU:25 now
where the time goes in v3:
time: 13.7 us; the launch traced here: 13.5 us
  starting transfers between devices  6.16 us (45%)
  Pallas kernels  3.64 us (27%)
  waiting for transfers between devices  2.11 us (15%)
  local copies, waits for them, and re-layouts  0.93 us (7%)
  between operations  0.69 us (5%)
    ppermute x6, starting transfers between devices, permute(): self.sent[key] = (value, lax.ppermute(value, self.axes, pairs))  6.16 us
    ppermute x6, waiting for transfers between devices, permute(): self.sent[key] = (value, lax.ppermute(value, self.axes, pairs))  2.11 us
    pallas_call x1, Pallas kernels, local(): pl.pallas_call(edge_kernel, out_shape=(out, out), in_specs=[vmem] * 5, ou...  2 us
    pallas_call x1, Pallas kernels, local(): pl.pallas_call(main_kernel, out_shape=[pltpu.VMEM((8 * depth, lanes), jnp...  0.95 us
    unnamed x4, local copies, waits for them, and re-layouts  0.93 us
    pallas_call x1, Pallas kernels, local(): pl.pallas_call(picks_kernel, out_shape=pltpu.VMEM((8 * NCL, 8 * depth), j...  0.55 us
  transfers between devices with their start and end apart: 6, of which 2 were waited for; matrix products, arithmetic and copies ran while one was open for 0% of the time, Pallas kernels for 12%

profile of v3, /device:TPU:25, one launch (start us, length us, event | category | flops | bytes accessed | tf_op | source)
XLA Modules:
  0.0 13.5 jit_solution(3890128814765113676)
XLA Ops:
  0.6 0.7 %collective-permute-start = (f32[3,8,8,128]{3,2,1,0:T(8,128)}, f32[3,8,8,128]{3,2,1,0:T(8,128)S(1)}, u32[]{:S(2)}, u32[]{:S(2)}) collective-permute-start(f32[3,8,8,128]{3,2,1,0:T(8,128)} %mine.1), channel_id=1, source_target_pairs={{0,8},{1,9},{2,10},{3,11},{4,12},{5,13},{6,14},{7,15},{8,0},{9,1},... | collective-permute-start | bytes 294920 | tf_op jit(solution)/shard_map/ppermute | solution.py:402
  1.4 1.2 %collective-permute-start.1 = (f32[3,8,8,128]{3,2,1,0:T(8,128)}, f32[3,8,8,128]{3,2,1,0:T(8,128)S(1)}, u32[]{:S(2)}, u32[]{:S(2)}) collective-permute-start(f32[3,8,8,128]{3,2,1,0:T(8,128)} %mine.1), channel_id=1, source_target_pairs={{0,16},{1,17},{2,18},{3,19},{4,20},{5,21},{6,22},{7,23},{8,24},{9,... | collective-permute-start | bytes 294920 | tf_op jit(solution)/shard_map/ppermute | solution.py:402
  2.6 0.0 collective-permute-done.other
  2.6 0.0 copy-start
  2.6 0.9 %copy-done = f32[3,8,8,128]{3,2,1,0:T(8,128)S(1)} copy-done((f32[3,8,8,128]{3,2,1,0:T(8,128)S(1)}, f32[3,8,8,128]{3,2,1,0:T(8,128)}, u32[]{:S(2)}) %copy-start) | copy-done | bytes 98328
  3.5 0.1 shard_map.43
  3.7 0.0 copy-start.1
  3.7 1.3 %collective-permute-start.4 = (f32[8,8,128]{2,1,0:T(8,128)S(1)}, f32[8,8,128]{2,1,0:T(8,128)S(1)}, u32[]{:S(2)}, u32[]{:S(2)}) collective-permute-start(f32[8,8,128]{2,1,0:T(8,128)S(1)} %get-tuple-element.8), channel_id=1, source_target_pairs={{0,8},{1,0},{2,1},{3,2},{4,3},{5,4},{6,5},{7,6},{8,9},{9,10},{10,1... | collective-permute-start | bytes 98312 | tf_op jit(solution)/shard_map/ppermute | solution.py:402
  4.9 1.2 %collective-permute-start.3 = (f32[8,8,128]{2,1,0:T(8,128)S(1)}, f32[8,8,128]{2,1,0:T(8,128)S(1)}, u32[]{:S(2)}, u32[]{:S(2)}) collective-permute-start(f32[8,8,128]{2,1,0:T(8,128)S(1)} %get-tuple-element.8), channel_id=1, source_target_pairs={{0,24},{1,16},{2,17},{3,18},{4,19},{5,20},{6,21},{7,22},{8,25},{9,... | collective-permute-start | bytes 98312 | tf_op jit(solution)/shard_map/ppermute | solution.py:402
  6.1 0.0 collective-permute-done.1.up_mine.down_mine
  6.1 0.7 %collective-permute-start.2 = (f32[3,8,8,128]{3,2,1,0:T(8,128)S(1)}, f32[3,8,8,128]{3,2,1,0:T(8,128)S(1)}, u32[]{:S(2)}, u32[]{:S(2)}) collective-permute-start(f32[3,8,8,128]{3,2,1,0:T(8,128)S(1)} %collective-permute-done.1.up_mine.down_mine), channel_id=1, source_target_pairs={{0,8},{1,9},{2,10},{3,11},{4,12},{5,13},{6,14},{7,15},{8,0},{9,1},... | collective-permute-start | bytes 294920 | tf_op jit(solution)/shard_map/ppermute | solution.py:402
  6.9 0.0 copy-done.1
  6.9 0.6 %shard_map.41.picks = f32[32,64]{1,0:T(8,128)S(1)} custom-call(s32[8]{0:T(128)S(1)} %copy-done.1), custom_call_target="tpu_custom_call" | custom-call | tf_op jit(solution)/shard_map/pallas_call | solution.py:453
  7.4 0.1 collective-permute-done.4.beside
  7.5 2.0 %collective-permute-done.3.below.above = f32[8,8,128]{2,1,0:T(8,128)S(1)} collective-permute-done((f32[8,8,128]{2,1,0:T(8,128)S(1)}, f32[8,8,128]{2,1,0:T(8,128)S(1)}, u32[]{:S(2)}, u32[]{:S(2)}) %collective-permute-start.3) | collective-permute-done | bytes 32800 | tf_op jit(solution)/shard_map/ppermute | solution.py:402
  9.5 1.0 %collective-permute-start.5 = (f32[20,8,128]{2,1,0:T(8,128)S(1)}, f32[20,8,128]{2,1,0:T(8,128)S(1)}, u32[]{:S(2)}, u32[]{:S(2)}) collective-permute-start(f32[20,8,128]{2,1,0:T(8,128)S(1)} %shard_map.45.mine), channel_id=1, source_target_pairs={{0,8},{1,9},{2,10},{3,11},{4,12},{5,13},{6,14},{7,15},{8,0},{9,1},... | collective-permute-start | bytes 245768 | tf_op jit(solution)/shard_map/ppermute | solution.py:402
  10.6 0.0 collective-permute-done.2.up_other.down_other
  10.6 0.9 %shard_map.44 = (f32[64,128]{1,0:T(8,128)S(1)}, f32[33,3,8,128]{3,2,1,0:T(8,128)S(1)}) custom-call(f32[128,128]{1,0:T(8,128)S(1)} %shard_map.42.columns, f32[16,3,8,128]{3,2,1,0:T(8,128)S(1)} %get-tuple-element.6.pair, f32[3,8,8,128]{3,2,1,0:T(8,128)S(1)} %collective-permute-done.1.up_mine.down_mine, ...), custom_call_target="tpu_custom_call" | custom-call | flops 10000000000 | bytes 393216 | tf_op jit(solution)/shard_map/pallas_call | solution.py:461
  11.5 0.0 collective-permute-done.5.other
  11.5 2.0 %shard_map.46 = (f32[3,4,1,16]{3,2,1,0:T(1,128)}, f32[3,4,1,16]{3,2,1,0:T(1,128)}) custom-call(f32[32,64]{1,0:T(8,128)S(1)} %shard_map.41.picks, f32[33,3,8,128]{3,2,1,0:T(8,128)S(1)} %get-tuple-element.7.stack, f32[20,8,128]{2,1,0:T(8,128)S(1)} %shard_map.45.mine, f32[20,8,128]{2,1,0:T(8,128)S(1)} %collective-permute-done.5.other, ...), custom_call_target="tpu_custom_call" | custom-call | tf_op jit(solution)/shard_map/pallas_call | solution.py:482
  (2 shorter events, 0.0 us)
Async XLA Ops:
  0.6 2.0 %collective-permute-start = (f32[3,8,8,128]{3,2,1,0:T(8,128)}, f32[3,8,8,128]{3,2,1,0:T(8,128)S(1)}, u32[]{:S(2)}, u32[]{:S(2)}) collective-permute-start(f32[3,8,8,128]{3,2,1,0:T(8,128)} %mine.1), channel_id=1, source_target_pairs={{0,8},{1,9},{2,10},{3,11},{4,12},{5,13},{6,14},{7,15},{8,0},{9,1},... | collective-permute-start | bytes 294920 | tf_op jit(solution)/shard_map/ppermute | solution.py:402
  1.4 4.8 %collective-permute-start.1 = (f32[3,8,8,128]{3,2,1,0:T(8,128)}, f32[3,8,8,128]{3,2,1,0:T(8,128)S(1)}, u32[]{:S(2)}, u32[]{:S(2)}) collective-permute-start(f32[3,8,8,128]{3,2,1,0:T(8,128)} %mine.1), channel_id=1, source_target_pairs={{0,16},{1,17},{2,18},{3,19},{4,20},{5,21},{6,22},{7,23},{8,24},{9,... | collective-permute-start | bytes 294920 | tf_op jit(solution)/shard_map/ppermute | solution.py:402
  2.6 0.9 %copy-start = (f32[3,8,8,128]{3,2,1,0:T(8,128)S(1)}, f32[3,8,8,128]{3,2,1,0:T(8,128)}, u32[]{:S(2)}) copy-start(f32[3,8,8,128]{3,2,1,0:T(8,128)} %mine.1) | copy-start | bytes 294916
  3.7 3.2 %copy-start.1 = (s32[8]{0:T(128)S(1)}, s32[8]{0:T(128)}, u32[]{:S(2)}) copy-start(s32[8]{0:T(128)} %layer_map.1) | copy-start | bytes 100
  3.7 3.8 %collective-permute-start.4 = (f32[8,8,128]{2,1,0:T(8,128)S(1)}, f32[8,8,128]{2,1,0:T(8,128)S(1)}, u32[]{:S(2)}, u32[]{:S(2)}) collective-permute-start(f32[8,8,128]{2,1,0:T(8,128)S(1)} %get-tuple-element.8), channel_id=1, source_target_pairs={{0,8},{1,0},{2,1},{3,2},{4,3},{5,4},{6,5},{7,6},{8,9},{9,10},{10,1... | collective-permute-start | bytes 98312 | tf_op jit(solution)/shard_map/ppermute | solution.py:402
  4.9 4.6 %collective-permute-start.3 = (f32[8,8,128]{2,1,0:T(8,128)S(1)}, f32[8,8,128]{2,1,0:T(8,128)S(1)}, u32[]{:S(2)}, u32[]{:S(2)}) collective-permute-start(f32[8,8,128]{2,1,0:T(8,128)S(1)} %get-tuple-element.8), channel_id=1, source_target_pairs={{0,24},{1,16},{2,17},{3,18},{4,19},{5,20},{6,21},{7,22},{8,25},{9,... | collective-permute-start | bytes 98312 | tf_op jit(solution)/shard_map/ppermute | solution.py:402
  6.1 4.4 %collective-permute-start.2 = (f32[3,8,8,128]{3,2,1,0:T(8,128)S(1)}, f32[3,8,8,128]{3,2,1,0:T(8,128)S(1)}, u32[]{:S(2)}, u32[]{:S(2)}) collective-permute-start(f32[3,8,8,128]{3,2,1,0:T(8,128)S(1)} %collective-permute-done.1.up_mine.down_mine), channel_id=1, source_target_pairs={{0,8},{1,9},{2,10},{3,11},{4,12},{5,13},{6,14},{7,15},{8,0},{9,1},... | collective-permute-start | bytes 294920 | tf_op jit(solution)/shard_map/ppermute | solution.py:402
  9.5 2.0 %collective-permute-start.5 = (f32[20,8,128]{2,1,0:T(8,128)S(1)}, f32[20,8,128]{2,1,0:T(8,128)S(1)}, u32[]{:S(2)}, u32[]{:S(2)}) collective-permute-start(f32[20,8,128]{2,1,0:T(8,128)S(1)} %shard_map.45.mine), channel_id=1, source_target_pairs={{0,8},{1,9},{2,10},{3,11},{4,12},{5,13},{6,14},{7,15},{8,0},{9,1},... | collective-permute-start | bytes 245768 | tf_op jit(solution)/shard_map/ppermute | solution.py:402

commit v4 on v3

v4 whole, which is shorter than its diff:
```python
import functools
import math

import jax
import jax.numpy as jnp
from jax import lax
from jax.experimental import pallas as pl
from jax.experimental.pallas import tpu as pltpu
from jax.sharding import PartitionSpec as P

NCL = 4
BXY = 8
SWEEPS = 4
KMIN = 0.01
EPS = 1e-06

LOW = SWEEPS
HIGH = SWEEPS + 1
RIGHT = BXY + HIGH
START = RIGHT + LOW


def sweep_weights(count):
    return [
        1.0 / (1.05 + 0.95 * math.cos(math.pi * (2 * s + 1) / (2 * count))) for s in range(count)
    ]


WEIGHTS = sweep_weights(SWEEPS)


SCALES = [math.prod(WEIGHTS[: s + 1]) for s in range(SWEEPS)]


def harmonic(left, right):
    return 2.0 * left * right / (left + right)


def lanes_of(shape):
    return lax.broadcasted_iota(jnp.int32, shape, len(shape) - 1)


def up(value, axis):
    return pltpu.roll(value, value.shape[axis] - 1, axis)


def down(value, axis):
    return pltpu.roll(value, 1, axis)


def layers_of(tile, comp, row):
    _, depth, width, lanes = tile.shape
    flat = tile.reshape(3 * depth * width, lanes)
    return flat[pl.ds(comp * depth * width + row, depth, stride=width), :]


LONG = 10**10


class Solver:
    def __init__(self, inverse_of, scratch, y_ends, y_starts):
        self.inverse_of = inverse_of
        self.scratch = scratch
        self.slots = {}
        self.cache = {}
        shape = scratch.shape[1:]
        layer = lax.broadcasted_iota(jnp.int32, shape, 0)
        self.top = layer == shape[0] - 1
        self.bottom = layer == 0
        self.y_ends = y_ends
        self.y_starts = y_starts

    def memo(self, key, make):
        if key not in self.cache:
            self.cache[key] = make()
        return self.cache[key]

    def stored(self, key, make):
        if key not in self.slots:
            value = make()
            self.slots[key] = len(self.slots)
            self.scratch[self.slots[key]] = value
        return self.scratch[self.slots[key]]

    def inverse(self, comp, row):
        return self.memo(("k", comp, row), lambda: self.inverse_of(comp, row))

    def x_face(self, row):
        return self.memo(("tx", row), lambda: 1.0 / (self.inverse(0, row) + self.inverse(0, row + 1)))

    def x_edge(self, row):
        return self.memo(("te", row), lambda: 1.0 / (self.inverse(0, row) + self.inverse(0, row)))

    def y_faces(self, row):
        def make():
            here = self.inverse(1, row)
            above = up(here, 1)
            if self.y_ends is None:
                upper = 1.0 / (here + above)
                return upper, down(upper, 1)
            below = jnp.where(self.y_starts, here, down(here, 1))
            return 1.0 / (here + jnp.where(self.y_ends, here, above)), 1.0 / (here + below)

        return self.memo(("ty", row), make)

    def z_faces(self, row):
        def make():
            here = self.inverse(2, row)
            above = jnp.where(self.top, here, up(here, 0))
            below = jnp.where(self.bottom, here, down(here, 0))
            return 1.0 / (here + above), 1.0 / (here + below)

        return self.memo(("tz", row), make)

    def side_faces(self, row):
        def make():
            ty, ty_low = self.y_faces(row)
            tz, tz_low = self.z_faces(row)
            total = (ty + ty_low) + (tz + tz_low)
            if self.y_ends is not None:
                ty = jnp.where(self.y_ends, 0.0, ty)
                ty_low = jnp.where(self.y_starts, 0.0, ty_low)
            return ty, ty_low, jnp.where(self.top, 0.0, tz), jnp.where(self.bottom, 0.0, tz_low), total

        return self.memo(("side", row), make)

    def x_faces(self, row, edge):
        upper = self.x_edge(row) if edge == "up" else self.x_face(row)
        lower = self.x_edge(row) if edge == "low" else self.x_face(row - 1)
        return upper, lower

    def edge_of(self, row, boundary):
        return boundary[0] if boundary is not None and boundary[1] == row else None

    def scale(self, row, edge):
        def make():
            upper, lower = self.x_faces(row, edge)
            return 1.0 / ((upper + lower) + self.side_faces(row)[4])

        return self.memo(("h", row, edge), make)

    def weight(self, which, row, edge):
        def make():
            faces = self.x_faces(row, edge) if which < 2 else self.side_faces(row)[:4]
            return faces[which % 2 if which < 2 else which - 2] * self.scale(row, edge)

        return self.stored(("a", which, row, edge), make)

    def drive(self, d, row, edge):
        def make():
            upper, lower = (
                self.x_faces(row, edge) if d == 0 else self.y_faces(row) if d == 1 else self.z_faces(row)
            )
            return (upper - lower) * self.scale(row, edge)

        return self.stored(("c", d, row, edge), make)

    def pressure(self, d, count, row, boundary):
        if boundary is not None and abs(row - boundary[1]) >= count:
            boundary = None
        edge = self.edge_of(row, boundary)
        if count == 1:
            return self.drive(d, row, edge)

        def make():
            a = lambda which: self.weight(which, row, edge)
            here = self.pressure(d, count - 1, row, boundary)
            w = WEIGHTS[count - 1]
            if count == 2:
                total = ((1.0 - w) / w + 1.0 / SCALES[0]) * here
            else:
                total = ((1.0 - w) / w) * here + (1.0 / SCALES[count - 2]) * self.drive(d, row, edge)
            side = a(2) * up(here, 1) + a(3) * down(here, 1)
            layers = a(4) * up(here, 0) + a(5) * down(here, 0)
            if edge != "up":
                total = total + a(0) * self.pressure(d, count - 1, row + 1, boundary)
            if edge != "low":
                total = total + a(1) * self.pressure(d, count - 1, row - 1, boundary)
            return total + (side + layers)

        return self.memo(("u", d, count, row, boundary), make)

    def sums(self, d, row, boundary):
        if boundary is not None:
            reach = SWEEPS + (1 if d == 0 and boundary[0] == "up" else 0)
            if abs(row - boundary[1]) >= reach:
                boundary = None

        def make():
            here = self.pressure(d, SWEEPS, row, boundary)
            edge = self.edge_of(row, boundary)
            if d == 0:
                face = self.x_faces(row, edge)[0]
                above = None if edge == "up" else self.pressure(d, SWEEPS, row + 1, boundary)
            elif d == 1:
                face = self.y_faces(row)[0]
                above = up(here, 1)
                if self.y_ends is not None:
                    above = jnp.where(self.y_ends, 0.0, above)
            else:
                face = self.z_faces(row)[0]
                above = jnp.where(self.top, 0.0, up(here, 0))
            drop = 1.0 / SCALES[-1] - here
            if above is not None:
                drop = drop + above
            square = drop * drop
            return face * square, square

        return self.memo(("s", d, row, boundary), make)

    def block(self, d, begin, patches):
        uses = {}
        for row in range(begin, begin + BXY):
            for boundary, weight in patches:
                pair = self.sums(d, row, boundary)
                uses.setdefault(id(pair), (pair, []))[1].append(weight)
        groups = {}
        for pair, weights in uses.values():
            groups.setdefault(tuple(map(id, weights)), (weights, []))[1].append(pair)
        totals = None
        for weights, pairs in groups.values():
            part = [functools.reduce(jnp.add, parts) for parts in zip(*pairs)]
            if weights != [None]:
                factor = sum(1.0 if w is None else w for w in weights)
                part = [factor * p for p in part]
            totals = part if totals is None else [a + b for a, b in zip(totals, part)]
        return totals


def accumulate(solver, present):
    low, high, high2 = present
    own = [(("up", BXY - 1), low), (None, None), (("low", 0), high)]
    after = [(("up", 2 * BXY - 1), None), (None, None), (("low", BXY), high2)]
    jobs = [(d, 0, own) for d in range(3)] + [(0, BXY, after)]
    results = {}
    order = [jobs[0], jobs[1], jobs[2], jobs[3]]
    for row in range(BXY):
        for d, begin, patches in order:
            for boundary, _ in patches:
                solver.sums(d, begin + row, boundary)
    for i, (d, begin, patches) in enumerate(jobs):
        results[i] = solver.block(d, begin, patches)
    return [value for i in range(len(jobs)) for value in results[i]]


def thirds(value):
    parts = []
    for _ in range(3):
        parts.append(value.astype(jnp.bfloat16))
        value = value - parts[-1].astype(jnp.float32)
    return parts


def sum_columns(sums, columns):
    value = jnp.concatenate(sums, axis=0)
    count = value.shape[0]
    parts = jnp.dot(
        jnp.concatenate(thirds(value), axis=0),
        columns.astype(jnp.bfloat16),
        preferred_element_type=jnp.float32,
    )
    return parts[:count] + parts[count : 2 * count] + parts[2 * count :]


def sum_layers(picks, value):
    return jnp.dot(
        jnp.concatenate([picks.astype(jnp.bfloat16)] * 3, axis=1),
        jnp.concatenate(thirds(value), axis=0),
        preferred_element_type=jnp.float32,
    )


def picks_kernel(layer_map, out):
    depth = out.shape[1] // (out.shape[0] // NCL)
    r = lax.broadcasted_iota(jnp.int32, out.shape, 0)
    c = lax.broadcasted_iota(jnp.int32, out.shape, 1)
    layer = jnp.zeros(out.shape, jnp.int32)
    for z in range(depth):
        layer = jnp.where(c % depth == z, layer_map[z], layer)
    out[...] = ((r // NCL == c // depth) & (r % NCL == layer)).astype(jnp.float32)


def place(axes):
    i, j = (lax.axis_index(a) for a in axes)
    nx, ny = (lax.axis_size(a) for a in axes)
    core, chip = i % 2, i // 2
    one = lambda test: jnp.where(test, 1.0, 0.0).astype(jnp.float32)
    tiles = one(i > 0), one(i < nx - 1), one(i < nx - 2)
    chips = one(chip > 0), one(chip < nx // 2 - 1)
    return core, tiles, chips, (one(j > 0), one(j < ny - 1))


def slots(width):
    return [(comp, row) for row in range(width) for comp in range(3)]


def table_kernel(out):
    lanes = out.shape[0]
    r = lax.broadcasted_iota(jnp.int32, out.shape, 0)
    c = lax.broadcasted_iota(jnp.int32, out.shape, 1)
    inner = (r // BXY == c) & (c > 0) & (c < lanes // BXY - 1)
    out[...] = inner.astype(jnp.float32)


def pack_kernel(mine, other, pair, packed):
    core, _, _, _ = place(("gx", "gy"))
    _, depth, width, lanes = mine.shape
    per = lanes // RIGHT
    lane = lanes_of((depth, lanes))
    rows = slots(width)
    count = packed.shape[0] // 2
    for tile, at in ((mine, core), (other, 1 - core)):
        strip = None
        for n, (comp, row) in enumerate(rows):
            value = layers_of(tile, comp, row)
            pair[at * width + row, comp] = value
            shift = RIGHT * (n % per)
            value = pltpu.roll(value, shift + core * START, 1)
            strip = value if n % per == 0 else jnp.where(lane < shift + core * RIGHT, strip, value)
            if n % per == per - 1 or n == len(rows) - 1:
                packed[at * count + n // per] = strip


def join_kernel(below, beside, above, out):
    half = beside.shape[0] // 2
    out[:half] = below[half:]
    out[half : 3 * half] = beside[...]
    out[3 * half :] = above[...]


def stack_kernel(pair, up_mine, up_other, down_mine, down_other, stack, placed):
    core, _, (has_down, has_up), _ = place(("gx", "gy"))
    width = up_mine.shape[2]
    depth, lanes = pair.shape[2:]
    first = core == 0
    lane = lanes_of((depth, lanes))
    half, start = lanes // 2, START
    stop = start + BXY + HIGH
    near = (lane >= start) & (lane < stop)
    second = (lane >= half - BXY - LOW) & (lane < half + stop)

    def put(row, comp, value):
        value = 1.0 / (value + KMIN)
        stack[LOW + row, comp] = value
        value = jnp.where(near, pltpu.roll(value, start, 1), value)
        placed[LOW + row, comp] = jnp.where(second, pltpu.roll(value, half, 1), value)

    for row in range(2 * width):
        for comp in range(3):
            put(row, comp, pair[row, comp])
    for row in range(width):
        for comp in range(3):
            mine, other = layers_of(up_mine, comp, row), layers_of(up_other, comp, row)
            put(2 * width + row, comp, jnp.where(first, mine, other) * has_up)
            if row < HIGH:
                put(3 * width + row, comp, jnp.where(first, other, mine) * has_up)
            if row >= width - LOW:
                mine, other = layers_of(down_mine, comp, row), layers_of(down_other, comp, row)
                put(row - width, comp, jnp.where(first, other, mine) * has_down)


def main_kernel(columns, stack, out, scratch):
    core, present, _, _ = place(("gx", "gy"))
    base = LOW + core * BXY
    solver = Solver(lambda comp, row: stack[base + row, comp], scratch, None, None)
    out[...] = sum_columns(accumulate(solver, present), columns[...])


def edge_kernel(picks, placed, mine, other, inner, perm_out, trans_out, scratch):
    core, present, _, (has_left, has_right) = place(("gx", "gy"))
    depth, lanes = placed.shape[2:]
    width = BXY
    per = lanes // RIGHT
    lane = lanes_of((depth, lanes))
    half, start = lanes // 2, START
    first = core == 0
    low, high, high2 = present
    kept = {-1: low, 0: 1.0, 1: high, 2: high2}
    per_tile = mine.shape[0] // 5
    index = {key: at for at, key in enumerate(slots(width))}
    turned = (lane >= half) & (lane < half + START)
    strips = {}

    def strip(tile, n):
        if (tile, n) not in strips:
            at = (core + 1 + tile) * per_tile + n
            a, b = mine[at], other[at]
            strips[tile, n] = tuple(
                1.0 / (value * (kept[tile] * there) + KMIN)
                for value, there in ((jnp.where(first, a, b), has_right), (jnp.where(first, b, a), has_left))
            )
        return strips[tile, n]

    base = LOW + core * width

    def inverse(comp, row):
        at = index[comp, row % width]
        shift = -RIGHT * (at % per) % lanes
        right, left = (pltpu.roll(v, shift, 1) if shift else v for v in strip(row // width, at // per))
        theirs = jnp.where(lane < RIGHT, right, left)
        value = jnp.where(turned, pltpu.roll(theirs, half, 1), placed[base + row, comp])
        return jnp.where(lane < START, theirs, value)

    y_ends = (lane == BXY - 1) | (lane == half + start + BXY - 1)
    y_starts = lane == half - BXY
    solver = Solver(inverse, scratch, y_ends, y_starts)
    sums = accumulate(solver, present)
    r = lax.broadcasted_iota(jnp.int32, (lanes, lanes), 0)
    c = lax.broadcasted_iota(jnp.int32, (lanes, lanes), 1)
    count = lanes // BXY

    def span(begin):
        return (r >= begin) & (r < begin + BXY)

    first = jnp.where(span(start), 1.0, 0.0) + jnp.where(span(half + start), has_left, 0.0)
    final = jnp.where(span(lanes - BXY), 1.0, 0.0) + jnp.where(span(half - BXY), has_right, 0.0)
    beyond = jnp.where(span(0) | span(half), has_right, 0.0)
    columns = jnp.where(
        c == 0, first, jnp.where(c == count - 1, final, jnp.where(c == count, beyond, 0.0))
    )
    total = sum_layers(picks[...], inner[...] + sum_columns(sums, columns))
    cells = (width + 2 * BXY, lanes + 2 * BXY, depth)
    energy = [total[2 * NCL * q : 2 * NCL * q + NCL] for q in range(4)]
    square = [total[2 * NCL * q + NCL : 2 * NCL * (q + 1)] for q in range(4)]
    perms = [
        2.0 * energy[q] / (square[q] + EPS * (cells[d] / SCALES[-1]) ** 2)
        for q, d in enumerate((0, 1, 2, 0))
    ]
    layer = lax.broadcasted_iota(jnp.int32, perms[0].shape, 0)
    trans = [
        harmonic(perms[0], perms[3] * present[1]),
        harmonic(perms[1], up(perms[1], 1)),
    ]
    above = jnp.concatenate([perms[2][1:], jnp.zeros_like(perms[2][:1])], axis=0)
    trans.append(harmonic(perms[2], above))
    for d in range(3):
        for l in range(NCL):
            perm_out[d, l, :, :] = perms[d][l : l + 1, :count]
            trans_out[d, l, :, :] = trans[d][l : l + 1, :count]


class Exchange:
    def __init__(self, axes):
        self.axes = axes
        self.nx, self.ny = (lax.axis_size(a) for a in axes)
        self.sent = {}

    def permute(self, value, target):
        nx, ny = self.nx, self.ny
        pairs = []
        for i in range(nx):
            for j in range(ny):
                a, b = target(i, j)
                pairs.append((i * ny + j, a % nx * ny + b))
        key = (id(value), tuple(pairs))
        if key not in self.sent:
            self.sent[key] = (value, lax.ppermute(value, self.axes, pairs))
        return self.sent[key][1]

    def swap(self, value):
        return self.permute(value, lambda i, j: (i ^ 1, j))

    def straight(self, value, pairs):
        return self.permute(value, lambda i, j: (i - 2 * pairs, j))

    def sideways(self, value, pairs):
        def target(i, j):
            to = j - 1 if i % 2 == 0 else j + 1
            i -= 2 * pairs
            return (i, to) if 0 <= to < self.ny else (i ^ 1, j)

        return self.permute(value, target)


def local(permeability, layer_map):
    _, depth, width, lanes = permeability.shape
    net = Exchange(("gx", "gy"))
    if width != BXY or depth != 8 or lanes != 128 or net.nx % 2:
        raise ValueError("unsupported tile")
    vmem = pl.BlockSpec(memory_space=pltpu.VMEM)
    smem = pl.BlockSpec(memory_space=pltpu.SMEM)
    limit = pltpu.CompilerParams(vmem_limit_bytes=16 << 20)
    held = lambda value: pltpu.with_memory_space_constraint(value, pltpu.VMEM)
    strips = -(-len(slots(width)) // (lanes // RIGHT))

    columns = pl.pallas_call(
        table_kernel,
        out_shape=pltpu.VMEM((lanes, lanes), jnp.float32),
        out_specs=vmem,
        compiler_params=limit,
        cost_estimate=pl.CostEstimate(flops=LONG, bytes_accessed=lanes * lanes * 4, transcendentals=0),
    )()
    other = net.swap(permeability)
    up, down = net.straight(permeability, 1), net.straight(permeability, -1)
    pair, packed = pl.pallas_call(
        pack_kernel,
        out_shape=[
            pltpu.VMEM((2 * width, 3, depth, lanes), jnp.float32),
            pltpu.VMEM((2 * strips, depth, lanes), jnp.float32),
        ],
        in_specs=[vmem] * 2,
        out_specs=[vmem] * 2,
        compiler_params=limit,
    )(held(permeability), held(other))
    above, below = net.sideways(packed, 1), net.sideways(packed, -1)
    beside = net.sideways(packed, 0)
    up_other, down_other = net.swap(up), net.swap(down)
    picks = pl.pallas_call(
        picks_kernel,
        out_shape=pltpu.VMEM((8 * NCL, 8 * depth), jnp.float32),
        in_specs=[smem],
        out_specs=vmem,
        compiler_params=limit,
    )(layer_map)
    scratch = pltpu.VMEM((256, depth, lanes), jnp.float32)
    rows = LOW + 3 * width + HIGH
    stack, placed = pl.pallas_call(
        stack_kernel,
        out_shape=[pltpu.VMEM((rows, 3, depth, lanes), jnp.float32)] * 2,
        in_specs=[vmem] * 5,
        out_specs=[vmem] * 2,
        compiler_params=limit,
        cost_estimate=pl.CostEstimate(flops=LONG, bytes_accessed=4 * permeability.size * 4, transcendentals=0),
    )(held(pair), held(up), held(up_other), held(down), held(down_other))
    inner = pl.pallas_call(
        main_kernel,
        out_shape=pltpu.VMEM((8 * depth, lanes), jnp.float32),
        in_specs=[vmem] * 2,
        out_specs=vmem,
        scratch_shapes=[scratch],
        compiler_params=limit,
        cost_estimate=pl.CostEstimate(flops=LONG, bytes_accessed=4 * permeability.size * 4, transcendentals=0),
    )(held(columns), held(stack))
    joined = pl.pallas_call(
        join_kernel,
        out_shape=pltpu.VMEM((5 * strips, depth, lanes), jnp.float32),
        in_specs=[vmem] * 3,
        out_specs=vmem,
        compiler_params=limit,
    )(held(below), held(beside), held(above))
    theirs = net.swap(joined)
    out = jax.ShapeDtypeStruct((3, NCL, width // BXY, lanes // BXY), jnp.float32)
    return pl.pallas_call(
        edge_kernel,
        out_shape=(out, out),
        in_specs=[vmem] * 5,
        out_specs=(vmem, vmem),
        scratch_shapes=[scratch],
        compiler_params=limit,
    )(held(picks), held(placed), held(joined), held(theirs), held(inner))


def solution(mesh):
    in_specs = (P(None, None, "gx", "gy"), P())
    out_specs = (P(None, None, "gx", "gy"), P(None, None, "gx", "gy"))
    return jax.shard_map(local, mesh=mesh, in_specs=in_specs, out_specs=out_specs, check_vma=False)
```

time: 13.7 us -> 13.5 us (0.985)
  waiting for transfers between devices: 2.11 us -> 1.95 us
    pallas_call x1 -> x2, Pallas kernels: 0.95 us -> 1.17 us  [the longest x1 0.79 us: local(): pl.pallas_call(main_kernel, out_shape=pltpu.VMEM((8 * depth, lanes), jnp....]
    pallas_call x1, Pallas kernels: 2 us -> 1.8 us  [local(): pl.pallas_call(edge_kernel, out_shape=(out, out), in_specs=[vmem] * 5, ou...]
    ppermute x6, waiting for transfers between devices: 2.11 us -> 1.95 us  [permute(): self.sent[key] = (value, lax.ppermute(value, self.axes, pairs))]
  transfers between devices with their start and end apart: 6 -> 6, of which waited for: 2 -> 2; matrix products, arithmetic and copies ran while one was open for 0% -> 0% of each run, Pallas kernels for 12% -> 14%
where the time goes in v4:
time: 13.5 us; the launch traced here: 13.3 us
  starting transfers between devices  6.08 us (45%)
  Pallas kernels  3.68 us (27%)
  waiting for transfers between devices  1.95 us (14%)
  local copies, waits for them, and re-layouts  0.93 us (7%)
  between operations  0.69 us (5%)
    ppermute x6, starting transfers between devices, permute(): self.sent[key] = (value, lax.ppermute(value, self.axes, pairs))  6.08 us
    ppermute x6, waiting for transfers between devices, permute(): self.sent[key] = (value, lax.ppermute(value, self.axes, pairs))  1.95 us
    pallas_call x1, Pallas kernels, local(): pl.pallas_call(edge_kernel, out_shape=(out, out), in_specs=[vmem] * 5, ou...  1.8 us
    unnamed x4, local copies, waits for them, and re-layouts  0.93 us
    pallas_call x1, Pallas kernels, local(): pl.pallas_call(main_kernel, out_shape=pltpu.VMEM((8 * depth, lanes), jnp....  0.79 us
    pallas_call x1, Pallas kernels, local(): pl.pallas_call(picks_kernel, out_shape=pltpu.VMEM((8 * NCL, 8 * depth), j...  0.55 us
    pallas_call x1, Pallas kernels, local(): pl.pallas_call(stack_kernel, out_shape=[pltpu.VMEM((rows, 3, depth, lanes...  0.38 us
  transfers between devices with their start and end apart: 6, of which 2 were waited for; matrix products, arithmetic and copies ran while one was open for 0% of the time, Pallas kernels for 14%

profile of v4, /device:TPU:25, one launch (start us, length us, event | category | flops | bytes accessed | tf_op | source)
XLA Modules:
  0.0 13.3 jit_solution(2497746345816586252)
XLA Ops:
  0.6 0.7 %collective-permute-start = (f32[3,8,8,128]{3,2,1,0:T(8,128)}, f32[3,8,8,128]{3,2,1,0:T(8,128)S(1)}, u32[]{:S(2)}, u32[]{:S(2)}) collective-permute-start(f32[3,8,8,128]{3,2,1,0:T(8,128)} %mine.1), channel_id=1, source_target_pairs={{0,8},{1,9},{2,10},{3,11},{4,12},{5,13},{6,14},{7,15},{8,0},{9,1},... | collective-permute-start | bytes 294920 | tf_op jit(solution)/shard_map/ppermute | solution.py:457
  1.4 1.2 %collective-permute-start.1 = (f32[3,8,8,128]{3,2,1,0:T(8,128)}, f32[3,8,8,128]{3,2,1,0:T(8,128)S(1)}, u32[]{:S(2)}, u32[]{:S(2)}) collective-permute-start(f32[3,8,8,128]{3,2,1,0:T(8,128)} %mine.1), channel_id=1, source_target_pairs={{0,16},{1,17},{2,18},{3,19},{4,20},{5,21},{6,22},{7,23},{8,24},{9,... | collective-permute-start | bytes 294920 | tf_op jit(solution)/shard_map/ppermute | solution.py:457
  2.6 0.0 collective-permute-done.other
  2.6 0.0 copy-start
  2.6 0.9 %copy-done = f32[3,8,8,128]{3,2,1,0:T(8,128)S(1)} copy-done((f32[3,8,8,128]{3,2,1,0:T(8,128)S(1)}, f32[3,8,8,128]{3,2,1,0:T(8,128)}, u32[]{:S(2)}) %copy-start) | copy-done | bytes 98328
  3.5 0.1 shard_map.42
  3.7 0.0 copy-start.1
  3.7 2.1 %collective-permute-start.3 = (f32[6,8,128]{2,1,0:T(8,128)S(1)}, f32[6,8,128]{2,1,0:T(8,128)S(1)}, u32[]{:S(2)}, u32[]{:S(2)}) collective-permute-start(f32[6,8,128]{2,1,0:T(8,128)S(1)} %get-tuple-element.8), channel_id=1, source_target_pairs={{0,24},{1,16},{2,17},{3,18},{4,19},{5,20},{6,21},{7,22},{8,25},{9,... | collective-permute-start | bytes 73736 | tf_op jit(solution)/shard_map/ppermute | solution.py:457
  5.8 0.5 %collective-permute-start.4 = (f32[6,8,128]{2,1,0:T(8,128)S(1)}, f32[6,8,128]{2,1,0:T(8,128)S(1)}, u32[]{:S(2)}, u32[]{:S(2)}) collective-permute-start(f32[6,8,128]{2,1,0:T(8,128)S(1)} %get-tuple-element.8), channel_id=1, source_target_pairs={{0,8},{1,0},{2,1},{3,2},{4,3},{5,4},{6,5},{7,6},{8,9},{9,10},{10,1... | collective-permute-start | bytes 73736 | tf_op jit(solution)/shard_map/ppermute | solution.py:457
  6.3 0.0 collective-permute-done.1.up_mine.down_mine
  6.3 0.5 %collective-permute-start.2 = (f32[3,8,8,128]{3,2,1,0:T(8,128)S(1)}, f32[3,8,8,128]{3,2,1,0:T(8,128)S(1)}, u32[]{:S(2)}, u32[]{:S(2)}) collective-permute-start(f32[3,8,8,128]{3,2,1,0:T(8,128)S(1)} %collective-permute-done.1.up_mine.down_mine), channel_id=1, source_target_pairs={{0,8},{1,9},{2,10},{3,11},{4,12},{5,13},{6,14},{7,15},{8,0},{9,1},... | collective-permute-start | bytes 294920 | tf_op jit(solution)/shard_map/ppermute | solution.py:457
  6.9 0.0 copy-done.1
  6.9 0.6 %shard_map.41.picks = f32[32,64]{1,0:T(8,128)S(1)} custom-call(s32[8]{0:T(128)S(1)} %copy-done.1), custom_call_target="tpu_custom_call" | custom-call | tf_op jit(solution)/shard_map/pallas_call | solution.py:508
  7.4 0.9 %collective-permute-done.3.below.above = f32[6,8,128]{2,1,0:T(8,128)S(1)} collective-permute-done((f32[6,8,128]{2,1,0:T(8,128)S(1)}, f32[6,8,128]{2,1,0:T(8,128)S(1)}, u32[]{:S(2)}, u32[]{:S(2)}) %collective-permute-start.3) | collective-permute-done | bytes 24608 | tf_op jit(solution)/shard_map/ppermute | solution.py:457
  8.3 1.1 %collective-permute-done.4.beside = f32[6,8,128]{2,1,0:T(8,128)S(1)} collective-permute-done((f32[6,8,128]{2,1,0:T(8,128)S(1)}, f32[6,8,128]{2,1,0:T(8,128)S(1)}, u32[]{:S(2)}, u32[]{:S(2)}) %collective-permute-start.4) | collective-permute-done | bytes 24608 | tf_op jit(solution)/shard_map/ppermute | solution.py:457
  9.4 0.9 %collective-permute-start.5 = (f32[15,8,128]{2,1,0:T(8,128)S(1)}, f32[15,8,128]{2,1,0:T(8,128)S(1)}, u32[]{:S(2)}, u32[]{:S(2)}) collective-permute-start(f32[15,8,128]{2,1,0:T(8,128)S(1)} %shard_map.44.mine), channel_id=1, source_target_pairs={{0,8},{1,9},{2,10},{3,11},{4,12},{5,13},{6,14},{7,15},{8,0},{9,1},... | collective-permute-start | bytes 184328 | tf_op jit(solution)/shard_map/ppermute | solution.py:457
  10.3 0.0 collective-permute-done.2.up_other.down_other
  10.3 0.4 %shard_map.43 = (f32[33,3,8,128]{3,2,1,0:T(8,128)S(1)}, f32[33,3,8,128]{3,2,1,0:T(8,128)S(1)}) custom-call(f32[16,3,8,128]{3,2,1,0:T(8,128)S(1)} %get-tuple-element.6.pair, f32[3,8,8,128]{3,2,1,0:T(8,128)S(1)} %collective-permute-done.1.up_mine.down_mine, f32[3,8,8,128]{3,2,1,0:T(8,128)S(1)} %collective-permute-done.2.up_other.down_other, ...), custom_call_target="tpu_custom_call" | custom-call | flops 10000000000 | bytes 393216 | tf_op jit(solution)/shard_map/pallas_call | solution.py:517
  10.7 0.8 %shard_map.46.inner = f32[64,128]{1,0:T(8,128)S(1)} custom-call(f32[128,128]{1,0:T(8,128)S(1)} %shard_map.45.columns, f32[33,3,8,128]{3,2,1,0:T(8,128)S(1)} %get-tuple-element.9.stack), custom_call_target="tpu_custom_call" | custom-call | flops 10000000000 | bytes 393216 | tf_op jit(solution)/shard_map/pallas_call | solution.py:525
  11.5 0.0 collective-permute-done.5.other
  11.5 1.8 %shard_map.47 = (f32[3,4,1,16]{3,2,1,0:T(1,128)}, f32[3,4,1,16]{3,2,1,0:T(1,128)}) custom-call(f32[32,64]{1,0:T(8,128)S(1)} %shard_map.41.picks, f32[33,3,8,128]{3,2,1,0:T(8,128)S(1)} %get-tuple-element.7.placed, f32[15,8,128]{2,1,0:T(8,128)S(1)} %shard_map.44.mine, f32[15,8,128]{2,1,0:T(8,128)S(1)} %collective-permute-done.5.other, ...), custom_call_target="tpu_custom_call" | custom-call | tf_op jit(solution)/shard_map/pallas_call | solution.py:543
  (2 shorter events, 0.0 us)
Async XLA Ops:
  0.6 2.0 %collective-permute-start = (f32[3,8,8,128]{3,2,1,0:T(8,128)}, f32[3,8,8,128]{3,2,1,0:T(8,128)S(1)}, u32[]{:S(2)}, u32[]{:S(2)}) collective-permute-start(f32[3,8,8,128]{3,2,1,0:T(8,128)} %mine.1), channel_id=1, source_target_pairs={{0,8},{1,9},{2,10},{3,11},{4,12},{5,13},{6,14},{7,15},{8,0},{9,1},... | collective-permute-start | bytes 294920 | tf_op jit(solution)/shard_map/ppermute | solution.py:457
  1.4 5.0 %collective-permute-start.1 = (f32[3,8,8,128]{3,2,1,0:T(8,128)}, f32[3,8,8,128]{3,2,1,0:T(8,128)S(1)}, u32[]{:S(2)}, u32[]{:S(2)}) collective-permute-start(f32[3,8,8,128]{3,2,1,0:T(8,128)} %mine.1), channel_id=1, source_target_pairs={{0,16},{1,17},{2,18},{3,19},{4,20},{5,21},{6,22},{7,23},{8,24},{9,... | collective-permute-start | bytes 294920 | tf_op jit(solution)/shard_map/ppermute | solution.py:457
  2.6 0.9 %copy-start = (f32[3,8,8,128]{3,2,1,0:T(8,128)S(1)}, f32[3,8,8,128]{3,2,1,0:T(8,128)}, u32[]{:S(2)}) copy-start(f32[3,8,8,128]{3,2,1,0:T(8,128)} %mine.1) | copy-start | bytes 294916
  3.7 3.2 %copy-start.1 = (s32[8]{0:T(128)S(1)}, s32[8]{0:T(128)}, u32[]{:S(2)}) copy-start(s32[8]{0:T(128)} %layer_map.1) | copy-start | bytes 100
  3.7 4.6 %collective-permute-start.3 = (f32[6,8,128]{2,1,0:T(8,128)S(1)}, f32[6,8,128]{2,1,0:T(8,128)S(1)}, u32[]{:S(2)}, u32[]{:S(2)}) collective-permute-start(f32[6,8,128]{2,1,0:T(8,128)S(1)} %get-tuple-element.8), channel_id=1, source_target_pairs={{0,24},{1,16},{2,17},{3,18},{4,19},{5,20},{6,21},{7,22},{8,25},{9,... | collective-permute-start | bytes 73736 | tf_op jit(solution)/shard_map/ppermute | solution.py:457
  5.8 3.6 %collective-permute-start.4 = (f32[6,8,128]{2,1,0:T(8,128)S(1)}, f32[6,8,128]{2,1,0:T(8,128)S(1)}, u32[]{:S(2)}, u32[]{:S(2)}) collective-permute-start(f32[6,8,128]{2,1,0:T(8,128)S(1)} %get-tuple-element.8), channel_id=1, source_target_pairs={{0,8},{1,0},{2,1},{3,2},{4,3},{5,4},{6,5},{7,6},{8,9},{9,10},{10,1... | collective-permute-start | bytes 73736 | tf_op jit(solution)/shard_map/ppermute | solution.py:457
  6.3 4.0 %collective-permute-start.2 = (f32[3,8,8,128]{3,2,1,0:T(8,128)S(1)}, f32[3,8,8,128]{3,2,1,0:T(8,128)S(1)}, u32[]{:S(2)}, u32[]{:S(2)}) collective-permute-start(f32[3,8,8,128]{3,2,1,0:T(8,128)S(1)} %collective-permute-done.1.up_mine.down_mine), channel_id=1, source_target_pairs={{0,8},{1,9},{2,10},{3,11},{4,12},{5,13},{6,14},{7,15},{8,0},{9,1},... | collective-permute-start | bytes 294920 | tf_op jit(solution)/shard_map/ppermute | solution.py:457
  9.4 2.1 %collective-permute-start.5 = (f32[15,8,128]{2,1,0:T(8,128)S(1)}, f32[15,8,128]{2,1,0:T(8,128)S(1)}, u32[]{:S(2)}, u32[]{:S(2)}) collective-permute-start(f32[15,8,128]{2,1,0:T(8,128)S(1)} %shard_map.44.mine), channel_id=1, source_target_pairs={{0,8},{1,9},{2,10},{3,11},{4,12},{5,13},{6,14},{7,15},{8,0},{9,1},... | collective-permute-start | bytes 184328 | tf_op jit(solution)/shard_map/ppermute | solution.py:457

commit v5 on v4

--- a/solution.py
+++ b/solution.py
@@ -17,6 +17,7 @@
 LOW = SWEEPS
 HIGH = SWEEPS + 1
 RIGHT = BXY + HIGH
+FIRST, LAST = -LOW, 2 * BXY + HIGH - 1
 START = RIGHT + LOW
 
 
@@ -251,33 +252,40 @@
     return parts
 
 
-def sum_columns(sums, columns):
-    value = jnp.concatenate(sums, axis=0)
+def reduce_sums(sums, masks, columns):
+    depth = sums[0].shape[0]
+    at = lax.broadcasted_iota(jnp.int32, sums[0].shape, 0)
+    per = depth // NCL
+    rows = []
+    for first in range(0, len(sums), per):
+        value = None
+        for n, total in enumerate(sums[first : first + per]):
+            for layer in range(NCL):
+                part = total * masks[layer]
+                shift = depth // 2
+                while shift:
+                    part = part + pltpu.roll(part, shift, 0)
+                    shift //= 2
+                place_at = n * NCL + layer
+                value = part if value is None else jnp.where(at < place_at, value, part)
+        rows.append(value)
+    value = jnp.concatenate(rows, axis=0)
     count = value.shape[0]
     parts = jnp.dot(
         jnp.concatenate(thirds(value), axis=0),
-        columns.astype(jnp.bfloat16),
+        columns,
         preferred_element_type=jnp.float32,
     )
     return parts[:count] + parts[count : 2 * count] + parts[2 * count :]
 
 
-def sum_layers(picks, value):
-    return jnp.dot(
-        jnp.concatenate([picks.astype(jnp.bfloat16)] * 3, axis=1),
-        jnp.concatenate(thirds(value), axis=0),
-        preferred_element_type=jnp.float32,
-    )
-
-
-def picks_kernel(layer_map, out):
-    depth = out.shape[1] // (out.shape[0] // NCL)
-    r = lax.broadcasted_iota(jnp.int32, out.shape, 0)
-    c = lax.broadcasted_iota(jnp.int32, out.shape, 1)
-    layer = jnp.zeros(out.shape, jnp.int32)
-    for z in range(depth):
-        layer = jnp.where(c % depth == z, layer_map[z], layer)
-    out[...] = ((r // NCL == c // depth) & (r % NCL == layer)).astype(jnp.float32)
+def masks_kernel(layer_map, out):
+    layer = lax.broadcasted_iota(jnp.int32, out.shape[1:], 0)
+    held = jnp.zeros(out.shape[1:], jnp.int32)
+    for z in range(out.shape[1]):
+        held = jnp.where(layer == z, layer_map[z], held)
+    for coarse in range(out.shape[0]):
+        out[coarse] = jnp.where(held == coarse, 1.0, 0.0)
 
 
 def place(axes):
@@ -294,12 +302,25 @@
     return [(comp, row) for row in range(width) for comp in range(3)]
 
 
-def table_kernel(out):
-    lanes = out.shape[0]
-    r = lax.broadcasted_iota(jnp.int32, out.shape, 0)
-    c = lax.broadcasted_iota(jnp.int32, out.shape, 1)
-    inner = (r // BXY == c) & (c > 0) & (c < lanes // BXY - 1)
-    out[...] = inner.astype(jnp.float32)
+def table_kernel(inside, edges):
+    _, _, _, (has_left, has_right) = place(("gx", "gy"))
+    lanes = inside.shape[0]
+    count, half, start = lanes // BXY, lanes // 2, START
+    r = lax.broadcasted_iota(jnp.int32, inside.shape, 0)
+    c = lax.broadcasted_iota(jnp.int32, inside.shape, 1)
+    inner = (r // BXY == c) & (c > 0) & (c < count - 1)
+    inside[...] = jnp.where(inner, 1.0, 0.0).astype(jnp.bfloat16)
+
+    def span(begin):
+        return (r >= begin) & (r < begin + BXY)
+
+    first = jnp.where(span(start), 1.0, 0.0) + jnp.where(span(half + start), has_left, 0.0)
+    final = jnp.where(span(lanes - BXY), 1.0, 0.0) + jnp.where(span(half - BXY), has_right, 0.0)
+    beyond = jnp.where(span(0) | span(half), has_right, 0.0)
+    columns = jnp.where(
+        c == 0, first, jnp.where(c == count - 1, final, jnp.where(c == count, beyond, 0.0))
+    )
+    edges[...] = columns.astype(jnp.bfloat16)
 
 
 def pack_kernel(mine, other, pair, packed):
@@ -322,10 +343,35 @@
 
 
 def join_kernel(below, beside, above, out):
+    core, _, (has_down, has_up), (has_left, has_right) = place(("gx", "gy"))
+    side = jnp.where(core == 0, has_right, has_left)
     half = beside.shape[0] // 2
-    out[:half] = below[half:]
-    out[half : 3 * half] = beside[...]
-    out[3 * half :] = above[...]
+    out[:half] = 1.0 / (below[half:] * (side * has_down) + KMIN)
+    out[half : 3 * half] = 1.0 / (beside[...] * side + KMIN)
+    out[3 * half :] = 1.0 / (above[...] * (side * has_up) + KMIN)
+
+
+def needed():
+    return [(row, comp) for row in range(FIRST, LAST + 1) for comp in range(1 if row in (FIRST, LAST) else 3)]
+
+
+def with_strips(core, strips, of, width, shape):
+    lanes = shape[-1]
+    lane = lanes_of(shape)
+    begin, end = of * RIGHT, RIGHT + of * LOW
+    near = (lane >= begin) & (lane < end)
+    far = (lane >= lanes // 2 + begin) & (lane < lanes // 2 + end)
+    per, per_tile = lanes // RIGHT, strips.shape[0] // 5
+    index = {key: at for at, key in enumerate(slots(width))}
+
+    def put(row, comp, value):
+        at = index[comp, row % width]
+        strip = strips[(core + 1 + row // width) * per_tile + at // per]
+        shift = -RIGHT * (at % per) % lanes
+        value = jnp.where(far, pltpu.roll(strip, (shift + lanes // 2) % lanes, 1), value)
+        return jnp.where(near, pltpu.roll(strip, shift, 1) if shift else strip, value)
+
+    return put
 
 
 def stack_kernel(pair, up_mine, up_other, down_mine, down_other, stack, placed):
@@ -359,66 +405,33 @@
                 put(row - width, comp, jnp.where(first, other, mine) * has_down)
 
 
-def main_kernel(columns, stack, out, scratch):
+def main_kernel(columns, masks, stack, placed, mine, out, rows, scratch):
     core, present, _, _ = place(("gx", "gy"))
     base = LOW + core * BXY
     solver = Solver(lambda comp, row: stack[base + row, comp], scratch, None, None)
-    out[...] = sum_columns(accumulate(solver, present), columns[...])
-
-
-def edge_kernel(picks, placed, mine, other, inner, perm_out, trans_out, scratch):
-    core, present, _, (has_left, has_right) = place(("gx", "gy"))
-    depth, lanes = placed.shape[2:]
+    out[...] = reduce_sums(accumulate(solver, present), masks, columns[...])
+    put = with_strips(core, mine, core, BXY, placed.shape[2:])
+    for row, comp in needed():
+        rows[row - FIRST, comp] = put(row, comp, placed[base + row, comp])
+
+
+def edge_kernel(columns, masks, rows, other, inner, perm_out, trans_out, scratch):
+    core, present, _, _ = place(("gx", "gy"))
+    depth, lanes = rows.shape[2:]
     width = BXY
-    per = lanes // RIGHT
     lane = lanes_of((depth, lanes))
     half, start = lanes // 2, START
-    first = core == 0
-    low, high, high2 = present
-    kept = {-1: low, 0: 1.0, 1: high, 2: high2}
-    per_tile = mine.shape[0] // 5
-    index = {key: at for at, key in enumerate(slots(width))}
-    turned = (lane >= half) & (lane < half + START)
-    strips = {}
-
-    def strip(tile, n):
-        if (tile, n) not in strips:
-            at = (core + 1 + tile) * per_tile + n
-            a, b = mine[at], other[at]
-            strips[tile, n] = tuple(
-                1.0 / (value * (kept[tile] * there) + KMIN)
-                for value, there in ((jnp.where(first, a, b), has_right), (jnp.where(first, b, a), has_left))
-            )
-        return strips[tile, n]
-
-    base = LOW + core * width
+    put = with_strips(core, other, 1 - core, width, (depth, lanes))
 
     def inverse(comp, row):
-        at = index[comp, row % width]
-        shift = -RIGHT * (at % per) % lanes
-        right, left = (pltpu.roll(v, shift, 1) if shift else v for v in strip(row // width, at // per))
-        theirs = jnp.where(lane < RIGHT, right, left)
-        value = jnp.where(turned, pltpu.roll(theirs, half, 1), placed[base + row, comp])
-        return jnp.where(lane < START, theirs, value)
+        return put(row, comp, rows[row - FIRST, comp])
 
     y_ends = (lane == BXY - 1) | (lane == half + start + BXY - 1)
     y_starts = lane == half - BXY
     solver = Solver(inverse, scratch, y_ends, y_starts)
     sums = accumulate(solver, present)
-    r = lax.broadcasted_iota(jnp.int32, (lanes, lanes), 0)
-    c = lax.broadcasted_iota(jnp.int32, (lanes, lanes), 1)
     count = lanes // BXY
-
-    def span(begin):
-        return (r >= begin) & (r < begin + BXY)
-
-    first = jnp.where(span(start), 1.0, 0.0) + jnp.where(span(half + start), has_left, 0.0)
-    final = jnp.where(span(lanes - BXY), 1.0, 0.0) + jnp.where(span(half - BXY), has_right, 0.0)
-    beyond = jnp.where(span(0) | span(half), has_right, 0.0)
-    columns = jnp.where(
-        c == 0, first, jnp.where(c == count - 1, final, jnp.where(c == count, beyond, 0.0))
-    )
-    total = sum_layers(picks[...], inner[...] + sum_columns(sums, columns))
+    total = inner[...] + reduce_sums(sums, masks, columns[...])
     cells = (width + 2 * BXY, lanes + 2 * BXY, depth)
     energy = [total[2 * NCL * q : 2 * NCL * q + NCL] for q in range(4)]
     square = [total[2 * NCL * q + NCL : 2 * NCL * (q + 1)] for q in range(4)]
@@ -483,10 +496,10 @@
     held = lambda value: pltpu.with_memory_space_constraint(value, pltpu.VMEM)
     strips = -(-len(slots(width)) // (lanes // RIGHT))
 
-    columns = pl.pallas_call(
+    inside, edges = pl.pallas_call(
         table_kernel,
-        out_shape=pltpu.VMEM((lanes, lanes), jnp.float32),
-        out_specs=vmem,
+        out_shape=[pltpu.VMEM((lanes, lanes), jnp.bfloat16)] * 2,
+        out_specs=[vmem] * 2,
         compiler_params=limit,
         cost_estimate=pl.CostEstimate(flops=LONG, bytes_accessed=lanes * lanes * 4, transcendentals=0),
     )()
@@ -505,9 +518,9 @@
     above, below = net.sideways(packed, 1), net.sideways(packed, -1)
     beside = net.sideways(packed, 0)
     up_other, down_other = net.swap(up), net.swap(down)
-    picks = pl.pallas_call(
-        picks_kernel,
-        out_shape=pltpu.VMEM((8 * NCL, 8 * depth), jnp.float32),
+    masks = pl.pallas_call(
+        masks_kernel,
+        out_shape=pltpu.VMEM((NCL, depth, lanes), jnp.float32),
         in_specs=[smem],
         out_specs=vmem,
         compiler_params=limit,
@@ -522,15 +535,6 @@
         compiler_params=limit,
         cost_estimate=pl.CostEstimate(flops=LONG, bytes_accessed=4 * permeability.size * 4, transcendentals=0),
     )(held(pair), held(up), held(up_other), held(down), held(down_other))
-    inner = pl.pallas_call(
-        main_kernel,
-        out_shape=pltpu.VMEM((8 * depth, lanes), jnp.float32),
-        in_specs=[vmem] * 2,
-        out_specs=vmem,
-        scratch_shapes=[scratch],
-        compiler_params=limit,
-        cost_estimate=pl.CostEstimate(flops=LONG, bytes_accessed=4 * permeability.size * 4, transcendentals=0),
-    )(held(columns), held(stack))
     joined = pl.pallas_call(
         join_kernel,
         out_shape=pltpu.VMEM((5 * strips, depth, lanes), jnp.float32),
@@ -539,6 +543,18 @@
         compiler_params=limit,
     )(held(below), held(beside), held(above))
     theirs = net.swap(joined)
+    inner, near = pl.pallas_call(
+        main_kernel,
+        out_shape=[
+            pltpu.VMEM((8 * NCL, lanes), jnp.float32),
+            pltpu.VMEM((LAST + 1 - FIRST, 3, depth, lanes), jnp.float32),
+        ],
+        in_specs=[vmem] * 5,
+        out_specs=[vmem] * 2,
+        scratch_shapes=[scratch],
+        compiler_params=limit,
+        cost_estimate=pl.CostEstimate(flops=LONG, bytes_accessed=4 * permeability.size * 4, transcendentals=0),
+    )(held(inside), held(masks), held(stack), held(placed), held(joined))
     out = jax.ShapeDtypeStruct((3, NCL, width // BXY, lanes // BXY), jnp.float32)
     return pl.pallas_call(
         edge_kernel,
@@ -547,7 +563,7 @@
         out_specs=(vmem, vmem),
         scratch_shapes=[scratch],
         compiler_params=limit,
-    )(held(picks), held(placed), held(joined), held(theirs), held(inner))
+    )(held(edges), held(masks), held(near), held(theirs), held(inner))
 
 
 def solution(mesh):

time: 13.5 us -> 13.4 us (level)
    pallas_call x1, Pallas kernels: 1.8 us -> 1.61 us  [local(): pl.pallas_call(edge_kernel, out_shape=(out, out), in_specs=[vmem] * 5, ou...]
  transfers between devices with their start and end apart: 6 -> 6, of which waited for: 2 -> 2; matrix products, arithmetic and copies ran while one was open for 0% -> 0% of each run, Pallas kernels for 14% -> 15%
where the time goes in v5:
time: 13.4 us; the launch traced here: 13.3 us
  starting transfers between devices  6.15 us (46%)
  Pallas kernels  3.56 us (27%)
  waiting for transfers between devices  1.95 us (15%)
  local copies, waits for them, and re-layouts  0.93 us (7%)
  between operations  0.69 us (5%)
    ppermute x6, starting transfers between devices, permute(): self.sent[key] = (value, lax.ppermute(value, self.axes, pairs))  6.15 us
    ppermute x6, waiting for transfers between devices, permute(): self.sent[key] = (value, lax.ppermute(value, self.axes, pairs))  1.95 us
    pallas_call x1, Pallas kernels, local(): pl.pallas_call(edge_kernel, out_shape=(out, out), in_specs=[vmem] * 5, ou...  1.61 us
    unnamed x4, local copies, waits for them, and re-layouts  0.93 us
    pallas_call x1, Pallas kernels, local(): pl.pallas_call(main_kernel, out_shape=[pltpu.VMEM((8 * NCL, lanes), jnp.f...  0.85 us
    pallas_call x1, Pallas kernels, local(): pl.pallas_call(masks_kernel, out_shape=pltpu.VMEM((NCL, depth, lanes), jn...  0.55 us
    pallas_call x1, Pallas kernels, local(): pl.pallas_call(stack_kernel, out_shape=[pltpu.VMEM((rows, 3, depth, lanes...  0.38 us
  transfers between devices with their start and end apart: 6, of which 2 were waited for; matrix products, arithmetic and copies ran while one was open for 0% of the time, Pallas kernels for 15%

profile of v5, /device:TPU:25, one launch (start us, length us, event | category | flops | bytes accessed | tf_op | source)
XLA Modules:
  0.0 13.3 jit_solution(13979053677547569936)
XLA Ops:
  0.6 0.7 %collective-permute-start = (f32[3,8,8,128]{3,2,1,0:T(8,128)}, f32[3,8,8,128]{3,2,1,0:T(8,128)S(1)}, u32[]{:S(2)}, u32[]{:S(2)}) collective-permute-start(f32[3,8,8,128]{3,2,1,0:T(8,128)} %mine.1), channel_id=1, source_target_pairs={{0,8},{1,9},{2,10},{3,11},{4,12},{5,13},{6,14},{7,15},{8,0},{9,1},... | collective-permute-start | bytes 294920 | tf_op jit(solution)/shard_map/ppermute | solution.py:470
  1.4 1.2 %collective-permute-start.1 = (f32[3,8,8,128]{3,2,1,0:T(8,128)}, f32[3,8,8,128]{3,2,1,0:T(8,128)S(1)}, u32[]{:S(2)}, u32[]{:S(2)}) collective-permute-start(f32[3,8,8,128]{3,2,1,0:T(8,128)} %mine.1), channel_id=1, source_target_pairs={{0,16},{1,17},{2,18},{3,19},{4,20},{5,21},{6,22},{7,23},{8,24},{9,... | collective-permute-start | bytes 294920 | tf_op jit(solution)/shard_map/ppermute | solution.py:470
  2.6 0.0 collective-permute-done.other
  2.6 0.0 copy-start
  2.6 0.9 %copy-done = f32[3,8,8,128]{3,2,1,0:T(8,128)S(1)} copy-done((f32[3,8,8,128]{3,2,1,0:T(8,128)S(1)}, f32[3,8,8,128]{3,2,1,0:T(8,128)}, u32[]{:S(2)}) %copy-start) | copy-done | bytes 98328
  3.5 0.1 shard_map.43
  3.7 0.0 copy-start.1
  3.7 2.1 %collective-permute-start.3 = (f32[6,8,128]{2,1,0:T(8,128)S(1)}, f32[6,8,128]{2,1,0:T(8,128)S(1)}, u32[]{:S(2)}, u32[]{:S(2)}) collective-permute-start(f32[6,8,128]{2,1,0:T(8,128)S(1)} %get-tuple-element.15), channel_id=1, source_target_pairs={{0,24},{1,16},{2,17},{3,18},{4,19},{5,20},{6,21},{7,22},{8,25},{9,... | collective-permute-start | bytes 73736 | tf_op jit(solution)/shard_map/ppermute | solution.py:470
  5.8 0.5 %collective-permute-start.4 = (f32[6,8,128]{2,1,0:T(8,128)S(1)}, f32[6,8,128]{2,1,0:T(8,128)S(1)}, u32[]{:S(2)}, u32[]{:S(2)}) collective-permute-start(f32[6,8,128]{2,1,0:T(8,128)S(1)} %get-tuple-element.15), channel_id=1, source_target_pairs={{0,8},{1,0},{2,1},{3,2},{4,3},{5,4},{6,5},{7,6},{8,9},{9,10},{10,1... | collective-permute-start | bytes 73736 | tf_op jit(solution)/shard_map/ppermute | solution.py:470
  6.3 0.0 collective-permute-done.1.up_mine.down_mine
  6.3 0.5 %collective-permute-start.2 = (f32[3,8,8,128]{3,2,1,0:T(8,128)S(1)}, f32[3,8,8,128]{3,2,1,0:T(8,128)S(1)}, u32[]{:S(2)}, u32[]{:S(2)}) collective-permute-start(f32[3,8,8,128]{3,2,1,0:T(8,128)S(1)} %collective-permute-done.1.up_mine.down_mine), channel_id=1, source_target_pairs={{0,8},{1,9},{2,10},{3,11},{4,12},{5,13},{6,14},{7,15},{8,0},{9,1},... | collective-permute-start | bytes 294920 | tf_op jit(solution)/shard_map/ppermute | solution.py:470
  6.9 0.0 copy-done.1
  6.9 0.6 %shard_map.42.masks = f32[4,8,128]{2,1,0:T(8,128)S(1)} custom-call(s32[8]{0:T(128)S(1)} %copy-done.1), custom_call_target="tpu_custom_call" | custom-call | tf_op jit(solution)/shard_map/pallas_call | solution.py:521
  7.4 0.9 %collective-permute-done.3.below.above = f32[6,8,128]{2,1,0:T(8,128)S(1)} collective-permute-done((f32[6,8,128]{2,1,0:T(8,128)S(1)}, f32[6,8,128]{2,1,0:T(8,128)S(1)}, u32[]{:S(2)}, u32[]{:S(2)}) %collective-permute-start.3) | collective-permute-done | bytes 24608 | tf_op jit(solution)/shard_map/ppermute | solution.py:470
  8.3 1.1 %collective-permute-done.4.beside = f32[6,8,128]{2,1,0:T(8,128)S(1)} collective-permute-done((f32[6,8,128]{2,1,0:T(8,128)S(1)}, f32[6,8,128]{2,1,0:T(8,128)S(1)}, u32[]{:S(2)}, u32[]{:S(2)}) %collective-permute-start.4) | collective-permute-done | bytes 24608 | tf_op jit(solution)/shard_map/ppermute | solution.py:470
  9.4 1.0 %collective-permute-start.5 = (f32[15,8,128]{2,1,0:T(8,128)S(1)}, f32[15,8,128]{2,1,0:T(8,128)S(1)}, u32[]{:S(2)}, u32[]{:S(2)}) collective-permute-start(f32[15,8,128]{2,1,0:T(8,128)S(1)} %shard_map.45.mine), channel_id=1, source_target_pairs={{0,8},{1,9},{2,10},{3,11},{4,12},{5,13},{6,14},{7,15},{8,0},{9,1},... | collective-permute-start | bytes 184328 | tf_op jit(solution)/shard_map/ppermute | solution.py:470
  10.4 0.0 collective-permute-done.2.up_other.down_other
  10.4 0.4 %shard_map.44 = (f32[33,3,8,128]{3,2,1,0:T(8,128)S(1)}, f32[33,3,8,128]{3,2,1,0:T(8,128)S(1)}) custom-call(f32[16,3,8,128]{3,2,1,0:T(8,128)S(1)} %get-tuple-element.12.pair, f32[3,8,8,128]{3,2,1,0:T(8,128)S(1)} %collective-permute-done.1.up_mine.down_mine, f32[3,8,8,128]{3,2,1,0:T(8,128)S(1)} %collective-permute-done.2.up_other.down_other, ...), custom_call_target="tpu_custom_call" | custom-call | flops 10000000000 | bytes 393216 | tf_op jit(solution)/shard_map/pallas_call | solution.py:530
  10.8 0.9 %shard_map.46 = (f32[32,128]{1,0:T(8,128)S(1)}, f32[25,3,8,128]{3,2,1,0:T(8,128)S(1)}) custom-call(bf16[128,128]{1,0:T(8,128)(2,1)S(1)} %get-tuple-element.11.columns, f32[4,8,128]{2,1,0:T(8,128)S(1)} %shard_map.42.masks, f32[33,3,8,128]{3,2,1,0:T(8,128)S(1)} %get-tuple-element.13.stack, f32[33,3,8,128]{3,2,1,0:T(8,128)S(1)} %get-tuple-element.14.placed, ...), custom_call_target="tpu_custom_call" | custom-call | flops 10000000000 | bytes 393216 | tf_op jit(solution)/shard_map/pallas_call | solution.py:546
  11.7 0.0 collective-permute-done.5.other
  11.7 1.6 %shard_map.47 = (f32[3,4,1,16]{3,2,1,0:T(1,128)}, f32[3,4,1,16]{3,2,1,0:T(1,128)}) custom-call(bf16[128,128]{1,0:T(8,128)(2,1)S(1)} %get-tuple-element.10.columns, f32[4,8,128]{2,1,0:T(8,128)S(1)} %shard_map.42.masks, f32[25,3,8,128]{3,2,1,0:T(8,128)S(1)} %get-tuple-element.16.rows, f32[15,8,128]{2,1,0:T(8,128)S(1)} %collective-permute-done.5.other, ...), custom_call_target="tpu_custom_call" | custom-call | tf_op jit(solution)/shard_map/pallas_call | solution.py:559
  (2 shorter events, 0.0 us)
Async XLA Ops:
  0.6 2.0 %collective-permute-start = (f32[3,8,8,128]{3,2,1,0:T(8,128)}, f32[3,8,8,128]{3,2,1,0:T(8,128)S(1)}, u32[]{:S(2)}, u32[]{:S(2)}) collective-permute-start(f32[3,8,8,128]{3,2,1,0:T(8,128)} %mine.1), channel_id=1, source_target_pairs={{0,8},{1,9},{2,10},{3,11},{4,12},{5,13},{6,14},{7,15},{8,0},{9,1},... | collective-permute-start | bytes 294920 | tf_op jit(solution)/shard_map/ppermute | solution.py:470
  1.4 5.0 %collective-permute-start.1 = (f32[3,8,8,128]{3,2,1,0:T(8,128)}, f32[3,8,8,128]{3,2,1,0:T(8,128)S(1)}, u32[]{:S(2)}, u32[]{:S(2)}) collective-permute-start(f32[3,8,8,128]{3,2,1,0:T(8,128)} %mine.1), channel_id=1, source_target_pairs={{0,16},{1,17},{2,18},{3,19},{4,20},{5,21},{6,22},{7,23},{8,24},{9,... | collective-permute-start | bytes 294920 | tf_op jit(solution)/shard_map/ppermute | solution.py:470
  2.6 0.9 %copy-start = (f32[3,8,8,128]{3,2,1,0:T(8,128)S(1)}, f32[3,8,8,128]{3,2,1,0:T(8,128)}, u32[]{:S(2)}) copy-start(f32[3,8,8,128]{3,2,1,0:T(8,128)} %mine.1) | copy-start | bytes 294916
  3.7 3.2 %copy-start.1 = (s32[8]{0:T(128)S(1)}, s32[8]{0:T(128)}, u32[]{:S(2)}) copy-start(s32[8]{0:T(128)} %layer_map.1) | copy-start | bytes 100
  3.7 4.6 %collective-permute-start.3 = (f32[6,8,128]{2,1,0:T(8,128)S(1)}, f32[6,8,128]{2,1,0:T(8,128)S(1)}, u32[]{:S(2)}, u32[]{:S(2)}) collective-permute-start(f32[6,8,128]{2,1,0:T(8,128)S(1)} %get-tuple-element.15), channel_id=1, source_target_pairs={{0,24},{1,16},{2,17},{3,18},{4,19},{5,20},{6,21},{7,22},{8,25},{9,... | collective-permute-start | bytes 73736 | tf_op jit(solution)/shard_map/ppermute | solution.py:470
  5.8 3.6 %collective-permute-start.4 = (f32[6,8,128]{2,1,0:T(8,128)S(1)}, f32[6,8,128]{2,1,0:T(8,128)S(1)}, u32[]{:S(2)}, u32[]{:S(2)}) collective-permute-start(f32[6,8,128]{2,1,0:T(8,128)S(1)} %get-tuple-element.15), channel_id=1, source_target_pairs={{0,8},{1,0},{2,1},{3,2},{4,3},{5,4},{6,5},{7,6},{8,9},{9,10},{10,1... | collective-permute-start | bytes 73736 | tf_op jit(solution)/shard_map/ppermute | solution.py:470
  6.3 4.1 %collective-permute-start.2 = (f32[3,8,8,128]{3,2,1,0:T(8,128)S(1)}, f32[3,8,8,128]{3,2,1,0:T(8,128)S(1)}, u32[]{:S(2)}, u32[]{:S(2)}) collective-permute-start(f32[3,8,8,128]{3,2,1,0:T(8,128)S(1)} %collective-permute-done.1.up_mine.down_mine), channel_id=1, source_target_pairs={{0,8},{1,9},{2,10},{3,11},{4,12},{5,13},{6,14},{7,15},{8,0},{9,1},... | collective-permute-start | bytes 294920 | tf_op jit(solution)/shard_map/ppermute | solution.py:470
  9.4 2.2 %collective-permute-start.5 = (f32[15,8,128]{2,1,0:T(8,128)S(1)}, f32[15,8,128]{2,1,0:T(8,128)S(1)}, u32[]{:S(2)}, u32[]{:S(2)}) collective-permute-start(f32[15,8,128]{2,1,0:T(8,128)S(1)} %shard_map.45.mine), channel_id=1, source_target_pairs={{0,8},{1,9},{2,10},{3,11},{4,12},{5,13},{6,14},{7,15},{8,0},{9,1},... | collective-permute-start | bytes 184328 | tf_op jit(solution)/shard_map/ppermute | solution.py:470

commit v6 on v5

--- a/solution.py
+++ b/solution.py
@@ -30,7 +30,22 @@
 WEIGHTS = sweep_weights(SWEEPS)
 
 
-SCALES = [math.prod(WEIGHTS[: s + 1]) for s in range(SWEEPS)]
+def sweep_polynomial(weights):
+    left = [1.0]
+    for w in weights:
+        grown = [0.0] * (len(left) + 1)
+        for i, value in enumerate(left):
+            grown[i] += (1.0 - w) * value
+            grown[i + 1] += w * value
+        left = grown
+    total, out = 1.0, []
+    for value in left[:-1]:
+        total -= value
+        out.append(total)
+    return out
+
+
+POLYNOMIAL = sweep_polynomial(WEIGHTS)
 
 
 def harmonic(left, right):
@@ -166,11 +181,7 @@
         def make():
             a = lambda which: self.weight(which, row, edge)
             here = self.pressure(d, count - 1, row, boundary)
-            w = WEIGHTS[count - 1]
-            if count == 2:
-                total = ((1.0 - w) / w + 1.0 / SCALES[0]) * here
-            else:
-                total = ((1.0 - w) / w) * here + (1.0 / SCALES[count - 2]) * self.drive(d, row, edge)
+            total = (POLYNOMIAL[SWEEPS - count] / POLYNOMIAL[-1]) * self.drive(d, row, edge)
             side = a(2) * up(here, 1) + a(3) * down(here, 1)
             layers = a(4) * up(here, 0) + a(5) * down(here, 0)
             if edge != "up":
@@ -201,7 +212,7 @@
             else:
                 face = self.z_faces(row)[0]
                 above = jnp.where(self.top, 0.0, up(here, 0))
-            drop = 1.0 / SCALES[-1] - here
+            drop = 1.0 / POLYNOMIAL[-1] - here
             if above is not None:
                 drop = drop + above
             square = drop * drop
@@ -234,7 +245,7 @@
     after = [(("up", 2 * BXY - 1), None), (None, None), (("low", BXY), high2)]
     jobs = [(d, 0, own) for d in range(3)] + [(0, BXY, after)]
     results = {}
-    order = [jobs[0], jobs[1], jobs[2], jobs[3]]
+    order = [jobs[1], jobs[2], jobs[0], jobs[3]]
     for row in range(BXY):
         for d, begin, patches in order:
             for boundary, _ in patches:
@@ -436,7 +447,7 @@
     energy = [total[2 * NCL * q : 2 * NCL * q + NCL] for q in range(4)]
     square = [total[2 * NCL * q + NCL : 2 * NCL * (q + 1)] for q in range(4)]
     perms = [
-        2.0 * energy[q] / (square[q] + EPS * (cells[d] / SCALES[-1]) ** 2)
+        2.0 * energy[q] / (square[q] + EPS * (cells[d] / POLYNOMIAL[-1]) ** 2)
         for q, d in enumerate((0, 1, 2, 0))
     ]
     layer = lax.broadcasted_iota(jnp.int32, perms[0].shape, 0)

time: 13.4 us -> 13.4 us (level)
  no operation moved by 1% of the time
where the time goes in v6:
time: 13.4 us; the launch traced here: 13.3 us
  starting transfers between devices  6.15 us (46%)
  Pallas kernels  3.55 us (26%)
  waiting for transfers between devices  1.95 us (15%)
  local copies, waits for them, and re-layouts  0.93 us (7%)
  between operations  0.69 us (5%)
    ppermute x6, starting transfers between devices, permute(): self.sent[key] = (value, lax.ppermute(value, self.axes, pairs))  6.15 us
    ppermute x6, waiting for transfers between devices, permute(): self.sent[key] = (value, lax.ppermute(value, self.axes, pairs))  1.95 us
    pallas_call x1, Pallas kernels, local(): pl.pallas_call(edge_kernel, out_shape=(out, out), in_specs=[vmem] * 5, ou...  1.61 us
    unnamed x4, local copies, waits for them, and re-layouts  0.93 us
    pallas_call x1, Pallas kernels, local(): pl.pallas_call(main_kernel, out_shape=[pltpu.VMEM((8 * NCL, lanes), jnp.f...  0.85 us
    pallas_call x1, Pallas kernels, local(): pl.pallas_call(masks_kernel, out_shape=pltpu.VMEM((NCL, depth, lanes), jn...  0.55 us
    pallas_call x1, Pallas kernels, local(): pl.pallas_call(stack_kernel, out_shape=[pltpu.VMEM((rows, 3, depth, lanes...  0.38 us
  transfers between devices with their start and end apart: 6, of which 2 were waited for; matrix products, arithmetic and copies ran while one was open for 0% of the time, Pallas kernels for 15%

profile of v6, /device:TPU:25, one launch (start us, length us, event | category | flops | bytes accessed | tf_op | source)
XLA Modules:
  0.0 13.3 jit_solution(14342986022294775175)
XLA Ops:
  0.6 0.7 %collective-permute-start = (f32[3,8,8,128]{3,2,1,0:T(8,128)}, f32[3,8,8,128]{3,2,1,0:T(8,128)S(1)}, u32[]{:S(2)}, u32[]{:S(2)}) collective-permute-start(f32[3,8,8,128]{3,2,1,0:T(8,128)} %mine.1), channel_id=1, source_target_pairs={{0,8},{1,9},{2,10},{3,11},{4,12},{5,13},{6,14},{7,15},{8,0},{9,1},... | collective-permute-start | bytes 294920 | tf_op jit(solution)/shard_map/ppermute | solution.py:481
  1.4 1.2 %collective-permute-start.1 = (f32[3,8,8,128]{3,2,1,0:T(8,128)}, f32[3,8,8,128]{3,2,1,0:T(8,128)S(1)}, u32[]{:S(2)}, u32[]{:S(2)}) collective-permute-start(f32[3,8,8,128]{3,2,1,0:T(8,128)} %mine.1), channel_id=1, source_target_pairs={{0,16},{1,17},{2,18},{3,19},{4,20},{5,21},{6,22},{7,23},{8,24},{9,... | collective-permute-start | bytes 294920 | tf_op jit(solution)/shard_map/ppermute | solution.py:481
  2.6 0.0 collective-permute-done.other
  2.6 0.0 copy-start
  2.6 0.9 %copy-done = f32[3,8,8,128]{3,2,1,0:T(8,128)S(1)} copy-done((f32[3,8,8,128]{3,2,1,0:T(8,128)S(1)}, f32[3,8,8,128]{3,2,1,0:T(8,128)}, u32[]{:S(2)}) %copy-start) | copy-done | bytes 98328
  3.5 0.1 shard_map.43
  3.7 0.0 copy-start.1
  3.7 2.1 %collective-permute-start.3 = (f32[6,8,128]{2,1,0:T(8,128)S(1)}, f32[6,8,128]{2,1,0:T(8,128)S(1)}, u32[]{:S(2)}, u32[]{:S(2)}) collective-permute-start(f32[6,8,128]{2,1,0:T(8,128)S(1)} %get-tuple-element.15), channel_id=1, source_target_pairs={{0,24},{1,16},{2,17},{3,18},{4,19},{5,20},{6,21},{7,22},{8,25},{9,... | collective-permute-start | bytes 73736 | tf_op jit(solution)/shard_map/ppermute | solution.py:481
  5.8 0.5 %collective-permute-start.4 = (f32[6,8,128]{2,1,0:T(8,128)S(1)}, f32[6,8,128]{2,1,0:T(8,128)S(1)}, u32[]{:S(2)}, u32[]{:S(2)}) collective-permute-start(f32[6,8,128]{2,1,0:T(8,128)S(1)} %get-tuple-element.15), channel_id=1, source_target_pairs={{0,8},{1,0},{2,1},{3,2},{4,3},{5,4},{6,5},{7,6},{8,9},{9,10},{10,1... | collective-permute-start | bytes 73736 | tf_op jit(solution)/shard_map/ppermute | solution.py:481
  6.3 0.0 collective-permute-done.1.up_mine.down_mine
  6.3 0.5 %collective-permute-start.2 = (f32[3,8,8,128]{3,2,1,0:T(8,128)S(1)}, f32[3,8,8,128]{3,2,1,0:T(8,128)S(1)}, u32[]{:S(2)}, u32[]{:S(2)}) collective-permute-start(f32[3,8,8,128]{3,2,1,0:T(8,128)S(1)} %collective-permute-done.1.up_mine.down_mine), channel_id=1, source_target_pairs={{0,8},{1,9},{2,10},{3,11},{4,12},{5,13},{6,14},{7,15},{8,0},{9,1},... | collective-permute-start | bytes 294920 | tf_op jit(solution)/shard_map/ppermute | solution.py:481
  6.9 0.0 copy-done.1
  6.9 0.6 %shard_map.42.masks = f32[4,8,128]{2,1,0:T(8,128)S(1)} custom-call(s32[8]{0:T(128)S(1)} %copy-done.1), custom_call_target="tpu_custom_call" | custom-call | tf_op jit(solution)/shard_map/pallas_call | solution.py:532
  7.4 0.9 %collective-permute-done.3.below.above = f32[6,8,128]{2,1,0:T(8,128)S(1)} collective-permute-done((f32[6,8,128]{2,1,0:T(8,128)S(1)}, f32[6,8,128]{2,1,0:T(8,128)S(1)}, u32[]{:S(2)}, u32[]{:S(2)}) %collective-permute-start.3) | collective-permute-done | bytes 24608 | tf_op jit(solution)/shard_map/ppermute | solution.py:481
  8.3 1.1 %collective-permute-done.4.beside = f32[6,8,128]{2,1,0:T(8,128)S(1)} collective-permute-done((f32[6,8,128]{2,1,0:T(8,128)S(1)}, f32[6,8,128]{2,1,0:T(8,128)S(1)}, u32[]{:S(2)}, u32[]{:S(2)}) %collective-permute-start.4) | collective-permute-done | bytes 24608 | tf_op jit(solution)/shard_map/ppermute | solution.py:481
  9.4 1.0 %collective-permute-start.5 = (f32[15,8,128]{2,1,0:T(8,128)S(1)}, f32[15,8,128]{2,1,0:T(8,128)S(1)}, u32[]{:S(2)}, u32[]{:S(2)}) collective-permute-start(f32[15,8,128]{2,1,0:T(8,128)S(1)} %shard_map.45.mine), channel_id=1, source_target_pairs={{0,8},{1,9},{2,10},{3,11},{4,12},{5,13},{6,14},{7,15},{8,0},{9,1},... | collective-permute-start | bytes 184328 | tf_op jit(solution)/shard_map/ppermute | solution.py:481
  10.4 0.0 collective-permute-done.2.up_other.down_other
  10.4 0.4 %shard_map.44 = (f32[33,3,8,128]{3,2,1,0:T(8,128)S(1)}, f32[33,3,8,128]{3,2,1,0:T(8,128)S(1)}) custom-call(f32[16,3,8,128]{3,2,1,0:T(8,128)S(1)} %get-tuple-element.12.pair, f32[3,8,8,128]{3,2,1,0:T(8,128)S(1)} %collective-permute-done.1.up_mine.down_mine, f32[3,8,8,128]{3,2,1,0:T(8,128)S(1)} %collective-permute-done.2.up_other.down_other, ...), custom_call_target="tpu_custom_call" | custom-call | flops 10000000000 | bytes 393216 | tf_op jit(solution)/shard_map/pallas_call | solution.py:541
  10.8 0.8 %shard_map.46 = (f32[32,128]{1,0:T(8,128)S(1)}, f32[25,3,8,128]{3,2,1,0:T(8,128)S(1)}) custom-call(bf16[128,128]{1,0:T(8,128)(2,1)S(1)} %get-tuple-element.11.columns, f32[4,8,128]{2,1,0:T(8,128)S(1)} %shard_map.42.masks, f32[33,3,8,128]{3,2,1,0:T(8,128)S(1)} %get-tuple-element.13.stack, f32[33,3,8,128]{3,2,1,0:T(8,128)S(1)} %get-tuple-element.14.placed, ...), custom_call_target="tpu_custom_call" | custom-call | flops 10000000000 | bytes 393216 | tf_op jit(solution)/shard_map/pallas_call | solution.py:557
  11.6 0.0 collective-permute-done.5.other
  11.7 1.6 %shard_map.47 = (f32[3,4,1,16]{3,2,1,0:T(1,128)}, f32[3,4,1,16]{3,2,1,0:T(1,128)}) custom-call(bf16[128,128]{1,0:T(8,128)(2,1)S(1)} %get-tuple-element.10.columns, f32[4,8,128]{2,1,0:T(8,128)S(1)} %shard_map.42.masks, f32[25,3,8,128]{3,2,1,0:T(8,128)S(1)} %get-tuple-element.16.rows, f32[15,8,128]{2,1,0:T(8,128)S(1)} %collective-permute-done.5.other, ...), custom_call_target="tpu_custom_call" | custom-call | tf_op jit(solution)/shard_map/pallas_call | solution.py:570
  (2 shorter events, 0.0 us)
Async XLA Ops:
  0.6 2.0 %collective-permute-start = (f32[3,8,8,128]{3,2,1,0:T(8,128)}, f32[3,8,8,128]{3,2,1,0:T(8,128)S(1)}, u32[]{:S(2)}, u32[]{:S(2)}) collective-permute-start(f32[3,8,8,128]{3,2,1,0:T(8,128)} %mine.1), channel_id=1, source_target_pairs={{0,8},{1,9},{2,10},{3,11},{4,12},{5,13},{6,14},{7,15},{8,0},{9,1},... | collective-permute-start | bytes 294920 | tf_op jit(solution)/shard_map/ppermute | solution.py:481
  1.4 5.0 %collective-permute-start.1 = (f32[3,8,8,128]{3,2,1,0:T(8,128)}, f32[3,8,8,128]{3,2,1,0:T(8,128)S(1)}, u32[]{:S(2)}, u32[]{:S(2)}) collective-permute-start(f32[3,8,8,128]{3,2,1,0:T(8,128)} %mine.1), channel_id=1, source_target_pairs={{0,16},{1,17},{2,18},{3,19},{4,20},{5,21},{6,22},{7,23},{8,24},{9,... | collective-permute-start | bytes 294920 | tf_op jit(solution)/shard_map/ppermute | solution.py:481
  2.6 0.9 %copy-start = (f32[3,8,8,128]{3,2,1,0:T(8,128)S(1)}, f32[3,8,8,128]{3,2,1,0:T(8,128)}, u32[]{:S(2)}) copy-start(f32[3,8,8,128]{3,2,1,0:T(8,128)} %mine.1) | copy-start | bytes 294916
  3.7 3.2 %copy-start.1 = (s32[8]{0:T(128)S(1)}, s32[8]{0:T(128)}, u32[]{:S(2)}) copy-start(s32[8]{0:T(128)} %layer_map.1) | copy-start | bytes 100
  3.7 4.6 %collective-permute-start.3 = (f32[6,8,128]{2,1,0:T(8,128)S(1)}, f32[6,8,128]{2,1,0:T(8,128)S(1)}, u32[]{:S(2)}, u32[]{:S(2)}) collective-permute-start(f32[6,8,128]{2,1,0:T(8,128)S(1)} %get-tuple-element.15), channel_id=1, source_target_pairs={{0,24},{1,16},{2,17},{3,18},{4,19},{5,20},{6,21},{7,22},{8,25},{9,... | collective-permute-start | bytes 73736 | tf_op jit(solution)/shard_map/ppermute | solution.py:481
  5.8 3.6 %collective-permute-start.4 = (f32[6,8,128]{2,1,0:T(8,128)S(1)}, f32[6,8,128]{2,1,0:T(8,128)S(1)}, u32[]{:S(2)}, u32[]{:S(2)}) collective-permute-start(f32[6,8,128]{2,1,0:T(8,128)S(1)} %get-tuple-element.15), channel_id=1, source_target_pairs={{0,8},{1,0},{2,1},{3,2},{4,3},{5,4},{6,5},{7,6},{8,9},{9,10},{10,1... | collective-permute-start | bytes 73736 | tf_op jit(solution)/shard_map/ppermute | solution.py:481
  6.3 4.1 %collective-permute-start.2 = (f32[3,8,8,128]{3,2,1,0:T(8,128)S(1)}, f32[3,8,8,128]{3,2,1,0:T(8,128)S(1)}, u32[]{:S(2)}, u32[]{:S(2)}) collective-permute-start(f32[3,8,8,128]{3,2,1,0:T(8,128)S(1)} %collective-permute-done.1.up_mine.down_mine), channel_id=1, source_target_pairs={{0,8},{1,9},{2,10},{3,11},{4,12},{5,13},{6,14},{7,15},{8,0},{9,1},... | collective-permute-start | bytes 294920 | tf_op jit(solution)/shard_map/ppermute | solution.py:481
  9.4 2.2 %collective-permute-start.5 = (f32[15,8,128]{2,1,0:T(8,128)S(1)}, f32[15,8,128]{2,1,0:T(8,128)S(1)}, u32[]{:S(2)}, u32[]{:S(2)}) collective-permute-start(f32[15,8,128]{2,1,0:T(8,128)S(1)} %shard_map.45.mine), channel_id=1, source_target_pairs={{0,8},{1,9},{2,10},{3,11},{4,12},{5,13},{6,14},{7,15},{8,0},{9,1},... | collective-permute-start | bytes 184328 | tf_op jit(solution)/shard_map/ppermute | solution.py:481

commit v7 on v6

--- a/solution.py
+++ b/solution.py
@@ -385,11 +385,8 @@
     return put
 
 
-def stack_kernel(pair, up_mine, up_other, down_mine, down_other, stack, placed):
-    core, _, (has_down, has_up), _ = place(("gx", "gy"))
-    width = up_mine.shape[2]
-    depth, lanes = pair.shape[2:]
-    first = core == 0
+def putter(stack, placed):
+    depth, lanes = stack.shape[2:]
     lane = lanes_of((depth, lanes))
     half, start = lanes // 2, START
     stop = start + BXY + HIGH
@@ -402,9 +399,21 @@
         value = jnp.where(near, pltpu.roll(value, start, 1), value)
         placed[LOW + row, comp] = jnp.where(second, pltpu.roll(value, half, 1), value)
 
-    for row in range(2 * width):
+    return put
+
+
+def within_kernel(pair, stack, placed):
+    put = putter(stack, placed)
+    for row in range(pair.shape[0]):
         for comp in range(3):
             put(row, comp, pair[row, comp])
+
+
+def stack_kernel(up_mine, up_other, down_mine, down_other, stack_in, placed_in, stack, placed):
+    core, _, (has_down, has_up), _ = place(("gx", "gy"))
+    width = up_mine.shape[2]
+    first = core == 0
+    put = putter(stack, placed)
     for row in range(width):
         for comp in range(3):
             mine, other = layers_of(up_mine, comp, row), layers_of(up_other, comp, row)
@@ -538,14 +547,23 @@
     )(layer_map)
     scratch = pltpu.VMEM((256, depth, lanes), jnp.float32)
     rows = LOW + 3 * width + HIGH
+    shapes = [pltpu.VMEM((rows, 3, depth, lanes), jnp.float32)] * 2
+    stack, placed = pl.pallas_call(
+        within_kernel,
+        out_shape=shapes,
+        in_specs=[vmem],
+        out_specs=[vmem] * 2,
+        compiler_params=limit,
+    )(held(pair))
     stack, placed = pl.pallas_call(
         stack_kernel,
-        out_shape=[pltpu.VMEM((rows, 3, depth, lanes), jnp.float32)] * 2,
-        in_specs=[vmem] * 5,
+        out_shape=shapes,
+        in_specs=[vmem] * 6,
         out_specs=[vmem] * 2,
+        input_output_aliases={4: 0, 5: 1},
         compiler_params=limit,
         cost_estimate=pl.CostEstimate(flops=LONG, bytes_accessed=4 * permeability.size * 4, transcendentals=0),
-    )(held(pair), held(up), held(up_other), held(down), held(down_other))
+    )(held(up), held(up_other), held(down), held(down_other), held(stack), held(placed))
     joined = pl.pallas_call(
         join_kernel,
         out_shape=pltpu.VMEM((5 * strips, depth, lanes), jnp.float32),

time: 13.4 us -> 13.3 us (level)
  waiting for transfers between devices: 1.95 us -> 1.74 us
    ppermute x6, waiting for transfers between devices: 1.95 us -> 1.74 us  [permute(): self.sent[key] = (value, lax.ppermute(value, self.axes, pairs))]
    pallas_call x1 -> x2, Pallas kernels: 0.38 us -> 0.44 us  [the longest x1 0.23 us: local(): pl.pallas_call(stack_kernel, out_shape=shapes, in_specs=[vmem] * 6, out_s...]
where the time goes in v7:
time: 13.3 us; the launch traced here: 13.1 us
  starting transfers between devices  6.15 us (46%)
  Pallas kernels  3.61 us (27%)
  waiting for transfers between devices  1.74 us (13%)
  local copies, waits for them, and re-layouts  0.93 us (7%)
  between operations  0.69 us (5%)
    ppermute x6, starting transfers between devices, permute(): self.sent[key] = (value, lax.ppermute(value, self.axes, pairs))  6.15 us
    ppermute x6, waiting for transfers between devices, permute(): self.sent[key] = (value, lax.ppermute(value, self.axes, pairs))  1.74 us
    pallas_call x1, Pallas kernels, local(): pl.pallas_call(edge_kernel, out_shape=(out, out), in_specs=[vmem] * 5, ou...  1.61 us
    unnamed x4, local copies, waits for them, and re-layouts  0.93 us
    pallas_call x1, Pallas kernels, local(): pl.pallas_call(main_kernel, out_shape=[pltpu.VMEM((8 * NCL, lanes), jnp.f...  0.85 us
    pallas_call x1, Pallas kernels, local(): pl.pallas_call(masks_kernel, out_shape=pltpu.VMEM((NCL, depth, lanes), jn...  0.55 us
  transfers between devices with their start and end apart: 6, of which 2 were waited for; matrix products, arithmetic and copies ran while one was open for 0% of the time, Pallas kernels for 15%

profile of v7, /device:TPU:25, one launch (start us, length us, event | category | flops | bytes accessed | tf_op | source)
XLA Modules:
  0.0 13.1 jit_solution(5377690457511320138)
XLA Ops:
  0.6 0.7 %collective-permute-start.2 = (f32[3,8,8,128]{3,2,1,0:T(8,128)}, f32[3,8,8,128]{3,2,1,0:T(8,128)S(1)}, u32[]{:S(2)}, u32[]{:S(2)}) collective-permute-start(f32[3,8,8,128]{3,2,1,0:T(8,128)} %mine.1), channel_id=1, source_target_pairs={{0,8},{1,9},{2,10},{3,11},{4,12},{5,13},{6,14},{7,15},{8,0},{9,1},... | collective-permute-start | bytes 294920 | tf_op jit(solution)/shard_map/ppermute | solution.py:490
  1.4 1.2 %collective-permute-start = (f32[3,8,8,128]{3,2,1,0:T(8,128)}, f32[3,8,8,128]{3,2,1,0:T(8,128)S(1)}, u32[]{:S(2)}, u32[]{:S(2)}) collective-permute-start(f32[3,8,8,128]{3,2,1,0:T(8,128)} %mine.1), channel_id=1, source_target_pairs={{0,16},{1,17},{2,18},{3,19},{4,20},{5,21},{6,22},{7,23},{8,24},{9,... | collective-permute-start | bytes 294920 | tf_op jit(solution)/shard_map/ppermute | solution.py:490
  2.6 0.0 collective-permute-done.2.other
  2.6 0.0 copy-start
  2.6 0.9 %copy-done = f32[3,8,8,128]{3,2,1,0:T(8,128)S(1)} copy-done((f32[3,8,8,128]{3,2,1,0:T(8,128)S(1)}, f32[3,8,8,128]{3,2,1,0:T(8,128)}, u32[]{:S(2)}) %copy-start) | copy-done | bytes 98328
  3.5 0.1 shard_map.43
  3.7 0.0 copy-start.1
  3.7 2.1 %collective-permute-start.3 = (f32[6,8,128]{2,1,0:T(8,128)S(1)}, f32[6,8,128]{2,1,0:T(8,128)S(1)}, u32[]{:S(2)}, u32[]{:S(2)}) collective-permute-start(f32[6,8,128]{2,1,0:T(8,128)S(1)} %get-tuple-element.19), channel_id=1, source_target_pairs={{0,24},{1,16},{2,17},{3,18},{4,19},{5,20},{6,21},{7,22},{8,25},{9,... | collective-permute-start | bytes 73736 | tf_op jit(solution)/shard_map/ppermute | solution.py:490
  5.8 0.5 %collective-permute-start.4 = (f32[6,8,128]{2,1,0:T(8,128)S(1)}, f32[6,8,128]{2,1,0:T(8,128)S(1)}, u32[]{:S(2)}, u32[]{:S(2)}) collective-permute-start(f32[6,8,128]{2,1,0:T(8,128)S(1)} %get-tuple-element.19), channel_id=1, source_target_pairs={{0,8},{1,0},{2,1},{3,2},{4,3},{5,4},{6,5},{7,6},{8,9},{9,10},{10,1... | collective-permute-start | bytes 73736 | tf_op jit(solution)/shard_map/ppermute | solution.py:490
  6.3 0.0 collective-permute-done.up_mine.down_mine
  6.3 0.5 %collective-permute-start.1 = (f32[3,8,8,128]{3,2,1,0:T(8,128)S(1)}, f32[3,8,8,128]{3,2,1,0:T(8,128)S(1)}, u32[]{:S(2)}, u32[]{:S(2)}) collective-permute-start(f32[3,8,8,128]{3,2,1,0:T(8,128)S(1)} %collective-permute-done.up_mine.down_mine), channel_id=1, source_target_pairs={{0,8},{1,9},{2,10},{3,11},{4,12},{5,13},{6,14},{7,15},{8,0},{9,1},... | collective-permute-start | bytes 294920 | tf_op jit(solution)/shard_map/ppermute | solution.py:490
  6.9 0.0 copy-done.1
  6.9 0.6 %shard_map.42.masks = f32[4,8,128]{2,1,0:T(8,128)S(1)} custom-call(s32[8]{0:T(128)S(1)} %copy-done.1), custom_call_target="tpu_custom_call" | custom-call | tf_op jit(solution)/shard_map/pallas_call | solution.py:541
  7.4 0.2 %shard_map.44 = (f32[33,3,8,128]{3,2,1,0:T(8,128)S(1)}, f32[33,3,8,128]{3,2,1,0:T(8,128)S(1)}) custom-call(f32[16,3,8,128]{3,2,1,0:T(8,128)S(1)} %get-tuple-element.14.pair), custom_call_target="tpu_custom_call" | custom-call | tf_op jit(solution)/shard_map/pallas_call | solution.py:551
  7.7 0.7 %collective-permute-done.3.below.above = f32[6,8,128]{2,1,0:T(8,128)S(1)} collective-permute-done((f32[6,8,128]{2,1,0:T(8,128)S(1)}, f32[6,8,128]{2,1,0:T(8,128)S(1)}, u32[]{:S(2)}, u32[]{:S(2)}) %collective-permute-start.3) | collective-permute-done | bytes 24608 | tf_op jit(solution)/shard_map/ppermute | solution.py:490
  8.3 1.1 %collective-permute-done.4.beside = f32[6,8,128]{2,1,0:T(8,128)S(1)} collective-permute-done((f32[6,8,128]{2,1,0:T(8,128)S(1)}, f32[6,8,128]{2,1,0:T(8,128)S(1)}, u32[]{:S(2)}, u32[]{:S(2)}) %collective-permute-start.4) | collective-permute-done | bytes 24608 | tf_op jit(solution)/shard_map/ppermute | solution.py:490
  9.4 1.0 %collective-permute-start.5 = (f32[15,8,128]{2,1,0:T(8,128)S(1)}, f32[15,8,128]{2,1,0:T(8,128)S(1)}, u32[]{:S(2)}, u32[]{:S(2)}) collective-permute-start(f32[15,8,128]{2,1,0:T(8,128)S(1)} %shard_map.46.mine), channel_id=1, source_target_pairs={{0,8},{1,9},{2,10},{3,11},{4,12},{5,13},{6,14},{7,15},{8,0},{9,1},... | collective-permute-start | bytes 184328 | tf_op jit(solution)/shard_map/ppermute | solution.py:490
  10.4 0.0 collective-permute-done.1.up_other.down_other
  10.4 0.2 %shard_map.45 = (f32[33,3,8,128]{3,2,1,0:T(8,128)S(1)}, f32[33,3,8,128]{3,2,1,0:T(8,128)S(1)}) custom-call(f32[3,8,8,128]{3,2,1,0:T(8,128)S(1)} %collective-permute-done.up_mine.down_mine, f32[3,8,8,128]{3,2,1,0:T(8,128)S(1)} %collective-permute-done.1.up_other.down_other, ...), custom_call_target="tpu_custom_call", output_to_operand_aliasing={{0}: (4, {}), {1}: (5, {})} | custom-call | flops 10000000000 | bytes 393216 | tf_op jit(solution)/shard_map/pallas_call | solution.py:558
  10.6 0.8 %shard_map.47 = (f32[32,128]{1,0:T(8,128)S(1)}, f32[25,3,8,128]{3,2,1,0:T(8,128)S(1)}) custom-call(bf16[128,128]{1,0:T(8,128)(2,1)S(1)} %get-tuple-element.13.columns, f32[4,8,128]{2,1,0:T(8,128)S(1)} %shard_map.42.masks, f32[33,3,8,128]{3,2,1,0:T(8,128)S(1)} %get-tuple-element.17.stack, f32[33,3,8,128]{3,2,1,0:T(8,128)S(1)} %get-tuple-element.18.placed, ...), custom_call_target="tpu_custom_call" | custom-call | flops 10000000000 | bytes 393216 | tf_op jit(solution)/shard_map/pallas_call | solution.py:575
  11.5 0.0 collective-permute-done.5.other
  11.5 1.6 %shard_map.48 = (f32[3,4,1,16]{3,2,1,0:T(1,128)}, f32[3,4,1,16]{3,2,1,0:T(1,128)}) custom-call(bf16[128,128]{1,0:T(8,128)(2,1)S(1)} %get-tuple-element.12.columns, f32[4,8,128]{2,1,0:T(8,128)S(1)} %shard_map.42.masks, f32[25,3,8,128]{3,2,1,0:T(8,128)S(1)} %get-tuple-element.20.rows, f32[15,8,128]{2,1,0:T(8,128)S(1)} %collective-permute-done.5.other, ...), custom_call_target="tpu_custom_call" | custom-call | tf_op jit(solution)/shard_map/pallas_call | solution.py:588
  (2 shorter events, 0.0 us)
Async XLA Ops:
  0.6 2.0 %collective-permute-start.2 = (f32[3,8,8,128]{3,2,1,0:T(8,128)}, f32[3,8,8,128]{3,2,1,0:T(8,128)S(1)}, u32[]{:S(2)}, u32[]{:S(2)}) collective-permute-start(f32[3,8,8,128]{3,2,1,0:T(8,128)} %mine.1), channel_id=1, source_target_pairs={{0,8},{1,9},{2,10},{3,11},{4,12},{5,13},{6,14},{7,15},{8,0},{9,1},... | collective-permute-start | bytes 294920 | tf_op jit(solution)/shard_map/ppermute | solution.py:490
  1.4 5.0 %collective-permute-start = (f32[3,8,8,128]{3,2,1,0:T(8,128)}, f32[3,8,8,128]{3,2,1,0:T(8,128)S(1)}, u32[]{:S(2)}, u32[]{:S(2)}) collective-permute-start(f32[3,8,8,128]{3,2,1,0:T(8,128)} %mine.1), channel_id=1, source_target_pairs={{0,16},{1,17},{2,18},{3,19},{4,20},{5,21},{6,22},{7,23},{8,24},{9,... | collective-permute-start | bytes 294920 | tf_op jit(solution)/shard_map/ppermute | solution.py:490
  2.6 0.9 %copy-start = (f32[3,8,8,128]{3,2,1,0:T(8,128)S(1)}, f32[3,8,8,128]{3,2,1,0:T(8,128)}, u32[]{:S(2)}) copy-start(f32[3,8,8,128]{3,2,1,0:T(8,128)} %mine.1) | copy-start | bytes 294916
  3.7 3.2 %copy-start.1 = (s32[8]{0:T(128)S(1)}, s32[8]{0:T(128)}, u32[]{:S(2)}) copy-start(s32[8]{0:T(128)} %layer_map.1) | copy-start | bytes 100
  3.7 4.6 %collective-permute-start.3 = (f32[6,8,128]{2,1,0:T(8,128)S(1)}, f32[6,8,128]{2,1,0:T(8,128)S(1)}, u32[]{:S(2)}, u32[]{:S(2)}) collective-permute-start(f32[6,8,128]{2,1,0:T(8,128)S(1)} %get-tuple-element.19), channel_id=1, source_target_pairs={{0,24},{1,16},{2,17},{3,18},{4,19},{5,20},{6,21},{7,22},{8,25},{9,... | collective-permute-start | bytes 73736 | tf_op jit(solution)/shard_map/ppermute | solution.py:490
  5.8 3.6 %collective-permute-start.4 = (f32[6,8,128]{2,1,0:T(8,128)S(1)}, f32[6,8,128]{2,1,0:T(8,128)S(1)}, u32[]{:S(2)}, u32[]{:S(2)}) collective-permute-start(f32[6,8,128]{2,1,0:T(8,128)S(1)} %get-tuple-element.19), channel_id=1, source_target_pairs={{0,8},{1,0},{2,1},{3,2},{4,3},{5,4},{6,5},{7,6},{8,9},{9,10},{10,1... | collective-permute-start | bytes 73736 | tf_op jit(solution)/shard_map/ppermute | solution.py:490
  6.3 4.1 %collective-permute-start.1 = (f32[3,8,8,128]{3,2,1,0:T(8,128)S(1)}, f32[3,8,8,128]{3,2,1,0:T(8,128)S(1)}, u32[]{:S(2)}, u32[]{:S(2)}) collective-permute-start(f32[3,8,8,128]{3,2,1,0:T(8,128)S(1)} %collective-permute-done.up_mine.down_mine), channel_id=1, source_target_pairs={{0,8},{1,9},{2,10},{3,11},{4,12},{5,13},{6,14},{7,15},{8,0},{9,1},... | collective-permute-start | bytes 294920 | tf_op jit(solution)/shard_map/ppermute | solution.py:490
  9.4 2.1 %collective-permute-start.5 = (f32[15,8,128]{2,1,0:T(8,128)S(1)}, f32[15,8,128]{2,1,0:T(8,128)S(1)}, u32[]{:S(2)}, u32[]{:S(2)}) collective-permute-start(f32[15,8,128]{2,1,0:T(8,128)S(1)} %shard_map.46.mine), channel_id=1, source_target_pairs={{0,8},{1,9},{2,10},{3,11},{4,12},{5,13},{6,14},{7,15},{8,0},{9,1},... | collective-permute-start | bytes 184328 | tf_op jit(solution)/shard_map/ppermute | solution.py:490
